TPU v7x, 32 devices: a whole 2x2x4 slice. The times are simulated.
32 devices in a mesh: groups: 2 (over y), space: 4 (over z), tm: 2 (over x), col: 2 (over core).
Axes of the slice: x: 2, y: 2, z: 4, core: 2. Of those that a mesh axis runs over, the one named last changes fastest.
Arguments:
- activations: bfloat16 [4, 16, 512, 256], P(('groups', 'tm'), ('space', 'col')), parts along dimension 0, may hold values from -6 to 6
- conv_weight: bfloat16 [3, 3, 256, 256], replicated, may hold values from -0.125 to 0.125
- conv_bias: float32 [256], replicated, may hold values from -3 to 3
- head_weight: bfloat16 [256, 32], replicated, may hold values from -0.375 to 0.375
- latent_grad: bfloat16 [4, 8, 256, 16], P(('groups', 'tm'), None, ('space', 'col')), parts along dimension 0, may hold values from -6 to 6
- noise_sample: bfloat16 [4, 8, 256, 16], P(('groups', 'tm'), ('space', 'col')), parts along dimension 0, may hold values from -5 to 5
Outputs:
- x_grad: bfloat16 [4, 16, 512, 256], P(('groups', 'tm'), ('space', 'col')), parts along dimension 0
- conv_weight_grad: float32 [3, 3, 512, 256], P(None, None, ('groups', 'space', 'col')), parts along dimension 2
- head_weight_grad: float32 [512, 32], P(('groups', 'space', 'col')), parts along dimension 0
- conv_bias_grad: float32 [512], P(('groups', 'space', 'col')), parts along dimension 0
There are 2 independent parts, one for each index of `groups`. A program takes and returns all parts, laid end to end along the dimension named above; an argument that names none is the same for every part. Nothing has to cross between parts.
All inputs are finite; a program needn't handle non-finite values.
Results may differ from a plain program's by a relative error of at most 0.007.
Values may be sent and summed in bfloat16 or wider, within the bound.
No kernel may reach another device: no remote copies, remote signals or barrier semaphores. Data moves between devices by JAX's collectives and lax.ppermute only.
A program may use at most 64 MiB of HBM per device.

v0:
```python
import math

import jax
import jax.numpy as jnp
from jax import lax
from jax.sharding import PartitionSpec as P

kl_weight = 1.0


def passed_along(x, axis, by):
    peers = lax.axis_size(axis)
    pairs = [(i, i + by) for i in range(peers) if 0 <= i + by < peers]
    return lax.ppermute(x, axis, pairs)


def window_at(padded, index, row_count, col_count):
    row_tap = index // 3
    col_tap = index % 3
    return padded[:, row_tap : row_tap + 2 * row_count : 2, col_tap : col_tap + 2 * col_count : 2]


def parity_gradient(pre_grad, conv_weight, row_count, col_count):
    frames = pre_grad.shape[0]
    channels = conv_weight.shape[2]
    planes = {}
    for index in range(9):
        row_tap = index // 3
        col_tap = index % 3
        contrib = jnp.einsum(
            "trco,ko->trck",
            pre_grad,
            conv_weight[row_tap, col_tap],
            preferred_element_type=jnp.float32,
        )
        placed = jnp.pad(
            contrib,
            ((0, 0), (row_tap // 2, 1 - row_tap // 2), (col_tap // 2, 1 - col_tap // 2), (0, 0)),
        )
        parity = (row_tap % 2, col_tap % 2)
        if parity in planes:
            planes[parity] = planes[parity] + placed
        else:
            planes[parity] = placed
    even_rows = jnp.stack([planes[0, 0], planes[0, 1]], 3).reshape(
        frames, row_count + 1, 2 * col_count + 2, channels
    )
    odd_rows = jnp.stack([planes[1, 0], planes[1, 1]], 3).reshape(
        frames, row_count + 1, 2 * col_count + 2, channels
    )
    woven = jnp.stack([even_rows, odd_rows], 2).reshape(
        frames, 2 * row_count + 2, 2 * col_count + 2, channels
    )
    return woven[:, : 2 * row_count + 1, : 2 * col_count + 1]


def body(activations, conv_weight, conv_bias, head_weight, latent_grad, noise_sample):
    frames, double_rows, double_cols, channels = activations.shape
    row_count = double_rows // 2
    col_count = double_cols // 2
    latent_dim = latent_grad.shape[-1]
    upstream = lax.all_to_all(
        latent_grad, ("space", "col"), split_axis=1, concat_axis=2, tiled=True
    )
    next_row = passed_along(activations[:, :1], ("space", "col"), -1)
    padded = jnp.pad(jnp.concatenate([activations, next_row], 1), ((0, 0), (0, 0), (0, 1), (0, 0)))
    pre_act = jnp.zeros((frames, row_count, col_count, channels), jnp.float32) + conv_bias
    for index in range(9):
        pre_act = pre_act + jnp.einsum(
            "trck,ko->trco",
            window_at(padded, index, row_count, col_count),
            conv_weight[index // 3, index % 3],
            preferred_element_type=jnp.float32,
        )
    hidden = jax.nn.silu(pre_act).astype(jnp.bfloat16)
    flattened = hidden.reshape(-1, channels)
    moments = jnp.dot(flattened, head_weight, preferred_element_type=jnp.float32)
    mean_part = moments[:, :latent_dim]
    logvar = moments[:, latent_dim:]
    upstream_flat = upstream.reshape(-1, latent_dim).astype(jnp.float32)
    sample = noise_sample.reshape(-1, latent_dim).astype(jnp.float32)
    spread = jnp.exp(0.5 * logvar)
    mean_grad = upstream_flat + kl_weight * mean_part
    logvar_grad = 0.5 * upstream_flat * sample * spread + 0.5 * kl_weight * (spread * spread - 1.0)
    moment_grad = jnp.concatenate([mean_grad, logvar_grad], 1).astype(jnp.bfloat16)
    head_term = jnp.dot(flattened.T, moment_grad, preferred_element_type=jnp.float32)
    hidden_grad = jnp.dot(moment_grad, head_weight.T, preferred_element_type=jnp.float32)
    hidden_grad = hidden_grad.reshape(frames, row_count, col_count, channels)
    gating = jax.nn.sigmoid(pre_act)
    pre_grad = (hidden_grad * gating * (1.0 + pre_act * (1.0 - gating))).astype(jnp.bfloat16)
    bias_term = jnp.sum(pre_grad, axis=(0, 1, 2), dtype=jnp.float32)
    kernel_terms = []
    for index in range(9):
        kernel_terms.append(
            jnp.einsum(
                "trck,trco->ko",
                window_at(padded, index, row_count, col_count),
                pre_grad,
                preferred_element_type=jnp.float32,
            )
        )
    kernel_term = jnp.stack(kernel_terms, 1).reshape(channels, 3, 3, channels)
    input_grad = parity_gradient(pre_grad, conv_weight, row_count, col_count)
    own_grad = input_grad[:, : 2 * row_count, : 2 * col_count]
    rim_grad = passed_along(input_grad[:, 2 * row_count :, : 2 * col_count], ("space", "col"), 1)
    own_grad = own_grad.at[:, :1].add(rim_grad)
    x_grad = own_grad.astype(jnp.bfloat16)
    totals = (
        lax.psum(kernel_term.astype(jnp.bfloat16), "tm").astype(jnp.float32),
        lax.psum(head_term.astype(jnp.bfloat16), "tm").astype(jnp.float32),
        lax.psum(bias_term.astype(jnp.bfloat16), "tm").astype(jnp.float32),
    )
    shares = (
        lax.psum_scatter(totals[0], ("space", "col"), scatter_dimension=0, tiled=True),
        lax.psum_scatter(totals[1], ("space", "col"), scatter_dimension=0, tiled=True),
        lax.psum_scatter(totals[2], ("space", "col"), scatter_dimension=0, tiled=True),
    )
    positions = (
        frames * lax.axis_size("tm") * row_count * lax.axis_size(("space", "col")) * col_count
    )
    grad_scale = 1.0 / math.sqrt(positions)
    kernel_grad = jnp.transpose(shares[0] * grad_scale, (1, 2, 0, 3))
    return (x_grad, kernel_grad, shares[1] * grad_scale, shares[2] * grad_scale)


def solution(mesh):
    in_specs = (
        P(("groups", "tm"), ("space", "col"), None, None),
        P(),
        P(),
        P(),
        P(("groups", "tm"), None, ("space", "col"), None),
        P(("groups", "tm"), ("space", "col"), None, None),
    )
    out_specs = (
        P(("groups", "tm"), ("space", "col"), None, None),
        P(None, None, ("groups", "space", "col"), None),
        P(("groups", "space", "col"), None),
        P(("groups", "space", "col")),
    )
    return jax.shard_map(body, mesh=mesh, in_specs=in_specs, out_specs=out_specs, check_vma=False)
```

profile of v0, /device:TPU:0, one launch (start us, length us, event | category | flops | bytes accessed | tf_op | source)
XLA Modules:
  0.0 126.6 jit_solution(13419863196311703334)
XLA Ops:
  8.1 1.0 slice.129
  9.1 1.3 %collective-permute-start = (bf16[1,1,512,256]{3,2,1,0:T(8,128)(2,1)S(1)}, bf16[1,1,512,256]{3,2,1,0:T(8,128)(2,1)S(1)}, u32[]{:S(2)}, u32[]{:S(2)}) collective-permute-start(bf16[1,1,512,256]{3,2,1,0:T(8,128)(2,1)S(1)} %slice.129), channel_id=1, source_target_pairs={{1,0},{4,1},{5,4},{8,5},{9,8},{12,9},{13,12},{3,2},{6,3},{7,6},{10... | collective-permute-start | bytes 786440 | tf_op jit(solution)/shard_map/ppermute | solution.py:14
  10.4 0.1 reshape.190
  10.5 12.5 %all_to_all.4 = bf16[8,2,256]{2,1,0:T(2,128)(2,1)S(1)} all-to-all(bf16[8,2,256]{2,1,0:T(2,128)(2,1)S(1)} %reshape.190), channel_id=1, replica_groups=mesh['groups'=2,'space'=4,'tm'=2,'col'=2] {'space','col'}, dimensions={0} | all-to-all | bytes 16384 | tf_op jit(solution)/shard_map/all_to_all | solution.py:62
  23.3 0.4 slice.130
  23.7 0.4 slice.132
  24.1 0.4 slice.134
  24.5 0.4 slice.136
  24.9 0.4 slice.138
  25.3 0.4 slice.140
  25.8 0.4 slice.142
  26.2 0.4 slice.144
  26.6 0.4 slice.146
  27.1 0.2 convolution_add_fusion.8
  27.3 0.2 convolution_add_fusion.7
  27.5 0.2 convolution_add_fusion.6
  27.7 0.2 convolution_add_fusion.5
  27.9 0.2 convolution_add_fusion.4
  28.1 0.2 convolution_add_fusion.3
  28.3 0.2 convolution_add_fusion.2
  28.5 0.2 convolution_add_fusion.1
  28.7 0.2 multiply_convert_fusion
  28.9 0.2 copy-done.10
  29.2 0.1 fusion.86
  29.4 0.2 fusion.85
  29.6 0.3 copy-done.9
  29.9 0.2 fusion.5
  30.1 0.2 fusion.7
  30.4 0.2 fusion.9
  30.6 0.2 fusion.11
  30.8 0.2 fusion.13
  31.1 0.2 fusion.15
  31.3 0.2 fusion.17
  31.5 0.2 fusion.19
  31.8 0.2 fusion.21
  32.0 1.0 copy-done.3
  33.1 0.2 convolution_convert_fusion.9
  33.3 10.3 %all-reduce.11 = (bf16[256,32]{1,0:T(8,128)(2,1)S(1)}, bf16[256]{0:T(256)(128)(2,1)S(1)}) all-reduce(bf16[256,32]{1,0:T(8,128)(2,1)S(1)} %convolution_convert_fusion.9, bf16[256]{0:T(256)(128)(2,1)S(1)} %get-tuple-element.22), channel_id=1, replica_groups=mesh['groups'=2,'space'=4,'tm'=2,'col'=2] {'tm'}, use_global_device_ids=true, to_apply=%region_2.3 | all-reduce | flops 8448 | bytes 33792 | tf_op jit(solution)/shard_map/psum | solution.py:110
  43.6 0.7 convert_element_type.67
  44.4 30.4 %all-reduce.14.cloned.1.call-done = bf16[256,3,3,256]{3,0,2,1:T(8,128)(2,1)} async-done(((bf16[256,3,3,256]{3,0,2,1:T(8,128)(2,1)}), bf16[256,3,3,256]{3,0,2,1:T(8,128)(2,1)}) %all-reduce.14.cloned.1.call-update) | async-done | bytes 1179664 | tf_op jit(solution)/shard_map/psum | solution.py:109
  74.8 2.9 %convert_element_type.65 = f32[256,3,3,256]{3,0,2,1:T(8,128)} convert(bf16[256,3,3,256]{3,0,2,1:T(8,128)(2,1)} %all-reduce.14.cloned.1.call-done) | non-fusion elementwise | flops 589824 | bytes 3538944 | tf_op jit(solution)/shard_map/convert_element_type | solution.py:109
  77.7 0.2 convolution_bitcast_fusion.3
  77.9 0.2 convolution_bitcast_fusion.4
  78.2 0.2 convolution_bitcast_fusion.5
  78.4 0.2 convolution_bitcast_fusion.6
  78.6 0.2 convolution_bitcast_fusion.7
  78.8 0.2 convolution_bitcast_fusion.8
  79.0 0.1 add_bitcast_fusion.1
  79.3 0.5 copy.20
  79.8 0.2 convolution_bitcast_fusion
  80.0 0.2 convolution_bitcast_fusion.1
  80.3 0.2 convolution_bitcast_fusion.2
  80.6 0.5 copy.21
  81.2 0.9 pad_maximum_fusion
  82.1 0.2 copy.22
  82.4 1.8 %collective-permute-start.1 = (f32[1,1,512,256]{3,2,1,0:T(8,128)S(1)}, f32[1,1,512,256]{3,2,1,0:T(8,128)S(1)}, u32[]{:S(2)}, u32[]{:S(2)}) collective-permute-start(f32[1,1,512,256]{3,2,1,0:T(8,128)S(1)} %slice.157), channel_id=1, source_target_pairs={{0,1},{1,4},{4,5},{5,8},{8,9},{9,12},{12,13},{2,3},{3,6},{6,7},{7,... | collective-permute-start | bytes 1572872 | tf_op jit(solution)/shard_map/ppermute | solution.py:14
  84.1 0.6 dynamic-slice.8
  85.4 0.8 slice.155
  86.2 23.0 %all-reduce.10 = f32[256]{0:T(256)S(1)} all-reduce(bf16[256]{0:T(256)(128)(2,1)S(1)} %get-tuple-element.17), channel_id=4, replica_groups=mesh['groups'=2,'space'=4,'tm'=2,'col'=2] {'space','col'}, use_global_device_ids=true, to_apply=%region_6.7.clone | all-reduce | flops 256 | bytes 1536
  109.3 0.6 dynamic-slice_multiply_fusion
  109.9 1.3 %broadcast_multiply_fusion = f32[32,32]{1,0:T(8,128)} fusion(f32[32,32]{1,0:T(8,128)} %reduce-scatter.5.cloned.1.call-done), kind=kLoop, calls=%fused_computation.128 | loop fusion | flops 1024 | bytes 8192 | tf_op jit(solution)/shard_map/mul | solution.py:123
  111.2 0.8 fusion.23
  111.9 5.5 %reduce-scatter.3.cloned.1.call-done = f32[32,3,3,256]{3,0,2,1:T(8,128)} async-done(((f32[256,3,3,256]{3,0,2,1:T(8,128)}), f32[32,3,3,256]{3,0,2,1:T(8,128)}) %reduce-scatter.3.cloned.1.call-update) | async-done | bytes 294928 | tf_op jit(solution)/shard_map/reduce_scatter | solution.py:114
  117.5 1.7 %multiply_bitcast_fusion = f32[3,3,32,256]{3,2,1,0:T(8,128)} fusion(f32[32,3,3,256]{3,0,2,1:T(8,128)} %reduce-scatter.3.cloned.1.call-done), kind=kLoop, calls=%fused_computation.62 | loop fusion | flops 73728 | bytes 589824 | tf_op jit(solution)/shard_map/transpose | solution.py:122
  (44 shorter events, 0.8 us)
Async XLA Ops:
  8.0 2.4 %copy-start = (bf16[1,8,32,16]{2,3,1,0:T(8,128)(2,1)S(1)}, bf16[1,8,32,16]{2,3,1,0:T(8,128)(2,1)}, u32[]{:S(2)}) copy-start(bf16[1,8,32,16]{2,3,1,0:T(8,128)(2,1)} %param.12) | copy-start | bytes 24580
  8.0 15.2 %copy-start.2 = (bf16[1,2,512,256]{3,2,1,0:T(8,128)(2,1)S(1)}, bf16[1,2,512,256]{3,2,1,0:T(8,128)(2,1)}, u32[]{:S(2)}) copy-start(bf16[1,2,512,256]{3,2,1,0:T(8,128)(2,1)} %param.8) | copy-start | bytes 1572868
  8.0 66.8 %all-reduce.14.cloned.1.call-start = ((), (), s32[]{:S(2)}) async-start(), calls=%async_computation.3 | async-start | bytes 2359296 | tf_op jit(solution)/shard_map/psum | solution.py:109
  9.1 14.1 %collective-permute-start = (bf16[1,1,512,256]{3,2,1,0:T(8,128)(2,1)S(1)}, bf16[1,1,512,256]{3,2,1,0:T(8,128)(2,1)S(1)}, u32[]{:S(2)}, u32[]{:S(2)}) collective-permute-start(bf16[1,1,512,256]{3,2,1,0:T(8,128)(2,1)S(1)} %slice.129), channel_id=1, source_target_pairs={{1,0},{4,1},{5,4},{8,5},{9,8},{12,9},{13,12},{3,2},{6,3},{7,6},{10... | collective-permute-start | bytes 786440 | tf_op jit(solution)/shard_map/ppermute | solution.py:14
  23.2 3.8 %copy-start.1 = (bf16[3,3,256,256]{3,2,1,0:T(8,128)(2,1)S(1)}, bf16[3,3,256,256]{3,2,1,0:T(8,128)(2,1)}, u32[]{:S(2)}) copy-start(bf16[3,3,256,256]{3,2,1,0:T(8,128)(2,1)} %param.9) | copy-start | bytes 3538948
  23.3 3.8 %copy-start.12 = (f32[256]{0:T(256)S(1)}, f32[256]{0:T(256)}, u32[]{:S(2)}) copy-start(f32[256]{0:T(256)} %param.10) | copy-start | bytes 3076
  23.7 3.6 %copy-start.8 = (bf16[1,1,256,256]{3,2,1,0:T(8,128)(2,1)}, bf16[1,1,256,256]{3,2,1,0:T(8,128)(2,1)S(1)}, u32[]{:S(2)}) copy-start(bf16[1,1,256,256]{3,2,1,0:T(8,128)(2,1)S(1)} %slice.130) | copy-start | bytes 393220
  27.1 1.6 %copy-start.4 = (bf16[1,1,256,256]{3,2,1,0:T(8,128)(2,1)}, bf16[1,1,256,256]{3,2,1,0:T(8,128)(2,1)S(1)}, u32[]{:S(2)}) copy-start(bf16[1,1,256,256]{3,2,1,0:T(8,128)(2,1)S(1)} %slice.146) | copy-start | bytes 393220
  28.5 0.7 copy-start.10
  28.5 0.9 copy-start.11
  28.9 1.4 %copy-start.6 = (bf16[256,256]{1,0:T(8,128)(2,1)}, bf16[256,256]{1,0:T(8,128)(2,1)S(1)}, u32[]{:S(2)}) copy-start(bf16[256,256]{1,0:T(8,128)(2,1)S(1)} %get-tuple-element.20) | copy-start | bytes 393220
  28.9 1.0 copy-start.9
  30.4 1.4 %copy-start.5 = (bf16[1,1,256,256]{3,2,1,0:T(8,128)(2,1)S(1)}, bf16[1,1,256,256]{3,2,1,0:T(8,128)(2,1)}, u32[]{:S(2)}) copy-start(bf16[1,1,256,256]{3,2,1,0:T(8,128)(2,1)} %copy-done.4) | copy-start | bytes 393220
  31.3 1.8 %copy-start.7 = (bf16[256,256]{1,0:T(8,128)(2,1)S(1)}, bf16[256,256]{1,0:T(8,128)(2,1)}, u32[]{:S(2)}) copy-start(bf16[256,256]{1,0:T(8,128)(2,1)} %copy-done.6) | copy-start | bytes 393220
  32.0 1.0 copy-start.3
  33.1 76.8 %reduce-scatter.5.cloned.1.call-start = ((), (), s32[]{:S(2)}) async-start(), calls=%async_computation.5 | async-start | bytes 147456 | tf_op jit(solution)/shard_map/reduce_scatter | solution.py:115
  44.3 73.1 %reduce-scatter.3.cloned.1.call-start = ((), (), s32[]{:S(2)}) async-start(), calls=%async_computation.4 | async-start | bytes 2654208 | tf_op jit(solution)/shard_map/reduce_scatter | solution.py:114
  82.1 2.0 %copy-start.13 = (u32[32]{0:T(128)S(1)}, u32[32]{0:T(128)}, u32[]{:S(2)}) copy-start(u32[32]{0:T(128)} %constant.72) | copy-start | bytes 388
  82.4 28.8 %collective-permute-start.1 = (f32[1,1,512,256]{3,2,1,0:T(8,128)S(1)}, f32[1,1,512,256]{3,2,1,0:T(8,128)S(1)}, u32[]{:S(2)}, u32[]{:S(2)}) collective-permute-start(f32[1,1,512,256]{3,2,1,0:T(8,128)S(1)} %slice.157), channel_id=1, source_target_pairs={{0,1},{1,4},{4,5},{5,8},{8,9},{9,12},{12,13},{2,3},{3,6},{6,7},{7,... | collective-permute-start | bytes 1572872 | tf_op jit(solution)/shard_map/ppermute | solution.py:14
Sparse Core Ops, SparseCore 0:
  33.2 41.5 all-reduce.13
Sparse Core Ops, SparseCore 1:
  44.4 27.5 reduce-scatter.4
  77.8 39.6 reduce-scatter.2
where the time goes:
time: 127 us
  blocking collectives  45.8 us (36%)
  waiting for transfers between devices  36 us (28%)
  between operations  16.8 us (13%)
  local copies, waits for them, and re-layouts  9.32 us (7%)
  other arithmetic  9.3 us (7%)
  matrix products  6.28 us (5%)
  starting transfers between devices  3.18 us (3%)
    psum x1, waiting for transfers between devices, body(): lax.psum(kernel_term.astype(jnp.bfloat16), 'tm').astype(jnp.float32)  30.4 us
    unnamed x1, blocking collectives  23 us
    all_to_all x1, blocking collectives, body(): lax.all_to_all(latent_grad, ('space', 'col'), split_axis=1, concat_axis=2...  12.5 us
    psum x1, blocking collectives, body(): lax.psum(head_term.astype(jnp.bfloat16), 'tm').astype(jnp.float32)  10.3 us
    reduce_scatter x1, waiting for transfers between devices, body(): lax.psum_scatter(totals[0], ('space', 'col'), scatter_dimension=0, tiled=...  5.51 us
    slice x9, local copies, waits for them, and re-layouts, window_at(): padded[:, row_tap:row_tap + 2 * row_count:2, col_tap:col_tap + 2 * col_co...  3.7 us
    ppermute x2, starting transfers between devices, passed_along(): return lax.ppermute(x, axis, pairs)  3.06 us
    convert_element_type x1, other arithmetic, body(): lax.psum(kernel_term.astype(jnp.bfloat16), 'tm').astype(jnp.float32)  2.91 us
  transfers between devices with their start and end apart: 5, of which 2 were waited for; matrix products, arithmetic and copies ran while one was open for 10% of the time, Pallas kernels for 0%

commit v1 on v0

v1 whole, which is shorter than its diff:
```python
import functools
import math

import jax
import jax.numpy as jnp
from jax import lax
from jax.experimental import pallas as pl
from jax.experimental.pallas import tpu as pltpu
from jax.sharding import PartitionSpec as P

f32 = jnp.float32
bf16 = jnp.bfloat16
kl_weight = 1.0
LANES = 128
TAIL = 8


def dot(a, b, ca, cb):
    return lax.dot_general(a, b, (((ca,), (cb,)), ((), ())), preferred_element_type=f32)


def params():
    return pltpu.CompilerParams(vmem_limit_bytes=24 << 20)


def full_call(kernel, out_shape, scratch, flops, moved, smem=0):
    def call(*args):
        specs = [pl.BlockSpec(memory_space=pltpu.SMEM)] * smem
        specs += [pl.BlockSpec(memory_space=pltpu.VMEM)] * (len(args) - smem)
        return pl.pallas_call(
            kernel,
            out_shape=out_shape,
            in_specs=specs,
            out_specs=jax.tree.map(lambda _: pl.BlockSpec(memory_space=pltpu.VMEM), out_shape),
            scratch_shapes=scratch,
            compiler_params=params(),
            cost_estimate=pl.CostEstimate(flops=flops, bytes_accessed=moved, transcendentals=0),
        )(*args)

    return call


def terms_kernel(
    me_ref, act_ref, next_ref, w_ref, bias_ref, head_ref, up_ref, noise_ref,
    pre_grad_ref, keep_ref, send_ref, stage,
):
    cols = pre_grad_ref.shape[0]
    spaces = keep_ref.shape[0]
    latent = noise_ref.shape[0]
    width = head_ref.shape[1]
    share = width // (2 * spaces) if width % (2 * spaces) == 0 else 0
    first = me_ref[0] == 0
    windows = []
    for row in range(3):
        source = (act_ref[row] if row < 2 else next_ref[...]).astype(f32)
        for lane in range(width // LANES):
            at = row * (width // LANES) + lane
            stage[at, : 2 * cols, :] = source[:, lane * LANES : (lane + 1) * LANES]
            stage[at, 2 * cols :, :] = jnp.zeros((8, LANES), f32)
    for row in range(3):
        for tap in range(3):
            halves = []
            for lane in range(width // LANES):
                at = row * (width // LANES) + lane
                halves.append(stage[at, pl.ds(tap, cols, stride=2), :])
            windows.append(jnp.concatenate(halves, 1).astype(bf16))
    pre_act = jnp.broadcast_to(bias_ref[...], (cols, width))
    for index in range(9):
        pre_act = pre_act + dot(windows[index], w_ref[index], 1, 0)
    gating = jax.nn.sigmoid(pre_act)
    hidden = (pre_act * gating).astype(bf16)
    moments = dot(head_ref[...], hidden, 1, 1)
    mean_part = moments[:latent]
    logvar = moments[latent:]
    tiles = [up_ref[i].astype(f32) for i in range(up_ref.shape[0])]
    upstream = jnp.concatenate(tiles, 1)
    sample = noise_ref[...].astype(f32)
    spread = jnp.exp(0.5 * logvar)
    mean_grad = upstream + kl_weight * mean_part
    logvar_grad = 0.5 * upstream * sample * spread + 0.5 * kl_weight * (spread * spread - 1.0)
    moment_grad = jnp.concatenate([mean_grad, logvar_grad], 0).astype(bf16)
    hidden_grad = dot(moment_grad, head_ref[...], 0, 0)
    pre_grad = (hidden_grad * gating * (1.0 + pre_act * (1.0 - gating))).astype(bf16)
    pre_grad_ref[...] = pre_grad

    def put(s, at, size, even, odd):
        keep_ref[s, at : at + size, :] = jnp.where(first, even, odd)
        send_ref[s, at : at + size, :] = jnp.where(first, odd, even).astype(bf16)

    for index in range(9):
        term = dot(windows[index], pre_grad, 0, 0)
        for s in range(spaces):
            at = 2 * share * s
            put(s, index * share, share, term[at : at + share], term[at + share : at + 2 * share])
    head_term = dot(hidden, moment_grad, 0, 1)
    bias_term = dot(jnp.ones((TAIL, cols), bf16), pre_grad, 1, 0)
    parts = share // TAIL

    def tail(at):
        pieces = [head_term[at + TAIL * i : at + TAIL * (i + 1)] for i in range(parts)]
        pieces.append(bias_term[:, at : at + share])
        used = sum(piece.shape[1] for piece in pieces)
        pieces.append(jnp.zeros((TAIL, width - used), f32))
        return jnp.concatenate(pieces, 1)

    for s in range(spaces):
        at = 2 * share * s
        put(s, 9 * share, TAIL, tail(at), tail(at + share))


def pair_kernel(me_ref, keep_ref, got_ref, *outs):
    me = me_ref[0]
    for k, out in enumerate(outs):
        at = jnp.bitwise_xor(me, k)
        out[...] = (keep_ref[at] + got_ref[at].astype(f32)).astype(out.dtype)


def line_kernel(own_ref, *refs):
    total = own_ref[...]
    for ref in refs[:-1]:
        total = total + ref[...].astype(f32)
    refs[-1][...] = total.astype(bf16)


def final_kernel(scale, a_ref, b_ref, kernel_ref, head_ref, bias_ref):
    share, latents = head_ref.shape
    taps = kernel_ref.shape[0]
    total = (a_ref[...].astype(f32) + b_ref[...].astype(f32)) * scale
    for index in range(taps):
        kernel_ref[index] = total[index * share : (index + 1) * share]
    tail = total[taps * share :]
    for i in range(share // TAIL):
        head_ref[TAIL * i : TAIL * (i + 1), :] = tail[:, latents * i : latents * (i + 1)]
    at = latents * (share // TAIL)
    bias_ref[...] = tail[:1, at : at + share]


def input_kernel(pre_grad_ref, prev_ref, w_ref, out_ref, stage):
    cols, width = pre_grad_ref.shape
    pre_grad = pre_grad_ref[...]
    row_at = lax.broadcasted_iota(jnp.int32, (cols, width), 0)

    def planes(source, row_tap):
        even = dot(source, w_ref[3 * row_tap], 1, 1)
        odd = dot(source, w_ref[3 * row_tap + 1], 1, 1)
        late = pltpu.roll(dot(source, w_ref[3 * row_tap + 2], 1, 1), 1, 0)
        return even + jnp.where(row_at == 0, 0.0, late), odd

    def weave(row, even, odd):
        for lane in range(width // LANES):
            at = row * (width // LANES) + lane
            here = slice(lane * LANES, (lane + 1) * LANES)
            stage[at, pl.ds(0, cols, stride=2), :] = even[:, here]
            stage[at, pl.ds(1, cols, stride=2), :] = odd[:, here]
            out_ref[row, :, here] = stage[at].astype(bf16)

    even, odd = planes(pre_grad, 1)
    weave(1, even, odd)
    even, odd = planes(pre_grad, 0)
    even_rim, odd_rim = planes(prev_ref[...], 2)
    weave(0, even + even_rim, odd + odd_rim)


def body(activations, conv_weight, conv_bias, head_weight, latent_grad, noise_sample):
    frames, double_rows, double_cols, channels = activations.shape
    cols = double_cols // 2
    latent_dim = latent_grad.shape[-1]
    spaces = lax.axis_size("space")
    times = lax.axis_size("tm")
    line = ("space", "col")
    peers = lax.axis_size(line)
    assert frames == 1 and double_rows == 2 and lax.axis_size("col") == 2
    taps = conv_weight.reshape(9, channels, channels)
    col_at = lax.axis_index("col").astype(jnp.int32).reshape(1)
    space_at = lax.axis_index("space").astype(jnp.int32).reshape(1)

    next_row = lax.ppermute(activations[0, 0], line, [(i, i - 1) for i in range(1, peers)])
    tiles = jnp.transpose(latent_grad[0], (0, 2, 1))
    upstream = lax.all_to_all(tiles, line, split_axis=0, concat_axis=0, tiled=True)

    share = channels // peers
    if share % TAIL or spaces & (spaces - 1) or spaces > 4 or times != 2:
        return wide_body(
            activations, taps, conv_bias, head_weight, upstream, noise_sample, next_row
        )
    rows = 9 * share + TAIL
    square = 2 * cols * channels * channels
    pre_grad, keep, send = full_call(
        terms_kernel,
        (
            jax.ShapeDtypeStruct((cols, channels), bf16),
            jax.ShapeDtypeStruct((spaces, rows, channels), f32),
            jax.ShapeDtypeStruct((spaces, rows, channels), bf16),
        ),
        [pltpu.VMEM((3 * (channels // LANES), double_cols + 8, LANES), f32)],
        18 * square,
        6 << 20,
        1,
    )(
        col_at,
        activations[0],
        next_row,
        taps,
        conv_bias.reshape(1, channels),
        head_weight.T,
        upstream,
        jnp.transpose(noise_sample[0, 0]),
    )
    got = lax.ppermute(send, "col", [(0, 1), (1, 0)])
    pieces = full_call(
        pair_kernel,
        tuple(
            jax.ShapeDtypeStruct((rows, channels), f32 if k == 0 else bf16) for k in range(spaces)
        ),
        [],
        spaces * rows * channels,
        3 << 20,
        1,
    )(space_at, keep, got)
    far = [
        lax.ppermute(pieces[k], "space", [(i, i ^ k) for i in range(spaces)])
        for k in range(1, spaces)
    ]
    prev = lax.ppermute(pre_grad, line, [(i, i + 1) for i in range(peers - 1)])
    x_grad = full_call(
        input_kernel,
        jax.ShapeDtypeStruct((2, double_cols, channels), bf16),
        [pltpu.VMEM((2 * (channels // LANES), double_cols, LANES), f32)],
        9 * square,
        4 << 20,
    )(pre_grad, prev, taps)
    frame_term = full_call(
        line_kernel,
        jax.ShapeDtypeStruct((rows, channels), bf16),
        [],
        4 * rows * channels,
        1 << 20,
    )(pieces[0], *far)
    other = lax.ppermute(frame_term, "tm", [(0, 1), (1, 0)])
    positions = frames * times * peers * cols
    kernel_grad, head_grad, bias_grad = full_call(
        functools.partial(final_kernel, 1.0 / math.sqrt(positions)),
        (
            jax.ShapeDtypeStruct((9, share, channels), f32),
            jax.ShapeDtypeStruct((share, 2 * latent_dim), f32),
            jax.ShapeDtypeStruct((1, share), f32),
        ),
        [],
        rows * channels,
        1 << 20,
    )(frame_term, other)
    return (
        x_grad[None],
        kernel_grad.reshape(3, 3, share, channels),
        head_grad,
        bias_grad.reshape(share),
    )


def wide_body(activations, taps, conv_bias, head_weight, upstream, noise_sample, next_row):
    _, _, double_cols, channels = activations.shape
    cols = double_cols // 2
    latent_dim = noise_sample.shape[-1]
    line = ("space", "col")
    peers = lax.axis_size(line)
    padded = jnp.pad(jnp.concatenate([activations[0], next_row[None]], 0), ((0, 0), (0, 1), (0, 0)))
    windows = [
        padded[index // 3, index % 3 : index % 3 + 2 * cols : 2] for index in range(9)
    ]
    pre_act = jnp.zeros((cols, channels), f32) + conv_bias
    for index in range(9):
        pre_act = pre_act + dot(windows[index], taps[index], 1, 0)
    gating = jax.nn.sigmoid(pre_act)
    hidden = (pre_act * gating).astype(bf16)
    moments = dot(hidden, head_weight, 1, 0)
    upstream = jnp.transpose(upstream, (0, 2, 1)).reshape(cols, latent_dim).astype(f32)
    spread = jnp.exp(0.5 * moments[:, latent_dim:])
    mean_grad = upstream + kl_weight * moments[:, :latent_dim]
    logvar_grad = 0.5 * upstream * noise_sample[0, 0].astype(f32) * spread
    logvar_grad = logvar_grad + 0.5 * kl_weight * (spread * spread - 1.0)
    moment_grad = jnp.concatenate([mean_grad, logvar_grad], 1).astype(bf16)
    hidden_grad = dot(moment_grad, head_weight, 1, 1)
    pre_grad = (hidden_grad * gating * (1.0 + pre_act * (1.0 - gating))).astype(bf16)
    prev = lax.ppermute(pre_grad, line, [(i, i + 1) for i in range(peers - 1)])
    x_grad = full_call(
        input_kernel,
        jax.ShapeDtypeStruct((2, double_cols, channels), bf16),
        [pltpu.VMEM((2 * (channels // LANES), double_cols, LANES), f32)],
        18 * cols * channels * channels,
        4 << 20,
    )(pre_grad, prev, taps)
    kernel_term = jnp.stack([dot(window, pre_grad, 0, 0) for window in windows], 1)
    terms = (
        kernel_term.reshape(channels, 9 * channels),
        dot(hidden, moment_grad, 0, 0),
        jnp.sum(pre_grad, axis=0, dtype=f32),
    )
    grad_scale = 1.0 / math.sqrt(lax.axis_size("tm") * peers * cols)
    shares = [
        lax.psum_scatter(lax.psum(term, "tm"), line, scatter_dimension=0, tiled=True) * grad_scale
        for term in terms
    ]
    kernel_grad = jnp.transpose(shares[0].reshape(-1, 3, 3, channels), (1, 2, 0, 3))
    return x_grad[None], kernel_grad, shares[1], shares[2]


def solution(mesh):
    in_specs = (
        P(("groups", "tm"), ("space", "col"), None, None),
        P(),
        P(),
        P(),
        P(("groups", "tm"), None, ("space", "col"), None),
        P(("groups", "tm"), ("space", "col"), None, None),
    )
    out_specs = (
        P(("groups", "tm"), ("space", "col"), None, None),
        P(None, None, ("groups", "space", "col"), None),
        P(("groups", "space", "col"), None),
        P(("groups", "space", "col")),
    )
    return jax.shard_map(body, mesh=mesh, in_specs=in_specs, out_specs=out_specs, check_vma=False)
```

time: 127 us -> 47.3 us (0.37)
  blocking collectives: 45.8 us -> 0 us
  waiting for transfers between devices: 36 us -> 19 us
  between operations: 16.8 us -> 0.7 us
  starting transfers between devices: 3.18 us -> 15.7 us
  other arithmetic: 9.3 us -> 0 us
  matrix products: 6.28 us -> 0 us
  Pallas kernels: 0 us -> 4.39 us
  local copies, waits for them, and re-layouts: 9.32 us -> 6.92 us
    psum x1 -> x0, waiting for transfers between devices: 30.4 us -> none  [body(): lax.psum(kernel_term.astype(jnp.bfloat16), 'tm').astype(jnp.float32)]
    unnamed x1 -> x0, blocking collectives: 23 us -> none
    ppermute x2 -> x7, waiting for transfers between devices: 0.01 us -> 13.4 us  [the longest x3 9.13 us: body(): lax.ppermute(pieces[k], 'space', [(i, i ^ k) for i in range(spaces)])]
    all_to_all x1 -> x0, blocking collectives: 12.5 us -> none  [body(): lax.all_to_all(latent_grad, ('space', 'col'), split_axis=1, concat_axis=2...]
    psum x1 -> x0, blocking collectives: 10.3 us -> none  [body(): lax.psum(head_term.astype(jnp.bfloat16), 'tm').astype(jnp.float32)]
    all_to_all x0 -> x1, starting transfers between devices: none -> 7.07 us  [body(): lax.all_to_all(tiles, line, split_axis=0, concat_axis=0, tiled=True)]
    dot_general x30 -> x0, matrix products: 6.28 us -> none  [the longest x9 2 us: body(): jnp.einsum('trck,trco->ko', window_at(padded, index, row_count, col_count...]
    all_to_all x0 -> x1, waiting for transfers between devices: none -> 5.6 us  [body(): lax.all_to_all(tiles, line, split_axis=0, concat_axis=0, tiled=True)]
  transfers between devices with their start and end apart: 5 -> 8, of which waited for: 2 -> 5; matrix products, arithmetic and copies ran while one was open for 10% -> 3% of each run, Pallas kernels for 0% -> 3%
where the time goes in v1:
time: 47.3 us; the launch traced here: 46.8 us
  waiting for transfers between devices  19 us (40%)
  starting transfers between devices  15.7 us (33%)
  local copies, waits for them, and re-layouts  6.92 us (15%)
  Pallas kernels  4.39 us (9%)
  between operations  0.7 us (1%)
    ppermute x3, waiting for transfers between devices, body(): lax.ppermute(pieces[k], 'space', [(i, i ^ k) for i in range(spaces)])  9.13 us
    all_to_all x1, starting transfers between devices, body(): lax.all_to_all(tiles, line, split_axis=0, concat_axis=0, tiled=True)  7.07 us
    unnamed x14, local copies, waits for them, and re-layouts  5.95 us
    all_to_all x1, waiting for transfers between devices, body(): lax.all_to_all(tiles, line, split_axis=0, concat_axis=0, tiled=True)  5.6 us
    ppermute x3, starting transfers between devices, body(): lax.ppermute(pieces[k], 'space', [(i, i ^ k) for i in range(spaces)])  4.45 us
    pallas_call x5, Pallas kernels, call(): pl.pallas_call(kernel, out_shape=out_shape, in_specs=specs, out_specs=jax...  4.39 us
    ppermute x1, waiting for transfers between devices, body(): other = lax.ppermute(frame_term, 'tm', [(0, 1), (1, 0)])  2.27 us
    ppermute x1, waiting for transfers between devices, body(): got = lax.ppermute(send, 'col', [(0, 1), (1, 0)])  2.01 us
  transfers between devices with their start and end apart: 8, of which 5 were waited for; matrix products, arithmetic and copies ran while one was open for 3% of the time, Pallas kernels for 3%

profile of v1, /device:TPU:0, one launch (start us, length us, event | category | flops | bytes accessed | tf_op | source)
XLA Modules:
  0.0 46.8 jit_solution(1217312772682939743)
XLA Ops:
  0.6 1.0 %slice_bitcast_fusion = bf16[512,256]{1,0:T(8,128)(2,1)S(1)} fusion(bf16[1,2,512,256]{3,2,1,0:T(8,128)(2,1)} %param.6), kind=kLoop, calls=%fused_computation | loop fusion | bytes 524288 | tf_op jit(solution)/shard_map/squeeze | solution.py:177
  1.6 1.3 %collective-permute-start = (bf16[512,256]{1,0:T(8,128)(2,1)S(1)}, bf16[512,256]{1,0:T(8,128)(2,1)S(1)}, u32[]{:S(2)}, u32[]{:S(2)}) collective-permute-start(bf16[512,256]{1,0:T(8,128)(2,1)S(1)} %slice_bitcast_fusion), channel_id=1, source_target_pairs={{1,0},{4,1},{5,4},{8,5},{9,8},{12,9},{13,12},{3,2},{6,3},{7,6},{10... | collective-permute-start | bytes 786440 | tf_op jit(solution)/shard_map/ppermute | solution.py:177
  2.9 1.5 %reshape.32 = bf16[8,2,256]{2,1,0:T(2,128)(2,1)} reshape(bf16[8,16,32]{2,1,0:T(8,128)(2,1)} %bitcast.24) | data formatting | bytes 16384
  4.4 7.1 %all-to-all-start = ((bf16[8,2,256]{2,1,0:T(2,128)(2,1)}), bf16[8,2,256]{2,1,0:T(2,128)(2,1)S(1)}, u32[]{:S(2)}, u32[]{:S(2)}) async-start(bf16[8,2,256]{2,1,0:T(2,128)(2,1)} %reshape.32), calls=%async_computation | async-start | bytes 16384 | tf_op jit(solution)/shard_map/all_to_all | solution.py:179
  11.4 5.6 %all-to-all-done = bf16[8,2,256]{2,1,0:T(2,128)(2,1)S(1)} async-done(((bf16[8,2,256]{2,1,0:T(2,128)(2,1)}), bf16[8,2,256]{2,1,0:T(2,128)(2,1)S(1)}, u32[]{:S(2)}, u32[]{:S(2)}) %all-to-all-start) | async-done | bytes 8224 | tf_op jit(solution)/shard_map/all_to_all | solution.py:179
  17.0 0.1 reshape.33.up_ref
  17.1 0.0 collective-permute-done.next_ref
  17.1 0.0 copy-start
  17.1 1.3 %copy-done = bf16[3,3,256,256]{3,2,1,0:T(8,128)(2,1)S(1)} copy-done((bf16[3,3,256,256]{3,2,1,0:T(8,128)(2,1)S(1)}, bf16[3,3,256,256]{3,2,1,0:T(8,128)(2,1)}, u32[]{:S(2)}) %copy-start) | copy-done | bytes 1179672
  18.4 0.0 copy-start.2
  18.4 1.0 %copy-done.2 = bf16[1,2,512,256]{3,2,1,0:T(8,128)(2,1)S(1)} copy-done((bf16[1,2,512,256]{3,2,1,0:T(8,128)(2,1)S(1)}, bf16[1,2,512,256]{3,2,1,0:T(8,128)(2,1)}, u32[]{:S(2)}) %copy-start.2) | copy-done | bytes 524312
  19.4 0.0 copy-start.3
  19.5 0.7 %copy-done.3 = bf16[256,32]{0,1:T(8,128)(2,1)S(1)} copy-done((bf16[256,32]{0,1:T(8,128)(2,1)S(1)}, bf16[256,32]{0,1:T(8,128)(2,1)}, u32[]{:S(2)}) %copy-start.3) | copy-done | bytes 16408
  20.2 0.0 copy-start.4
  20.2 0.7 %copy-done.4 = bf16[1,1,256,16]{2,3,1,0:T(8,128)(2,1)S(1)} copy-done((bf16[1,1,256,16]{2,3,1,0:T(8,128)(2,1)S(1)}, bf16[1,1,256,16]{2,3,1,0:T(8,128)(2,1)}, u32[]{:S(2)}) %copy-start.4) | copy-done | bytes 8216
  20.9 0.0 copy-start.5
  20.9 0.7 %copy-done.5 = f32[256]{0:T(256)S(1)} copy-done((f32[256]{0:T(256)S(1)}, f32[256]{0:T(256)}, u32[]{:S(2)}) %copy-start.5) | copy-done | bytes 1048
  21.5 2.0 %shard_map.93 = (bf16[256,256]{1,0:T(8,128)(2,1)S(1)}, f32[4,296,256]{2,1,0:T(8,128)S(1)}, bf16[4,296,256]{2,1,0:T(8,128)(2,1)S(1)}) custom-call(s32[1]{0:T(128)} %bitcast.me_ref, bf16[2,512,256]{2,1,0:T(8,128)(2,1)S(1)} %bitcast.19, bf16[512,256]{1,0:T(8,128)(2,1)S(1)} %collective-permute-done.next_ref, bf16[9,256,256]{2,1,0:T(8,128)(2,1)S(1)} %bitcast.17, ...), custom_call_target="tpu_custom_call" | custom-call | flops 603979776 | bytes 6291456 | tf_op jit(solution)/shard_map/pallas_call | solution.py:30
  23.5 0.1 collective-permute-start.2
  23.6 2.0 %collective-permute-done.2.got_ref = bf16[4,296,256]{2,1,0:T(8,128)(2,1)S(1)} collective-permute-done((bf16[4,296,256]{2,1,0:T(8,128)(2,1)S(1)}, bf16[4,296,256]{2,1,0:T(8,128)(2,1)S(1)}, u32[]{:S(2)}, u32[]{:S(2)}) %collective-permute-start.2) | collective-permute-done | bytes 606240 | tf_op jit(solution)/shard_map/ppermute | solution.py:209
  25.6 0.0 copy-start.1
  25.6 0.1 shard_map.95
  25.8 0.7 %collective-permute-start.3 = (bf16[296,256]{1,0:T(8,128)(2,1)S(1)}, bf16[296,256]{1,0:T(8,128)(2,1)S(1)}, u32[]{:S(2)}, u32[]{:S(2)}) collective-permute-start(bf16[296,256]{1,0:T(8,128)(2,1)S(1)} %get-tuple-element.18), channel_id=1, source_target_pairs={{0,4},{4,0},{8,12},{12,8},{1,5},{5,1},{9,13},{13,9},{2,6},{6,2},{1... | collective-permute-start | bytes 454664 | tf_op jit(solution)/shard_map/ppermute | solution.py:221
  26.4 0.5 %collective-permute-start.4 = (bf16[296,256]{1,0:T(8,128)(2,1)S(1)}, bf16[296,256]{1,0:T(8,128)(2,1)S(1)}, u32[]{:S(2)}, u32[]{:S(2)}) collective-permute-start(bf16[296,256]{1,0:T(8,128)(2,1)S(1)} %get-tuple-element.19), channel_id=1, source_target_pairs={{0,8},{4,12},{8,0},{12,4},{1,9},{5,13},{9,1},{13,5},{2,10},{6,14},... | collective-permute-start | bytes 454664 | tf_op jit(solution)/shard_map/ppermute | solution.py:221
  27.0 3.3 %collective-permute-start.5 = (bf16[296,256]{1,0:T(8,128)(2,1)S(1)}, bf16[296,256]{1,0:T(8,128)(2,1)S(1)}, u32[]{:S(2)}, u32[]{:S(2)}) collective-permute-start(bf16[296,256]{1,0:T(8,128)(2,1)S(1)} %get-tuple-element.20), channel_id=1, source_target_pairs={{0,12},{4,8},{8,4},{12,0},{1,13},{5,9},{9,5},{13,1},{2,14},{6,10},... | collective-permute-start | bytes 454664 | tf_op jit(solution)/shard_map/ppermute | solution.py:221
  30.2 1.3 %collective-permute-start.1 = (bf16[256,256]{1,0:T(8,128)(2,1)S(1)}, bf16[256,256]{1,0:T(8,128)(2,1)S(1)}, u32[]{:S(2)}, u32[]{:S(2)}) collective-permute-start(bf16[256,256]{1,0:T(8,128)(2,1)S(1)} %get-tuple-element.14.pre_grad_ref), channel_id=1, source_target_pairs={{0,1},{1,4},{4,5},{5,8},{8,9},{9,12},{12,13},{2,3},{3,6},{6,7},{7,... | collective-permute-start | bytes 393224 | tf_op jit(solution)/shard_map/ppermute | solution.py:224
  31.5 2.4 %collective-permute-done.3.refs_0_ = bf16[296,256]{1,0:T(8,128)(2,1)S(1)} collective-permute-done((bf16[296,256]{1,0:T(8,128)(2,1)S(1)}, bf16[296,256]{1,0:T(8,128)(2,1)S(1)}, u32[]{:S(2)}, u32[]{:S(2)}) %collective-permute-start.3) | collective-permute-done | bytes 151584 | tf_op jit(solution)/shard_map/ppermute | solution.py:221
  33.9 6.7 %collective-permute-done.4.refs_1_ = bf16[296,256]{1,0:T(8,128)(2,1)S(1)} collective-permute-done((bf16[296,256]{1,0:T(8,128)(2,1)S(1)}, bf16[296,256]{1,0:T(8,128)(2,1)S(1)}, u32[]{:S(2)}, u32[]{:S(2)}) %collective-permute-start.4) | collective-permute-done | bytes 151584 | tf_op jit(solution)/shard_map/ppermute | solution.py:221
  40.6 0.0 collective-permute-done.5.refs_2_
  40.6 0.1 shard_map.96.a_ref
  40.7 1.6 %collective-permute-start.6 = (bf16[296,256]{1,0:T(8,128)(2,1)S(1)}, bf16[296,256]{1,0:T(8,128)(2,1)S(1)}, u32[]{:S(2)}, u32[]{:S(2)}) collective-permute-start(bf16[296,256]{1,0:T(8,128)(2,1)S(1)} %shard_map.96.a_ref), channel_id=1, source_target_pairs={{0,2},{2,0},{1,3},{3,1},{4,6},{6,4},{5,7},{7,5},{8,10},{10,8},{9,1... | collective-permute-start | bytes 454664 | tf_op jit(solution)/shard_map/ppermute | solution.py:239
  42.3 0.0 collective-permute-done.1.prev_ref
  42.3 0.0 copy-done.1
  42.3 1.4 %shard_map.94 = bf16[2,512,256]{2,1,0:T(8,128)(2,1)} custom-call(bf16[256,256]{1,0:T(8,128)(2,1)S(1)} %get-tuple-element.14.pre_grad_ref, bf16[256,256]{1,0:T(8,128)(2,1)S(1)} %collective-permute-done.1.prev_ref, bf16[9,256,256]{2,1,0:T(8,128)(2,1)S(1)} %bitcast.18), custom_call_target="tpu_custom_call" | custom-call | flops 301989888 | bytes 4194304 | tf_op jit(solution)/shard_map/pallas_call | solution.py:30
  43.7 2.3 %collective-permute-done.6.b_ref = bf16[296,256]{1,0:T(8,128)(2,1)S(1)} collective-permute-done((bf16[296,256]{1,0:T(8,128)(2,1)S(1)}, bf16[296,256]{1,0:T(8,128)(2,1)S(1)}, u32[]{:S(2)}, u32[]{:S(2)}) %collective-permute-start.6) | collective-permute-done | bytes 151584 | tf_op jit(solution)/shard_map/ppermute | solution.py:239
  46.0 0.8 %shard_map.97 = (f32[9,32,256]{2,1,0:T(8,128)}, f32[32,32]{1,0:T(8,128)}, f32[1,32]{1,0:T(1,128)}) custom-call(bf16[296,256]{1,0:T(8,128)(2,1)S(1)} %shard_map.96.a_ref, bf16[296,256]{1,0:T(8,128)(2,1)S(1)} %collective-permute-done.6.b_ref), custom_call_target="tpu_custom_call" | custom-call | flops 75776 | bytes 1048576 | tf_op jit(solution)/shard_map/pallas_call | solution.py:30
Async XLA Ops:
  1.6 15.5 %collective-permute-start = (bf16[512,256]{1,0:T(8,128)(2,1)S(1)}, bf16[512,256]{1,0:T(8,128)(2,1)S(1)}, u32[]{:S(2)}, u32[]{:S(2)}) collective-permute-start(bf16[512,256]{1,0:T(8,128)(2,1)S(1)} %slice_bitcast_fusion), channel_id=1, source_target_pairs={{1,0},{4,1},{5,4},{8,5},{9,8},{12,9},{13,12},{3,2},{6,3},{7,6},{10... | collective-permute-start | bytes 786440 | tf_op jit(solution)/shard_map/ppermute | solution.py:177
  4.4 12.7 %all-to-all-start = ((bf16[8,2,256]{2,1,0:T(2,128)(2,1)}), bf16[8,2,256]{2,1,0:T(2,128)(2,1)S(1)}, u32[]{:S(2)}, u32[]{:S(2)}) async-start(bf16[8,2,256]{2,1,0:T(2,128)(2,1)} %reshape.32), calls=%async_computation | async-start | bytes 16384 | tf_op jit(solution)/shard_map/all_to_all | solution.py:179
  17.1 1.3 %copy-start = (bf16[3,3,256,256]{3,2,1,0:T(8,128)(2,1)S(1)}, bf16[3,3,256,256]{3,2,1,0:T(8,128)(2,1)}, u32[]{:S(2)}) copy-start(bf16[3,3,256,256]{3,2,1,0:T(8,128)(2,1)} %param.7) | copy-start | bytes 3538948
  18.4 1.0 %copy-start.2 = (bf16[1,2,512,256]{3,2,1,0:T(8,128)(2,1)S(1)}, bf16[1,2,512,256]{3,2,1,0:T(8,128)(2,1)}, u32[]{:S(2)}) copy-start(bf16[1,2,512,256]{3,2,1,0:T(8,128)(2,1)} %param.6) | copy-start | bytes 1572868
  19.4 0.7 %copy-start.3 = (bf16[256,32]{0,1:T(8,128)(2,1)S(1)}, bf16[256,32]{0,1:T(8,128)(2,1)}, u32[]{:S(2)}) copy-start(bf16[256,32]{0,1:T(8,128)(2,1)} %param.9) | copy-start | bytes 49156
  20.2 0.7 %copy-start.4 = (bf16[1,1,256,16]{2,3,1,0:T(8,128)(2,1)S(1)}, bf16[1,1,256,16]{2,3,1,0:T(8,128)(2,1)}, u32[]{:S(2)}) copy-start(bf16[1,1,256,16]{2,3,1,0:T(8,128)(2,1)} %param.11) | copy-start | bytes 24580
  20.9 0.7 %copy-start.5 = (f32[256]{0:T(256)S(1)}, f32[256]{0:T(256)}, u32[]{:S(2)}) copy-start(f32[256]{0:T(256)} %param.8) | copy-start | bytes 3076
  23.5 2.1 %collective-permute-start.2 = (bf16[4,296,256]{2,1,0:T(8,128)(2,1)S(1)}, bf16[4,296,256]{2,1,0:T(8,128)(2,1)S(1)}, u32[]{:S(2)}, u32[]{:S(2)}) collective-permute-start(bf16[4,296,256]{2,1,0:T(8,128)(2,1)S(1)} %get-tuple-element.16), channel_id=1, source_target_pairs={{0,1},{1,0},{2,3},{3,2},{4,5},{5,4},{6,7},{7,6},{8,9},{9,8},{10,11... | collective-permute-start | bytes 1818632 | tf_op jit(solution)/shard_map/ppermute | solution.py:209
  25.6 16.7 %copy-start.1 = (bf16[3,3,256,256]{3,2,1,0:T(8,128)(2,1)S(1)}, bf16[3,3,256,256]{3,2,1,0:T(8,128)(2,1)}, u32[]{:S(2)}) copy-start(bf16[3,3,256,256]{3,2,1,0:T(8,128)(2,1)} %param.7) | copy-start | bytes 3538948
  25.8 8.1 %collective-permute-start.3 = (bf16[296,256]{1,0:T(8,128)(2,1)S(1)}, bf16[296,256]{1,0:T(8,128)(2,1)S(1)}, u32[]{:S(2)}, u32[]{:S(2)}) collective-permute-start(bf16[296,256]{1,0:T(8,128)(2,1)S(1)} %get-tuple-element.18), channel_id=1, source_target_pairs={{0,4},{4,0},{8,12},{12,8},{1,5},{5,1},{9,13},{13,9},{2,6},{6,2},{1... | collective-permute-start | bytes 454664 | tf_op jit(solution)/shard_map/ppermute | solution.py:221
  26.4 14.2 %collective-permute-start.4 = (bf16[296,256]{1,0:T(8,128)(2,1)S(1)}, bf16[296,256]{1,0:T(8,128)(2,1)S(1)}, u32[]{:S(2)}, u32[]{:S(2)}) collective-permute-start(bf16[296,256]{1,0:T(8,128)(2,1)S(1)} %get-tuple-element.19), channel_id=1, source_target_pairs={{0,8},{4,12},{8,0},{12,4},{1,9},{5,13},{9,1},{13,5},{2,10},{6,14},... | collective-permute-start | bytes 454664 | tf_op jit(solution)/shard_map/ppermute | solution.py:221
  27.0 13.7 %collective-permute-start.5 = (bf16[296,256]{1,0:T(8,128)(2,1)S(1)}, bf16[296,256]{1,0:T(8,128)(2,1)S(1)}, u32[]{:S(2)}, u32[]{:S(2)}) collective-permute-start(bf16[296,256]{1,0:T(8,128)(2,1)S(1)} %get-tuple-element.20), channel_id=1, source_target_pairs={{0,12},{4,8},{8,4},{12,0},{1,13},{5,9},{9,5},{13,1},{2,14},{6,10},... | collective-permute-start | bytes 454664 | tf_op jit(solution)/shard_map/ppermute | solution.py:221
  30.2 12.1 %collective-permute-start.1 = (bf16[256,256]{1,0:T(8,128)(2,1)S(1)}, bf16[256,256]{1,0:T(8,128)(2,1)S(1)}, u32[]{:S(2)}, u32[]{:S(2)}) collective-permute-start(bf16[256,256]{1,0:T(8,128)(2,1)S(1)} %get-tuple-element.14.pre_grad_ref), channel_id=1, source_target_pairs={{0,1},{1,4},{4,5},{5,8},{8,9},{9,12},{12,13},{2,3},{3,6},{6,7},{7,... | collective-permute-start | bytes 393224 | tf_op jit(solution)/shard_map/ppermute | solution.py:224
  40.7 5.3 %collective-permute-start.6 = (bf16[296,256]{1,0:T(8,128)(2,1)S(1)}, bf16[296,256]{1,0:T(8,128)(2,1)S(1)}, u32[]{:S(2)}, u32[]{:S(2)}) collective-permute-start(bf16[296,256]{1,0:T(8,128)(2,1)S(1)} %shard_map.96.a_ref), channel_id=1, source_target_pairs={{0,2},{2,0},{1,3},{3,1},{4,6},{6,4},{5,7},{7,5},{8,10},{10,8},{9,1... | collective-permute-start | bytes 454664 | tf_op jit(solution)/shard_map/ppermute | solution.py:239

commit v2 on v1

v2 whole, which is shorter than its diff:
```python
import functools
import math

import jax
import jax.numpy as jnp
from jax import lax
from jax.experimental import pallas as pl
from jax.experimental.pallas import tpu as pltpu
from jax.sharding import PartitionSpec as P

f32 = jnp.float32
bf16 = jnp.bfloat16
kl_weight = 1.0
LANES = 128
HALVED = 6
TAIL = 8


def dot(a, b, ca, cb):
    return lax.dot_general(a, b, (((ca,), (cb,)), ((), ())), preferred_element_type=f32)


def params():
    return pltpu.CompilerParams(vmem_limit_bytes=24 << 20)


SPACES = {"s": pltpu.SMEM, "v": pltpu.VMEM, "h": pltpu.HBM}


def full_call(kernel, out_shape, scratch, flops, moved, places):
    call = pl.pallas_call(
        kernel,
        out_shape=out_shape,
        in_specs=[pl.BlockSpec(memory_space=SPACES[place]) for place in places],
        out_specs=jax.tree.map(lambda _: pl.BlockSpec(memory_space=pltpu.VMEM), out_shape),
        scratch_shapes=scratch,
        compiler_params=params(),
        cost_estimate=pl.CostEstimate(flops=flops, bytes_accessed=moved, transcendentals=0),
    )

    def placed(*args):
        pinned = [
            pltpu.with_memory_space_constraint(arg, pltpu.HBM) if place == "h" else arg
            for arg, place in zip(args, places)
        ]
        return call(*pinned)

    return placed


def start_kernel(core_ref, act_ref, tiles_ref, row_ref, later_ref, own_ref, send_ref, sems):
    core = core_ref[0]
    half = later_ref.shape[0]
    copies = [
        pltpu.make_async_copy(act_ref.at[0, pl.ds(half, half)], later_ref, sems.at[0]),
        pltpu.make_async_copy(act_ref.at[0], row_ref, sems.at[1]),
    ]
    for j in range(own_ref.shape[0]):
        mine = tiles_ref.at[2 * j + core]
        theirs = tiles_ref.at[2 * j + 1 - core]
        copies.append(pltpu.make_async_copy(mine, own_ref.at[j], sems.at[2 + 2 * j]))
        copies.append(pltpu.make_async_copy(theirs, send_ref.at[j], sems.at[3 + 2 * j]))
    for copy in copies:
        copy.start()
    for copy in copies:
        copy.wait()


def tiles_kernel(core_ref, space_ref, row_ref, later_ref, own_ref, got_ref, *outs):
    spaces = own_ref.shape[0]
    height, width = own_ref.shape[1:]
    half = later_ref.shape[0]
    first = core_ref[0] == 0
    down = outs[-1]
    down[:half, :] = jnp.where(first, row_ref[:half, :], later_ref[...])
    for k, out in enumerate(outs):
        at = lax.rem(space_ref[0] + k, spaces)
        mine, other = own_ref[at], got_ref[at]
        top = half if k == spaces - 1 else 0
        lanes = out.shape[1]
        pieces = [jnp.where(first, mine, other), jnp.where(first, other, mine)]
        pieces.append(jnp.zeros((height, lanes - 2 * width), bf16))
        out[top:, :] = jnp.concatenate(pieces, 1)


def split_columns(row, source, stage):
    length, width = source.shape
    lanes = width // LANES
    source = source.astype(f32)
    for lane in range(lanes):
        stage[row * lanes + lane, :length, :] = source[:, lane * LANES : (lane + 1) * LANES]
        stage[row * lanes + lane, length:, :] = jnp.zeros((8, LANES), f32)
    windows = []
    for tap in range(3):
        halves = [
            stage[row * lanes + lane, pl.ds(tap, length // 2, stride=2), :]
            for lane in range(lanes)
        ]
        windows.append(jnp.concatenate(halves, 1).astype(bf16))
    return windows


def early_kernel(
    act_ref, w_in, bias_in, head_in, noise_in,
    windows_ref, pre_act_ref, w_ref, head_ref, noise_ref, act, bias, stage, sems,
):
    pairs = [
        (act_ref.at[0], act.at[0]), (w_in.at[:3], w_ref.at[:3]),
        (act_ref.at[1], act.at[1]), (w_in.at[3:6], w_ref.at[3:6]),
        (bias_in, bias), (w_in.at[6:], w_ref.at[6:]), (head_in, head_ref), (noise_in, noise_ref),
    ]
    copies = [pltpu.make_async_copy(a, b, sems.at[i]) for i, (a, b) in enumerate(pairs)]
    for copy in copies:
        copy.start()
    copies[4].wait()
    pre_act = jnp.broadcast_to(bias[...], pre_act_ref.shape)
    for row in range(2):
        copies[2 * row].wait()
        windows = split_columns(row, act[row], stage)
        copies[2 * row + 1].wait()
        for tap in range(3):
            windows_ref[3 * row + tap] = windows[tap]
            pre_act = pre_act + dot(windows[tap], w_ref[3 * row + tap], 1, 0)
    pre_act_ref[...] = pre_act
    for copy in copies[5:]:
        copy.wait()


def terms_kernel(
    core_ref, space_ref, windows_ref, early_ref, w_ref, head_ref, noise_ref,
    beside_ref, fixed_ref, *rest,
):
    spaces = len(rest) - 7
    tiles = rest[:spaces]
    pre_grad_ref, keep_a, send_a, keep_b, send_b, tiles_at, stage = rest[spaces:]
    cols, width = pre_grad_ref.shape
    latent = noise_ref.shape[0]
    share = width // (2 * spaces)
    first = core_ref[0] == 0
    height, lanes = tiles_at.shape[1:]
    for k in range(spaces):
        top = tiles[k].shape[0] - height
        tiles_at[lax.rem(space_ref[0] + spaces - k, spaces)] = tiles[k][top:, :lanes]
    half = tiles[-1].shape[0] - height
    above = jnp.concatenate([fixed_ref[:half, :], tiles[-1][:half, :]], 0)
    above = jnp.where(space_ref[0] == spaces - 1, jnp.zeros_like(above), above)
    next_row = jnp.where(first, beside_ref[...], above)
    windows = [windows_ref[i] for i in range(6)] + split_columns(0, next_row, stage)
    pre_act = early_ref[...]
    for index in range(6, 9):
        pre_act = pre_act + dot(windows[index], w_ref[index], 1, 0)
    gating = jax.nn.sigmoid(pre_act)
    hidden = (pre_act * gating).astype(bf16)
    moments = dot(head_ref[...], hidden, 1, 1)
    mean_part = moments[:latent]
    logvar = moments[latent:]
    upstream = jnp.concatenate(
        [tiles_at[i][:, : cols // spaces].astype(f32) for i in range(spaces)], 1
    )
    sample = noise_ref[...].astype(f32)
    spread = jnp.exp(0.5 * logvar)
    mean_grad = upstream + kl_weight * mean_part
    logvar_grad = 0.5 * upstream * sample * spread + 0.5 * kl_weight * (spread * spread - 1.0)
    moment_grad = jnp.concatenate([mean_grad, logvar_grad], 0).astype(bf16)
    hidden_grad = dot(moment_grad, head_ref[...], 0, 0)
    pre_grad = (hidden_grad * gating * (1.0 + pre_act * (1.0 - gating))).astype(bf16)
    pre_grad_ref[...] = pre_grad

    def put(keep_ref, send_ref, s, at, even, odd):
        here = slice(at, at + even.shape[0])
        keep_ref[s, here, :] = jnp.where(first, even, odd)
        send_ref[s, here, :] = jnp.where(first, odd, even).astype(bf16)

    for index in range(9):
        term = dot(windows[index], pre_grad, 0, 0)
        refs = (keep_a, send_a) if index < HALVED else (keep_b, send_b)
        at = share * (index if index < HALVED else index - HALVED)
        for s in range(spaces):
            row = 2 * share * s
            put(*refs, s, at, term[row : row + share], term[row + share : row + 2 * share])
    head_term = dot(hidden, moment_grad, 0, 1)
    bias_term = dot(jnp.ones((TAIL, cols), bf16), pre_grad, 1, 0)

    def tail(row):
        pieces = [head_term[row + i : row + i + TAIL] for i in range(0, share, TAIL)]
        pieces.append(bias_term[:, row : row + share])
        used = sum(piece.shape[1] for piece in pieces)
        pieces.append(jnp.zeros((TAIL, width - used), f32))
        return jnp.concatenate(pieces, 1)

    for s in range(spaces):
        row = 2 * share * s
        put(keep_b, send_b, s, (9 - HALVED) * share, tail(row), tail(row + share))


def halve_kernel(time_ref, keep_ref, got_ref, own_ref, send_ref):
    half = own_ref.shape[2]
    first = time_ref[0] == 0
    total = keep_ref[...] + got_ref[...].astype(f32)
    own_ref[...] = jnp.where(first, total[:, :, :half], total[:, :, half:])
    send_ref[...] = jnp.where(first, total[:, :, half:], total[:, :, :half]).astype(bf16)


def pair_kernel(space_ref, keep_ref, got_ref, *outs):
    spaces = len(outs)
    for k, out in enumerate(outs):
        at = lax.rem(space_ref[0] + k, spaces)
        out[...] = (keep_ref[at] + got_ref[at].astype(f32)).astype(out.dtype)


def pair_rim_kernel(core_ref, space_ref, keep_ref, got_ref, mine_ref, beside_ref, *outs):
    spaces = len(outs)
    rows = keep_ref.shape[1]
    for k, out in enumerate(outs):
        at = lax.rem(space_ref[0] + k, spaces)
        out[:rows, :] = (keep_ref[at] + got_ref[at].astype(f32)).astype(out.dtype)
    half = mine_ref.shape[0] // 2
    first = core_ref[0] == 0
    outs[1][rows:, :] = jnp.where(first, beside_ref[half:, :], mine_ref[:half, :])


def line_kernel(own_ref, *refs):
    total = own_ref[...]
    for ref in refs[:-1]:
        total = total + ref[...].astype(f32)
    refs[-1][...] = total.astype(bf16)


def line_rim_kernel(own_ref, *refs):
    rows = own_ref.shape[0]
    total = own_ref[...]
    for ref in refs[:-2]:
        total = total + ref[:rows, :].astype(f32)
    refs[-2][...] = total.astype(bf16)
    refs[-1][...] = refs[0][rows:, :]


def final_kernel(
    scale, time_ref, a_ref, a_far_ref, b_ref, b_far_ref, kernel_ref, head_ref, bias_ref
):
    share, latents = head_ref.shape
    first = time_ref[0] == 0
    mine, far = a_ref[...].astype(f32) * scale, a_far_ref[...].astype(f32) * scale
    low, high = jnp.where(first, mine, far), jnp.where(first, far, mine)
    total = (b_ref[...].astype(f32) + b_far_ref[...].astype(f32)) * scale
    half = mine.shape[1]
    for index in range(HALVED):
        kernel_ref[index, :, :half] = low[index * share : (index + 1) * share]
        kernel_ref[index, :, half:] = high[index * share : (index + 1) * share]
    for index in range(HALVED, 9):
        at = (index - HALVED) * share
        kernel_ref[index] = total[at : at + share]
    tail = total[(9 - HALVED) * share :]
    for i in range(share // TAIL):
        head_ref[TAIL * i : TAIL * (i + 1), :] = tail[:, latents * i : latents * (i + 1)]
    at = latents * (share // TAIL)
    bias_ref[...] = tail[:1, at : at + share]


def input_kernel(pre_grad_ref, prev_ref, w_ref, out_ref, stage):
    input_rows(pre_grad_ref, prev_ref[...], w_ref, out_ref, stage)


def input_chip_kernel(
    core_ref, space_ref, pre_grad_ref, beside_ref, low_ref, high_ref, w_ref, out_ref, stage
):
    below = jnp.concatenate([low_ref[...], high_ref[...]], 0)
    below = jnp.where(space_ref[0] == 0, jnp.zeros_like(below), below)
    prev = jnp.where(core_ref[0] == 0, below, beside_ref[...])
    input_rows(pre_grad_ref, prev, w_ref, out_ref, stage)


def input_rows(pre_grad_ref, prev, w_ref, out_ref, stage):
    cols, width = pre_grad_ref.shape
    pre_grad = pre_grad_ref[...]
    row_at = lax.broadcasted_iota(jnp.int32, (cols, width), 0)

    def planes(source, row_tap):
        even = dot(source, w_ref[3 * row_tap], 1, 1)
        odd = dot(source, w_ref[3 * row_tap + 1], 1, 1)
        late = pltpu.roll(dot(source, w_ref[3 * row_tap + 2], 1, 1), 1, 0)
        return even + jnp.where(row_at == 0, 0.0, late), odd

    def weave(row, even, odd):
        for lane in range(width // LANES):
            at = row * (width // LANES) + lane
            here = slice(lane * LANES, (lane + 1) * LANES)
            stage[at, pl.ds(0, cols, stride=2), :] = even[:, here]
            stage[at, pl.ds(1, cols, stride=2), :] = odd[:, here]
            out_ref[row, :, here] = stage[at].astype(bf16)

    even, odd = planes(pre_grad, 1)
    weave(1, even, odd)
    even, odd = planes(pre_grad, 0)
    even_rim, odd_rim = planes(prev, 2)
    weave(0, even + even_rim, odd + odd_rim)


def body(activations, conv_weight, conv_bias, head_weight, latent_grad, noise_sample):
    frames, double_rows, double_cols, channels = activations.shape
    cols = double_cols // 2
    latent_dim = latent_grad.shape[-1]
    spaces = lax.axis_size("space")
    times = lax.axis_size("tm")
    line = ("space", "col")
    peers = lax.axis_size(line)
    assert frames == 1 and double_rows == 2 and lax.axis_size("col") == 2
    share = channels // peers
    taps = conv_weight.reshape(9, channels, channels)
    tiles = jnp.transpose(latent_grad[0], (0, 2, 1))
    if share % TAIL or not 2 <= spaces <= 4 or times != 2:
        return wide_body(activations, taps, conv_bias, head_weight, tiles, noise_sample)
    core_at = lax.axis_index("col").astype(jnp.int32).reshape(1)
    space_at = lax.axis_index("space").astype(jnp.int32).reshape(1)
    time_at = lax.axis_index("tm").astype(jnp.int32).reshape(1)
    swap = [(0, 1), (1, 0)]
    hops = list(range(spaces - 1, 0, -1))
    down = spaces - 1
    array = jax.ShapeDtypeStruct

    def over_space(pieces):
        sent = {
            k: lax.ppermute(pieces[k], "space", [(i, (i + k) % spaces) for i in range(spaces)])
            for k in hops
        }
        return [sent[k] for k in range(1, spaces)]

    tile = tiles.shape[1:]
    row, later, own_tiles, send_tiles = full_call(
        start_kernel,
        (
            array((double_cols, channels), bf16),
            array((cols, channels), bf16),
            array((spaces, *tile), bf16),
            array((spaces, *tile), bf16),
        ),
        [pltpu.SemaphoreType.DMA((2 + 2 * spaces,))],
        0,
        1 << 19,
        "shh",
    )(core_at, activations[0], tiles)
    got_tiles = lax.ppermute(send_tiles, "col", swap)
    got_later = lax.ppermute(later, "col", swap)
    tile_sets = full_call(
        tiles_kernel,
        tuple(
            array((cols + tile[0], channels) if k == down else (tile[0], LANES), bf16)
            for k in range(spaces)
        ),
        [],
        0,
        1 << 15,
        "ssvvvv",
    )(core_at, space_at, row, got_later, own_tiles, got_tiles)
    far_tiles = over_space(tile_sets)
    beside = lax.ppermute(row, "col", swap)
    square = 2 * cols * channels * channels
    windows, early, w_here, head_here, noise_here = full_call(
        early_kernel,
        (
            array((6, cols, channels), bf16),
            array((cols, channels), f32),
            array(taps.shape, bf16),
            array((2 * latent_dim, channels), bf16),
            array((latent_dim, cols), bf16),
        ),
        [
            pltpu.VMEM((2, double_cols, channels), bf16),
            pltpu.VMEM((1, channels), f32),
            pltpu.VMEM((2 * (channels // LANES), double_cols + 8, LANES), f32),
            pltpu.SemaphoreType.DMA((8,)),
        ],
        6 * square,
        5 << 20,
        "hhhhh",
    )(
        activations[0],
        taps,
        conv_bias.reshape(1, channels),
        head_weight.T,
        jnp.transpose(noise_sample[0, 0]),
    )
    early, *far_tiles = lax.optimization_barrier((early, *far_tiles))
    fixed = lax.ppermute(far_tiles[-1], "col", swap)
    rows_a = HALVED * share
    rows_b = (9 - HALVED) * share + TAIL
    half = channels // 2
    pre_grad, keep_a, send_a, keep_b, send_b = full_call(
        terms_kernel,
        (
            array((cols, channels), bf16),
            array((spaces, rows_a, channels), f32),
            array((spaces, rows_a, channels), bf16),
            array((spaces, rows_b, channels), f32),
            array((spaces, rows_b, channels), bf16),
        ),
        [
            pltpu.VMEM((spaces, tile[0], LANES), bf16),
            pltpu.VMEM((channels // LANES, double_cols + 8, LANES), f32),
        ],
        12 * square,
        5 << 20,
        "ss" + "v" * (7 + spaces),
    )(
        core_at, space_at, windows, early, w_here, head_here, noise_here, beside, fixed,
        tile_sets[0], *far_tiles,
    )
    beside_grad = lax.ppermute(pre_grad, "col", swap)
    got_a = lax.ppermute(send_a, "col", swap)
    got_b = lax.ppermute(send_b, "col", swap)
    own_a, cross_a = full_call(
        halve_kernel,
        (array((spaces, rows_a, half), f32), array((spaces, rows_a, half), bf16)),
        [],
        spaces * rows_a * channels,
        2 << 20,
        "svv",
    )(time_at, keep_a, got_a)
    crossed_a = lax.ppermute(cross_a, "tm", swap)

    half_grad = cols // 2
    pieces_b = full_call(
        pair_rim_kernel,
        tuple(
            array((rows_b + (half_grad if k == 1 else 0), channels), f32 if k == 0 else bf16)
            for k in range(spaces)
        ),
        [],
        spaces * rows_b * channels,
        1 << 20,
        "ssvvvv",
    )(core_at, space_at, keep_b, got_b, pre_grad, beside_grad)
    far_b = over_space(pieces_b)
    pieces_a = full_call(
        pair_kernel,
        tuple(array((rows_a, half), f32 if k == 0 else bf16) for k in range(spaces)),
        [],
        spaces * rows_a * half,
        1 << 20,
        "svv",
    )(space_at, own_a, crossed_a)
    far_a = over_space(pieces_a)
    sum_b, high = full_call(
        line_rim_kernel,
        (array((rows_b, channels), bf16), array((half_grad, channels), bf16)),
        [],
        4 * rows_b * channels,
        1 << 19,
        "v" * spaces,
    )(pieces_b[0], *far_b)
    other_b = lax.ppermute(sum_b, "tm", swap)
    low = lax.ppermute(high, "col", swap)
    sum_a = full_call(
        line_kernel, array((rows_a, half), bf16), [], 4 * rows_a * half, 1 << 19, "v" * spaces
    )(pieces_a[0], *far_a)
    other_a = lax.ppermute(sum_a, "tm", swap)
    x_grad = full_call(
        input_chip_kernel,
        array((2, double_cols, channels), bf16),
        [pltpu.VMEM((2 * (channels // LANES), double_cols, LANES), f32)],
        9 * square,
        4 << 20,
        "ssvvvvv",
    )(core_at, space_at, pre_grad, beside_grad, low, high, w_here)
    positions = frames * times * peers * cols
    kernel_grad, head_grad, bias_grad = full_call(
        functools.partial(final_kernel, 1.0 / math.sqrt(positions)),
        (
            array((9, share, channels), f32),
            array((share, 2 * latent_dim), f32),
            array((1, share), f32),
        ),
        [],
        rows_a * half + rows_b * channels,
        1 << 20,
        "svvvv",
    )(time_at, sum_a, other_a, sum_b, other_b)
    return (
        x_grad[None],
        kernel_grad.reshape(3, 3, share, channels),
        head_grad,
        bias_grad.reshape(share),
    )


def input_gradient(pre_grad, prev, taps):
    cols, channels = pre_grad.shape
    return full_call(
        input_kernel,
        jax.ShapeDtypeStruct((2, 2 * cols, channels), bf16),
        [pltpu.VMEM((2 * (channels // LANES), 2 * cols, LANES), f32)],
        18 * cols * channels * channels,
        4 << 20,
        "vvv",
    )(pre_grad, prev, taps)


def wide_body(activations, taps, conv_bias, head_weight, tiles, noise_sample):
    _, _, double_cols, channels = activations.shape
    cols = double_cols // 2
    latent_dim = noise_sample.shape[-1]
    line = ("space", "col")
    peers = lax.axis_size(line)
    next_row = lax.ppermute(activations[0, 0], line, [(i, i - 1) for i in range(1, peers)])
    upstream = lax.all_to_all(tiles, line, split_axis=0, concat_axis=0, tiled=True)
    padded = jnp.pad(jnp.concatenate([activations[0], next_row[None]], 0), ((0, 0), (0, 1), (0, 0)))
    windows = [
        padded[index // 3, index % 3 : index % 3 + 2 * cols : 2] for index in range(9)
    ]
    pre_act = jnp.zeros((cols, channels), f32) + conv_bias
    for index in range(9):
        pre_act = pre_act + dot(windows[index], taps[index], 1, 0)
    gating = jax.nn.sigmoid(pre_act)
    hidden = (pre_act * gating).astype(bf16)
    moments = dot(hidden, head_weight, 1, 0)
    upstream = jnp.transpose(upstream, (0, 2, 1)).reshape(cols, latent_dim).astype(f32)
    spread = jnp.exp(0.5 * moments[:, latent_dim:])
    mean_grad = upstream + kl_weight * moments[:, :latent_dim]
    logvar_grad = 0.5 * upstream * noise_sample[0, 0].astype(f32) * spread
    logvar_grad = logvar_grad + 0.5 * kl_weight * (spread * spread - 1.0)
    moment_grad = jnp.concatenate([mean_grad, logvar_grad], 1).astype(bf16)
    hidden_grad = dot(moment_grad, head_weight, 1, 1)
    pre_grad = (hidden_grad * gating * (1.0 + pre_act * (1.0 - gating))).astype(bf16)
    prev = lax.ppermute(pre_grad, line, [(i, i + 1) for i in range(peers - 1)])
    x_grad = input_gradient(pre_grad, prev, taps)
    kernel_term = jnp.stack([dot(window, pre_grad, 0, 0) for window in windows], 1)
    terms = (
        kernel_term.reshape(channels, 9 * channels),
        dot(hidden, moment_grad, 0, 0),
        jnp.sum(pre_grad, axis=0, dtype=f32),
    )
    grad_scale = 1.0 / math.sqrt(lax.axis_size("tm") * peers * cols)
    shares = [
        lax.psum_scatter(lax.psum(term, "tm"), line, scatter_dimension=0, tiled=True) * grad_scale
        for term in terms
    ]
    kernel_grad = jnp.transpose(shares[0].reshape(-1, 3, 3, channels), (1, 2, 0, 3))
    return x_grad[None], kernel_grad, shares[1], shares[2]


def solution(mesh):
    in_specs = (
        P(("groups", "tm"), ("space", "col"), None, None),
        P(),
        P(),
        P(),
        P(("groups", "tm"), None, ("space", "col"), None),
        P(("groups", "tm"), ("space", "col"), None, None),
    )
    out_specs = (
        P(("groups", "tm"), ("space", "col"), None, None),
        P(None, None, ("groups", "space", "col"), None),
        P(("groups", "space", "col"), None),
        P(("groups", "space", "col")),
    )
    return jax.shard_map(body, mesh=mesh, in_specs=in_specs, out_specs=out_specs, check_vma=False)
```

time: 47.3 us -> 39.9 us (0.84)
  waiting for transfers between devices: 19 us -> 11.2 us
  local copies, waits for them, and re-layouts: 6.92 us -> 0 us
  starting transfers between devices: 15.7 us -> 20.1 us
  Pallas kernels: 4.39 us -> 7.68 us
    ppermute x7 -> x20, starting transfers between devices: 8.65 us -> 20.1 us  [the longest x9 16 us: over_space(): lax.ppermute(pieces[k], 'space', [(i, (i + k) % spaces) for i in range(sp...]
    all_to_all x1 -> x0, starting transfers between devices: 7.07 us -> none  [body(): lax.all_to_all(tiles, line, split_axis=0, concat_axis=0, tiled=True)]
    unnamed x14 -> x0, local copies, waits for them, and re-layouts: 5.95 us -> none
    all_to_all x1 -> x0, waiting for transfers between devices: 5.6 us -> none  [body(): lax.all_to_all(tiles, line, split_axis=0, concat_axis=0, tiled=True)]
    pallas_call x5 -> x11, Pallas kernels: 4.39 us -> 7.68 us  [placed(): return call(*pinned)]
    ppermute x7 -> x20, waiting for transfers between devices: 13.4 us -> 11.2 us  [the longest x9 4.87 us: over_space(): lax.ppermute(pieces[k], 'space', [(i, (i + k) % spaces) for i in range(sp...]
    squeeze x1 -> x0, local copies, waits for them, and re-layouts: 0.97 us -> none  [body(): activations[0, 0]]
  transfers between devices with their start and end apart: 8 -> 20, of which waited for: 5 -> 10; matrix products, arithmetic and copies ran while one was open for 3% -> 0% of each run, Pallas kernels for 3% -> 9%
where the time goes in v2:
time: 39.9 us; the launch traced here: 39.7 us
  starting transfers between devices  20.1 us (50%)
  waiting for transfers between devices  11.2 us (28%)
  Pallas kernels  7.68 us (19%)
  between operations  0.71 us (2%)
    ppermute x9, starting transfers between devices, over_space(): lax.ppermute(pieces[k], 'space', [(i, (i + k) % spaces) for i in range(sp...  16 us
    pallas_call x11, Pallas kernels, placed(): return call(*pinned)  7.68 us
    ppermute x9, waiting for transfers between devices, over_space(): lax.ppermute(pieces[k], 'space', [(i, (i + k) % spaces) for i in range(sp...  4.87 us
    ppermute x1, waiting for transfers between devices, body(): other_a = lax.ppermute(sum_a, 'tm', swap)  1.74 us
    ppermute x1, starting transfers between devices, body(): crossed_a = lax.ppermute(cross_a, 'tm', swap)  1.56 us
    ppermute x1, waiting for transfers between devices, body(): fixed = lax.ppermute(far_tiles[-1], 'col', swap)  1.34 us
    ppermute x1, waiting for transfers between devices, body(): got_a = lax.ppermute(send_a, 'col', swap)  1.28 us
    ppermute x1, waiting for transfers between devices, body(): got_tiles = lax.ppermute(send_tiles, 'col', swap)  1.11 us
  transfers between devices with their start and end apart: 20, of which 10 were waited for; matrix products, arithmetic and copies ran while one was open for 0% of the time, Pallas kernels for 9%

profile of v2, /device:TPU:0, one launch (start us, length us, event | category | flops | bytes accessed | tf_op | source)
XLA Modules:
  0.0 39.7 jit_solution(11816624841686671075)
XLA Ops:
  0.6 1.1 %shard_map.94 = (bf16[512,256]{1,0:T(8,128)(2,1)S(1)}, bf16[256,256]{1,0:T(8,128)(2,1)S(1)}, bf16[4,16,32]{2,1,0:T(8,128)(2,1)S(1)}, bf16[4,16,32]{2,1,0:T(8,128)(2,1)S(1)}) custom-call(s32[1]{0:T(128)} %bitcast.core_ref, bf16[2,512,256]{2,1,0:T(8,128)(2,1)} %bitcast.16, bf16[8,16,32]{2,1,0:T(8,128)(2,1)} %bitcast.20), custom_call_target="tpu_custom_call" | custom-call | bytes 524288 | tf_op jit(solution)/shard_map/pallas_call | solution.py:46
  1.8 0.5 %collective-permute-start = (bf16[256,256]{1,0:T(8,128)(2,1)S(1)}, bf16[256,256]{1,0:T(8,128)(2,1)S(1)}, u32[]{:S(2)}, u32[]{:S(2)}) collective-permute-start(bf16[256,256]{1,0:T(8,128)(2,1)S(1)} %get-tuple-element.44), channel_id=1, source_target_pairs={{0,1},{1,0},{2,3},{3,2},{4,5},{5,4},{6,7},{7,6},{8,9},{9,8},{10,11... | collective-permute-start | bytes 393224 | tf_op jit(solution)/shard_map/ppermute | solution.py:343
  2.3 0.1 collective-permute-start.1
  2.4 1.1 %collective-permute-done.1.got_ref = bf16[4,16,32]{2,1,0:T(8,128)(2,1)S(1)} collective-permute-done((bf16[4,16,32]{2,1,0:T(8,128)(2,1)S(1)}, bf16[4,16,32]{2,1,0:T(8,128)(2,1)S(1)}, u32[]{:S(2)}, u32[]{:S(2)}) %collective-permute-start.1) | collective-permute-done | bytes 4128 | tf_op jit(solution)/shard_map/ppermute | solution.py:342
  3.5 0.0 collective-permute-done.later_ref
  3.5 0.1 shard_map.95
  3.6 4.8 %collective-permute-start.4 = (bf16[272,256]{1,0:T(8,128)(2,1)S(1)}, bf16[272,256]{1,0:T(8,128)(2,1)S(1)}, u32[]{:S(2)}, u32[]{:S(2)}) collective-permute-start(bf16[272,256]{1,0:T(8,128)(2,1)S(1)} %get-tuple-element.49), channel_id=1, source_target_pairs={{0,12},{4,0},{8,4},{12,8},{1,13},{5,1},{9,5},{13,9},{2,14},{6,2},{... | collective-permute-start | bytes 417800 | tf_op jit(solution)/shard_map/ppermute | solution.py:323
  8.4 0.0 collective-permute-start.5
  8.4 0.0 collective-permute-start.2
  8.4 1.0 %collective-permute-start.3 = (bf16[16,128]{1,0:T(8,128)(2,1)S(1)}, bf16[16,128]{1,0:T(8,128)(2,1)S(1)}, u32[]{:S(2)}, u32[]{:S(2)}) collective-permute-start(bf16[16,128]{1,0:T(8,128)(2,1)S(1)} %get-tuple-element.48), channel_id=1, source_target_pairs={{0,8},{4,12},{8,0},{12,4},{1,9},{5,13},{9,1},{13,5},{2,10},{6,14},... | collective-permute-start | bytes 12296 | tf_op jit(solution)/shard_map/ppermute | solution.py:323
  9.4 2.1 %shard_map.93 = (bf16[6,256,256]{2,1,0:T(8,128)(2,1)S(1)}, f32[256,256]{1,0:T(8,128)S(1)}, bf16[9,256,256]{2,1,0:T(8,128)(2,1)S(1)}, bf16[32,256]{1,0:T(8,128)(2,1)S(1)}, bf16[16,256]{1,0:T(8,128)(2,1)S(1)}) custom-call(bf16[2,512,256]{2,1,0:T(8,128)(2,1)} %bitcast.17, bf16[9,256,256]{2,1,0:T(8,128)(2,1)} %bitcast.18, f32[1,256]{1,0:T(1,128)} %bitcast.23, ...), custom_call_target="tpu_custom_call" | custom-call | flops 201326592 | bytes 5242880 | tf_op jit(solution)/shard_map/pallas_call | solution.py:46
  11.5 2.3 %collective-permute-done.2.rest_1_ = bf16[16,128]{1,0:T(8,128)(2,1)S(1)} collective-permute-done((bf16[16,128]{1,0:T(8,128)(2,1)S(1)}, bf16[16,128]{1,0:T(8,128)(2,1)S(1)}, u32[]{:S(2)}, u32[]{:S(2)}) %collective-permute-start.2) | collective-permute-done | bytes 4128 | tf_op jit(solution)/shard_map/ppermute | solution.py:323
  13.8 0.0 collective-permute-done.3.rest_2_
  13.8 0.0 collective-permute-done.4.rest_3_
  13.8 0.0 collective-permute-start.6
  13.9 0.0 collective-permute-done.5.beside_ref
  13.9 1.3 %collective-permute-done.6.fixed_ref = bf16[272,256]{1,0:T(8,128)(2,1)S(1)} collective-permute-done((bf16[272,256]{1,0:T(8,128)(2,1)S(1)}, bf16[272,256]{1,0:T(8,128)(2,1)S(1)}, u32[]{:S(2)}, u32[]{:S(2)}) %collective-permute-start.6) | collective-permute-done | bytes 139296 | tf_op jit(solution)/shard_map/ppermute | solution.py:384
  15.2 2.0 %shard_map.96 = (bf16[256,256]{1,0:T(8,128)(2,1)S(1)}, f32[4,192,256]{2,1,0:T(8,128)S(1)}, bf16[4,192,256]{2,1,0:T(8,128)(2,1)}, f32[4,104,256]{2,1,0:T(8,128)S(1)}, bf16[4,104,256]{2,1,0:T(8,128)(2,1)S(1)}) custom-call(s32[1]{0:T(128)} %bitcast.core_ref, s32[1]{0:T(128)} %bitcast.1.space_ref, bf16[6,256,256]{2,1,0:T(8,128)(2,1)S(1)} %get-tuple-element.41.windows_ref, ...), custom_call_target="tpu_custom_call" | custom-call | flops 402653184 | bytes 5242880 | tf_op jit(solution)/shard_map/pallas_call | solution.py:46
  17.2 0.1 collective-permute-start.13
  17.3 0.4 collective-permute-start.8
  17.7 0.1 collective-permute-start.7
  17.8 1.3 %collective-permute-done.13.got_ref = bf16[4,192,256]{2,1,0:T(8,128)(2,1)S(1)} collective-permute-done((bf16[4,192,256]{2,1,0:T(8,128)(2,1)}, bf16[4,192,256]{2,1,0:T(8,128)(2,1)S(1)}, u32[]{:S(2)}, u32[]{:S(2)}) %collective-permute-start.13) | collective-permute-done | bytes 393248 | tf_op jit(solution)/shard_map/ppermute | solution.py:409
  19.1 0.1 shard_map.100
  19.2 1.6 %collective-permute-start.14 = (bf16[4,192,128]{2,1,0:T(8,128)(2,1)S(1)}, bf16[4,192,128]{2,1,0:T(8,128)(2,1)S(1)}, u32[]{:S(2)}, u32[]{:S(2)}) collective-permute-start(bf16[4,192,128]{2,1,0:T(8,128)(2,1)S(1)} %get-tuple-element.69), channel_id=1, source_target_pairs={{0,2},{2,0},{1,3},{3,1},{4,6},{6,4},{5,7},{7,5},{8,10},{10,8},{9,1... | collective-permute-start | bytes 589832 | tf_op jit(solution)/shard_map/ppermute | solution.py:419
  20.8 0.0 collective-permute-done.7.beside_ref
  20.8 0.0 collective-permute-done.8.got_ref
  20.8 0.1 shard_map.97
  20.8 1.2 %collective-permute-start.9 = (bf16[232,256]{1,0:T(8,128)(2,1)S(1)}, bf16[232,256]{1,0:T(8,128)(2,1)S(1)}, u32[]{:S(2)}, u32[]{:S(2)}) collective-permute-start(bf16[232,256]{1,0:T(8,128)(2,1)S(1)} %get-tuple-element.62), channel_id=1, source_target_pairs={{0,4},{4,8},{8,12},{12,0},{1,5},{5,9},{9,13},{13,1},{2,6},{6,10},{... | collective-permute-start | bytes 356360 | tf_op jit(solution)/shard_map/ppermute | solution.py:323
  22.0 2.3 %collective-permute-start.10 = (bf16[104,256]{1,0:T(8,128)(2,1)S(1)}, bf16[104,256]{1,0:T(8,128)(2,1)S(1)}, u32[]{:S(2)}, u32[]{:S(2)}) collective-permute-start(bf16[104,256]{1,0:T(8,128)(2,1)S(1)} %get-tuple-element.63), channel_id=1, source_target_pairs={{0,8},{4,12},{8,0},{12,4},{1,9},{5,13},{9,1},{13,5},{2,10},{6,14},... | collective-permute-start | bytes 159752 | tf_op jit(solution)/shard_map/ppermute | solution.py:323
  24.4 1.0 %collective-permute-start.11 = (bf16[104,256]{1,0:T(8,128)(2,1)S(1)}, bf16[104,256]{1,0:T(8,128)(2,1)S(1)}, u32[]{:S(2)}, u32[]{:S(2)}) collective-permute-start(bf16[104,256]{1,0:T(8,128)(2,1)S(1)} %get-tuple-element.64), channel_id=1, source_target_pairs={{0,12},{4,0},{8,4},{12,8},{1,13},{5,1},{9,5},{13,9},{2,14},{6,2},{... | collective-permute-start | bytes 159752 | tf_op jit(solution)/shard_map/ppermute | solution.py:323
  25.3 0.9 %collective-permute-done.14.got_ref = bf16[4,192,128]{2,1,0:T(8,128)(2,1)S(1)} collective-permute-done((bf16[4,192,128]{2,1,0:T(8,128)(2,1)S(1)}, bf16[4,192,128]{2,1,0:T(8,128)(2,1)S(1)}, u32[]{:S(2)}, u32[]{:S(2)}) %collective-permute-start.14) | collective-permute-done | bytes 196640 | tf_op jit(solution)/shard_map/ppermute | solution.py:419
  26.3 1.2 %collective-permute-start.15 = (bf16[192,128]{1,0:T(8,128)(2,1)S(1)}, bf16[192,128]{1,0:T(8,128)(2,1)S(1)}, u32[]{:S(2)}, u32[]{:S(2)}) collective-permute-start(bf16[192,128]{1,0:T(8,128)(2,1)S(1)} %get-tuple-element.71), channel_id=1, source_target_pairs={{0,4},{4,8},{8,12},{12,0},{1,5},{5,9},{9,13},{13,1},{2,6},{6,10},{... | collective-permute-start | bytes 147464 | tf_op jit(solution)/shard_map/ppermute | solution.py:323
  27.5 2.3 %collective-permute-start.16 = (bf16[192,128]{1,0:T(8,128)(2,1)S(1)}, bf16[192,128]{1,0:T(8,128)(2,1)S(1)}, u32[]{:S(2)}, u32[]{:S(2)}) collective-permute-start(bf16[192,128]{1,0:T(8,128)(2,1)S(1)} %get-tuple-element.72), channel_id=1, source_target_pairs={{0,8},{4,12},{8,0},{12,4},{1,9},{5,13},{9,1},{13,5},{2,10},{6,14},... | collective-permute-start | bytes 147464 | tf_op jit(solution)/shard_map/ppermute | solution.py:323
  29.8 0.3 collective-permute-done.10.refs_1_
  30.1 2.1 %collective-permute-start.17 = (bf16[192,128]{1,0:T(8,128)(2,1)S(1)}, bf16[192,128]{1,0:T(8,128)(2,1)S(1)}, u32[]{:S(2)}, u32[]{:S(2)}) collective-permute-start(bf16[192,128]{1,0:T(8,128)(2,1)S(1)} %get-tuple-element.73), channel_id=1, source_target_pairs={{0,12},{4,0},{8,4},{12,8},{1,13},{5,1},{9,5},{13,9},{2,14},{6,2},{... | collective-permute-start | bytes 147464 | tf_op jit(solution)/shard_map/ppermute | solution.py:323
  32.2 0.0 collective-permute-done.11.refs_2_
  32.2 0.0 collective-permute-done.9.refs_0_
  32.2 0.1 collective-permute-start.12
  32.3 0.2 collective-permute-start.19
  32.5 0.3 collective-permute-done.15.refs_0_
  32.8 1.6 %collective-permute-done.16.refs_1_ = bf16[192,128]{1,0:T(8,128)(2,1)S(1)} collective-permute-done((bf16[192,128]{1,0:T(8,128)(2,1)S(1)}, bf16[192,128]{1,0:T(8,128)(2,1)S(1)}, u32[]{:S(2)}, u32[]{:S(2)}) %collective-permute-start.16) | collective-permute-done | bytes 49184 | tf_op jit(solution)/shard_map/ppermute | solution.py:323
  34.4 0.4 collective-permute-done.17.refs_2_
  34.8 1.0 %collective-permute-start.18 = (bf16[192,128]{1,0:T(8,128)(2,1)S(1)}, bf16[192,128]{1,0:T(8,128)(2,1)S(1)}, u32[]{:S(2)}, u32[]{:S(2)}) collective-permute-start(bf16[192,128]{1,0:T(8,128)(2,1)S(1)} %shard_map.102.a_ref), channel_id=1, source_target_pairs={{0,2},{2,0},{1,3},{3,1},{4,6},{6,4},{5,7},{7,5},{8,10},{10,8},{9,1... | collective-permute-start | bytes 147464 | tf_op jit(solution)/shard_map/ppermute | solution.py:456
  35.8 0.0 collective-permute-done.12.low_ref
  35.8 1.4 %shard_map.99 = bf16[2,512,256]{2,1,0:T(8,128)(2,1)} custom-call(s32[1]{0:T(128)} %bitcast.core_ref, s32[1]{0:T(128)} %bitcast.1.space_ref, bf16[256,256]{1,0:T(8,128)(2,1)S(1)} %get-tuple-element.58.mine_ref.pre_grad_ref, bf16[256,256]{1,0:T(8,128)(2,1)S(1)} %collective-permute-done.7.beside_ref, bf16[128,256]{1,0:T(8,128)(2,1)S(1)} %collective-permute-done.12.low_ref, ...), custom_call_target="tpu_custom_call" | custom-call | flops 301989888 | bytes 4194304 | tf_op jit(solution)/shard_map/pallas_call | solution.py:46
  37.2 0.0 collective-permute-done.19.b_far_ref
  37.2 1.7 %collective-permute-done.18.a_far_ref = bf16[192,128]{1,0:T(8,128)(2,1)S(1)} collective-permute-done((bf16[192,128]{1,0:T(8,128)(2,1)S(1)}, bf16[192,128]{1,0:T(8,128)(2,1)S(1)}, u32[]{:S(2)}, u32[]{:S(2)}) %collective-permute-start.18) | collective-permute-done | bytes 49184 | tf_op jit(solution)/shard_map/ppermute | solution.py:456
  39.0 0.8 %shard_map.103 = (f32[9,32,256]{2,1,0:T(8,128)}, f32[32,32]{1,0:T(8,128)}, f32[1,32]{1,0:T(1,128)}) custom-call(s32[1]{0:T(128)} %bitcast.11.time_ref, bf16[192,128]{1,0:T(8,128)(2,1)S(1)} %shard_map.102.a_ref, bf16[192,128]{1,0:T(8,128)(2,1)S(1)} %collective-permute-done.18.a_far_ref, bf16[104,256]{1,0:T(8,128)(2,1)S(1)} %get-tuple-element.74.b_ref, ...), custom_call_target="tpu_custom_call" | custom-call | flops 51200 | bytes 1048576 | tf_op jit(solution)/shard_map/pallas_call | solution.py:46
  (3 shorter events, 0.1 us)
Async XLA Ops:
  1.8 1.7 %collective-permute-start = (bf16[256,256]{1,0:T(8,128)(2,1)S(1)}, bf16[256,256]{1,0:T(8,128)(2,1)S(1)}, u32[]{:S(2)}, u32[]{:S(2)}) collective-permute-start(bf16[256,256]{1,0:T(8,128)(2,1)S(1)} %get-tuple-element.44), channel_id=1, source_target_pairs={{0,1},{1,0},{2,3},{3,2},{4,5},{5,4},{6,7},{7,6},{8,9},{9,8},{10,11... | collective-permute-start | bytes 393224 | tf_op jit(solution)/shard_map/ppermute | solution.py:343
  2.3 1.2 %collective-permute-start.1 = (bf16[4,16,32]{2,1,0:T(8,128)(2,1)S(1)}, bf16[4,16,32]{2,1,0:T(8,128)(2,1)S(1)}, u32[]{:S(2)}, u32[]{:S(2)}) collective-permute-start(bf16[4,16,32]{2,1,0:T(8,128)(2,1)S(1)} %get-tuple-element.46), channel_id=1, source_target_pairs={{0,1},{1,0},{2,3},{3,2},{4,5},{5,4},{6,7},{7,6},{8,9},{9,8},{10,11... | collective-permute-start | bytes 12296 | tf_op jit(solution)/shard_map/ppermute | solution.py:342
  3.6 10.3 %collective-permute-start.4 = (bf16[272,256]{1,0:T(8,128)(2,1)S(1)}, bf16[272,256]{1,0:T(8,128)(2,1)S(1)}, u32[]{:S(2)}, u32[]{:S(2)}) collective-permute-start(bf16[272,256]{1,0:T(8,128)(2,1)S(1)} %get-tuple-element.49), channel_id=1, source_target_pairs={{0,12},{4,0},{8,4},{12,8},{1,13},{5,1},{9,5},{13,9},{2,14},{6,2},{... | collective-permute-start | bytes 417800 | tf_op jit(solution)/shard_map/ppermute | solution.py:323
  8.4 5.5 %collective-permute-start.5 = (bf16[512,256]{1,0:T(8,128)(2,1)S(1)}, bf16[512,256]{1,0:T(8,128)(2,1)S(1)}, u32[]{:S(2)}, u32[]{:S(2)}) collective-permute-start(bf16[512,256]{1,0:T(8,128)(2,1)S(1)} %get-tuple-element.43.row_ref), channel_id=1, source_target_pairs={{0,1},{1,0},{2,3},{3,2},{4,5},{5,4},{6,7},{7,6},{8,9},{9,8},{10,11... | collective-permute-start | bytes 786440 | tf_op jit(solution)/shard_map/ppermute | solution.py:356
  8.4 5.4 %collective-permute-start.2 = (bf16[16,128]{1,0:T(8,128)(2,1)S(1)}, bf16[16,128]{1,0:T(8,128)(2,1)S(1)}, u32[]{:S(2)}, u32[]{:S(2)}) collective-permute-start(bf16[16,128]{1,0:T(8,128)(2,1)S(1)} %get-tuple-element.47), channel_id=1, source_target_pairs={{0,4},{4,8},{8,12},{12,0},{1,5},{5,9},{9,13},{13,1},{2,6},{6,10},{... | collective-permute-start | bytes 12296 | tf_op jit(solution)/shard_map/ppermute | solution.py:323
  8.4 5.4 %collective-permute-start.3 = (bf16[16,128]{1,0:T(8,128)(2,1)S(1)}, bf16[16,128]{1,0:T(8,128)(2,1)S(1)}, u32[]{:S(2)}, u32[]{:S(2)}) collective-permute-start(bf16[16,128]{1,0:T(8,128)(2,1)S(1)} %get-tuple-element.48), channel_id=1, source_target_pairs={{0,8},{4,12},{8,0},{12,4},{1,9},{5,13},{9,1},{13,5},{2,10},{6,14},... | collective-permute-start | bytes 12296 | tf_op jit(solution)/shard_map/ppermute | solution.py:323
  13.8 1.4 %collective-permute-start.6 = (bf16[272,256]{1,0:T(8,128)(2,1)S(1)}, bf16[272,256]{1,0:T(8,128)(2,1)S(1)}, u32[]{:S(2)}, u32[]{:S(2)}) collective-permute-start(bf16[272,256]{1,0:T(8,128)(2,1)S(1)} %collective-permute-done.4.rest_3_), channel_id=1, source_target_pairs={{0,1},{1,0},{2,3},{3,2},{4,5},{5,4},{6,7},{7,6},{8,9},{9,8},{10,11... | collective-permute-start | bytes 417800 | tf_op jit(solution)/shard_map/ppermute | solution.py:384
  17.2 1.9 %collective-permute-start.13 = (bf16[4,192,256]{2,1,0:T(8,128)(2,1)}, bf16[4,192,256]{2,1,0:T(8,128)(2,1)S(1)}, u32[]{:S(2)}, u32[]{:S(2)}) collective-permute-start(bf16[4,192,256]{2,1,0:T(8,128)(2,1)} %get-tuple-element.67), channel_id=1, source_target_pairs={{0,1},{1,0},{2,3},{3,2},{4,5},{5,4},{6,7},{7,6},{8,9},{9,8},{10,11... | collective-permute-start | bytes 1179656 | tf_op jit(solution)/shard_map/ppermute | solution.py:409
  17.3 3.5 %collective-permute-start.8 = (bf16[4,104,256]{2,1,0:T(8,128)(2,1)S(1)}, bf16[4,104,256]{2,1,0:T(8,128)(2,1)S(1)}, u32[]{:S(2)}, u32[]{:S(2)}) collective-permute-start(bf16[4,104,256]{2,1,0:T(8,128)(2,1)S(1)} %get-tuple-element.60), channel_id=1, source_target_pairs={{0,1},{1,0},{2,3},{3,2},{4,5},{5,4},{6,7},{7,6},{8,9},{9,8},{10,11... | collective-permute-start | bytes 638984 | tf_op jit(solution)/shard_map/ppermute | solution.py:410
  17.7 3.1 %collective-permute-start.7 = (bf16[256,256]{1,0:T(8,128)(2,1)S(1)}, bf16[256,256]{1,0:T(8,128)(2,1)S(1)}, u32[]{:S(2)}, u32[]{:S(2)}) collective-permute-start(bf16[256,256]{1,0:T(8,128)(2,1)S(1)} %get-tuple-element.58.mine_ref.pre_grad_ref), channel_id=1, source_target_pairs={{0,1},{1,0},{2,3},{3,2},{4,5},{5,4},{6,7},{7,6},{8,9},{9,8},{10,11... | collective-permute-start | bytes 393224 | tf_op jit(solution)/shard_map/ppermute | solution.py:408
  19.2 7.0 %collective-permute-start.14 = (bf16[4,192,128]{2,1,0:T(8,128)(2,1)S(1)}, bf16[4,192,128]{2,1,0:T(8,128)(2,1)S(1)}, u32[]{:S(2)}, u32[]{:S(2)}) collective-permute-start(bf16[4,192,128]{2,1,0:T(8,128)(2,1)S(1)} %get-tuple-element.69), channel_id=1, source_target_pairs={{0,2},{2,0},{1,3},{3,1},{4,6},{6,4},{5,7},{7,5},{8,10},{10,8},{9,1... | collective-permute-start | bytes 589832 | tf_op jit(solution)/shard_map/ppermute | solution.py:419
  20.8 11.3 %collective-permute-start.9 = (bf16[232,256]{1,0:T(8,128)(2,1)S(1)}, bf16[232,256]{1,0:T(8,128)(2,1)S(1)}, u32[]{:S(2)}, u32[]{:S(2)}) collective-permute-start(bf16[232,256]{1,0:T(8,128)(2,1)S(1)} %get-tuple-element.62), channel_id=1, source_target_pairs={{0,4},{4,8},{8,12},{12,0},{1,5},{5,9},{9,13},{13,1},{2,6},{6,10},{... | collective-permute-start | bytes 356360 | tf_op jit(solution)/shard_map/ppermute | solution.py:323
  22.0 8.1 %collective-permute-start.10 = (bf16[104,256]{1,0:T(8,128)(2,1)S(1)}, bf16[104,256]{1,0:T(8,128)(2,1)S(1)}, u32[]{:S(2)}, u32[]{:S(2)}) collective-permute-start(bf16[104,256]{1,0:T(8,128)(2,1)S(1)} %get-tuple-element.63), channel_id=1, source_target_pairs={{0,8},{4,12},{8,0},{12,4},{1,9},{5,13},{9,1},{13,5},{2,10},{6,14},... | collective-permute-start | bytes 159752 | tf_op jit(solution)/shard_map/ppermute | solution.py:323
  24.4 7.8 %collective-permute-start.11 = (bf16[104,256]{1,0:T(8,128)(2,1)S(1)}, bf16[104,256]{1,0:T(8,128)(2,1)S(1)}, u32[]{:S(2)}, u32[]{:S(2)}) collective-permute-start(bf16[104,256]{1,0:T(8,128)(2,1)S(1)} %get-tuple-element.64), channel_id=1, source_target_pairs={{0,12},{4,0},{8,4},{12,8},{1,13},{5,1},{9,5},{13,9},{2,14},{6,2},{... | collective-permute-start | bytes 159752 | tf_op jit(solution)/shard_map/ppermute | solution.py:323
  26.3 6.5 %collective-permute-start.15 = (bf16[192,128]{1,0:T(8,128)(2,1)S(1)}, bf16[192,128]{1,0:T(8,128)(2,1)S(1)}, u32[]{:S(2)}, u32[]{:S(2)}) collective-permute-start(bf16[192,128]{1,0:T(8,128)(2,1)S(1)} %get-tuple-element.71), channel_id=1, source_target_pairs={{0,4},{4,8},{8,12},{12,0},{1,5},{5,9},{9,13},{13,1},{2,6},{6,10},{... | collective-permute-start | bytes 147464 | tf_op jit(solution)/shard_map/ppermute | solution.py:323
  27.5 6.9 %collective-permute-start.16 = (bf16[192,128]{1,0:T(8,128)(2,1)S(1)}, bf16[192,128]{1,0:T(8,128)(2,1)S(1)}, u32[]{:S(2)}, u32[]{:S(2)}) collective-permute-start(bf16[192,128]{1,0:T(8,128)(2,1)S(1)} %get-tuple-element.72), channel_id=1, source_target_pairs={{0,8},{4,12},{8,0},{12,4},{1,9},{5,13},{9,1},{13,5},{2,10},{6,14},... | collective-permute-start | bytes 147464 | tf_op jit(solution)/shard_map/ppermute | solution.py:323
  30.1 4.7 %collective-permute-start.17 = (bf16[192,128]{1,0:T(8,128)(2,1)S(1)}, bf16[192,128]{1,0:T(8,128)(2,1)S(1)}, u32[]{:S(2)}, u32[]{:S(2)}) collective-permute-start(bf16[192,128]{1,0:T(8,128)(2,1)S(1)} %get-tuple-element.73), channel_id=1, source_target_pairs={{0,12},{4,0},{8,4},{12,8},{1,13},{5,1},{9,5},{13,9},{2,14},{6,2},{... | collective-permute-start | bytes 147464 | tf_op jit(solution)/shard_map/ppermute | solution.py:323
  32.2 3.6 %collective-permute-start.12 = (bf16[128,256]{1,0:T(8,128)(2,1)S(1)}, bf16[128,256]{1,0:T(8,128)(2,1)S(1)}, u32[]{:S(2)}, u32[]{:S(2)}) collective-permute-start(bf16[128,256]{1,0:T(8,128)(2,1)S(1)} %get-tuple-element.65.high_ref), channel_id=1, source_target_pairs={{0,1},{1,0},{2,3},{3,2},{4,5},{5,4},{6,7},{7,6},{8,9},{9,8},{10,11... | collective-permute-start | bytes 196616 | tf_op jit(solution)/shard_map/ppermute | solution.py:452
  32.3 4.9 %collective-permute-start.19 = (bf16[104,256]{1,0:T(8,128)(2,1)S(1)}, bf16[104,256]{1,0:T(8,128)(2,1)S(1)}, u32[]{:S(2)}, u32[]{:S(2)}) collective-permute-start(bf16[104,256]{1,0:T(8,128)(2,1)S(1)} %get-tuple-element.74.b_ref), channel_id=1, source_target_pairs={{0,2},{2,0},{1,3},{3,1},{4,6},{6,4},{5,7},{7,5},{8,10},{10,8},{9,1... | collective-permute-start | bytes 159752 | tf_op jit(solution)/shard_map/ppermute | solution.py:451
  34.8 4.2 %collective-permute-start.18 = (bf16[192,128]{1,0:T(8,128)(2,1)S(1)}, bf16[192,128]{1,0:T(8,128)(2,1)S(1)}, u32[]{:S(2)}, u32[]{:S(2)}) collective-permute-start(bf16[192,128]{1,0:T(8,128)(2,1)S(1)} %shard_map.102.a_ref), channel_id=1, source_target_pairs={{0,2},{2,0},{1,3},{3,1},{4,6},{6,4},{5,7},{7,5},{8,10},{10,8},{9,1... | collective-permute-start | bytes 147464 | tf_op jit(solution)/shard_map/ppermute | solution.py:456

commit v3 on v2

--- a/solution.py
+++ b/solution.py
@@ -21,7 +21,7 @@
 
 
 def params():
-    return pltpu.CompilerParams(vmem_limit_bytes=24 << 20)
+    return pltpu.CompilerParams(vmem_limit_bytes=12 << 20)
 
 
 SPACES = {"s": pltpu.SMEM, "v": pltpu.VMEM, "h": pltpu.HBM}
@@ -48,39 +48,40 @@
     return placed
 
 
-def start_kernel(core_ref, act_ref, tiles_ref, row_ref, later_ref, own_ref, send_ref, sems):
-    core = core_ref[0]
-    half = later_ref.shape[0]
+def start_kernel(act_ref, tiles_in, row_ref, tiles_ref, sems):
     copies = [
-        pltpu.make_async_copy(act_ref.at[0, pl.ds(half, half)], later_ref, sems.at[0]),
+        pltpu.make_async_copy(tiles_in, tiles_ref, sems.at[0]),
         pltpu.make_async_copy(act_ref.at[0], row_ref, sems.at[1]),
     ]
-    for j in range(own_ref.shape[0]):
-        mine = tiles_ref.at[2 * j + core]
-        theirs = tiles_ref.at[2 * j + 1 - core]
-        copies.append(pltpu.make_async_copy(mine, own_ref.at[j], sems.at[2 + 2 * j]))
-        copies.append(pltpu.make_async_copy(theirs, send_ref.at[j], sems.at[3 + 2 * j]))
     for copy in copies:
         copy.start()
     for copy in copies:
         copy.wait()
 
 
-def tiles_kernel(core_ref, space_ref, row_ref, later_ref, own_ref, got_ref, *outs):
-    spaces = own_ref.shape[0]
+def tiles_kernel(core_ref, space_ref, row_ref, own_ref, got_ref, here_ref, far_ref, down_ref):
+    spaces = own_ref.shape[0] // 2
     height, width = own_ref.shape[1:]
-    half = later_ref.shape[0]
-    first = core_ref[0] == 0
-    down = outs[-1]
-    down[:half, :] = jnp.where(first, row_ref[:half, :], later_ref[...])
-    for k, out in enumerate(outs):
-        at = lax.rem(space_ref[0] + k, spaces)
+    cols = row_ref.shape[0]
+    core, chip = core_ref[0], space_ref[0]
+    first = core == 0
+
+    def side_by_side(at):
         mine, other = own_ref[at], got_ref[at]
-        top = half if k == spaces - 1 else 0
-        lanes = out.shape[1]
-        pieces = [jnp.where(first, mine, other), jnp.where(first, other, mine)]
-        pieces.append(jnp.zeros((height, lanes - 2 * width), bf16))
-        out[top:, :] = jnp.concatenate(pieces, 1)
+        return [jnp.where(first, mine, other), jnp.where(first, other, mine)]
+
+    def put(ref, top, pieces):
+        used = width * len(pieces)
+        if used < ref.shape[1]:
+            pieces = [*pieces, jnp.zeros((height, ref.shape[1] - used), bf16)]
+        ref[top:, :] = jnp.concatenate(pieces, 1)
+
+    put(here_ref, 0, side_by_side(2 * chip + core))
+    there = 2 * lax.rem(chip + 1 + core, spaces)
+    put(far_ref, 0, side_by_side(there) + side_by_side(there + 1))
+    down_ref[:cols, :] = row_ref[...]
+    there = 2 * lax.rem(chip + spaces - 1, spaces)
+    put(down_ref, cols, side_by_side(there) + side_by_side(there + 1))
 
 
 def split_columns(row, source, stage):
@@ -101,19 +102,21 @@
 
 
 def early_kernel(
-    act_ref, w_in, bias_in, head_in, noise_in,
-    windows_ref, pre_act_ref, w_ref, head_ref, noise_ref, act, bias, stage, sems,
+    act_ref, w_in, bias_in, head_in, noise_in, here_ref,
+    windows_ref, pre_act_ref, w_ref, act, bias, head, noise, stage, sems,
 ):
     pairs = [
         (act_ref.at[0], act.at[0]), (w_in.at[:3], w_ref.at[:3]),
         (act_ref.at[1], act.at[1]), (w_in.at[3:6], w_ref.at[3:6]),
-        (bias_in, bias), (w_in.at[6:], w_ref.at[6:]), (head_in, head_ref), (noise_in, noise_ref),
+        (bias_in, bias), (w_in.at[6:], w_ref.at[6:]), (head_in, head), (noise_in, noise),
     ]
     copies = [pltpu.make_async_copy(a, b, sems.at[i]) for i, (a, b) in enumerate(pairs)]
     for copy in copies:
         copy.start()
     copies[4].wait()
-    pre_act = jnp.broadcast_to(bias[...], pre_act_ref.shape)
+    cols = noise.shape[1]
+    width = head.shape[1]
+    pre_act = jnp.broadcast_to(bias[...], (cols, width))
     for row in range(2):
         copies[2 * row].wait()
         windows = split_columns(row, act[row], stage)
@@ -121,64 +124,93 @@
         for tap in range(3):
             windows_ref[3 * row + tap] = windows[tap]
             pre_act = pre_act + dot(windows[tap], w_ref[3 * row + tap], 1, 0)
-    pre_act_ref[...] = pre_act
+    pre_act_ref[:cols, :] = pre_act
     for copy in copies[5:]:
         copy.wait()
-
-
-def terms_kernel(
-    core_ref, space_ref, windows_ref, early_ref, w_ref, head_ref, noise_ref,
-    beside_ref, fixed_ref, *rest,
+    at = cols
+    for ref in (head, noise, here_ref):
+        pre_act_ref[at : at + ref.shape[0], : ref.shape[1]] = ref[...].astype(f32)
+        at += ref.shape[0]
+
+
+def conv_kernel(
+    chips, core_ref, space_ref, early_ref, w_ref, far_ref, above_ref,
+    pre_act_ref, windows_ref, hidden_ref, tiles_ref, stage,
 ):
-    spaces = len(rest) - 7
-    tiles = rest[:spaces]
-    pre_grad_ref, keep_a, send_a, keep_b, send_b, tiles_at, stage = rest[spaces:]
+    cols = hidden_ref.shape[0]
+    height = far_ref.shape[0]
+    lanes = far_ref.shape[1]
+    last = (core_ref[0] == 1) & (space_ref[0] == chips - 1)
+    row = above_ref[: 2 * cols, :]
+    windows = split_columns(0, jnp.where(last, jnp.zeros_like(row), row), stage)
+    tiles_ref[:height, :] = far_ref[...]
+    tiles_ref[height:, :] = above_ref[2 * cols :, :lanes]
+    pre_act = early_ref[:cols, :]
+    for tap in range(3):
+        windows_ref[tap] = windows[tap]
+        pre_act = pre_act + dot(windows[tap], w_ref[6 + tap], 1, 0)
+    pre_act_ref[...] = pre_act
+    hidden_ref[...] = jax.nn.silu(pre_act).astype(bf16)
+
+
+def grad_kernel(
+    core_ref, space_ref, early_ref, pre_act_ref, hidden_ref, tiles_ref, other_tiles_ref,
+    pre_grad_ref, moment_grad_ref, tiles_at,
+):
     cols, width = pre_grad_ref.shape
-    latent = noise_ref.shape[0]
-    share = width // (2 * spaces)
+    spaces, latent, lanes = tiles_at.shape
+    head = early_ref[cols : cols + 2 * latent, :].astype(bf16)
+    at = cols + 2 * latent
+    sample = early_ref[at : at + latent, :cols]
+    chip = space_ref[0]
     first = core_ref[0] == 0
-    height, lanes = tiles_at.shape[1:]
-    for k in range(spaces):
-        top = tiles[k].shape[0] - height
-        tiles_at[lax.rem(space_ref[0] + spaces - k, spaces)] = tiles[k][top:, :lanes]
-    half = tiles[-1].shape[0] - height
-    above = jnp.concatenate([fixed_ref[:half, :], tiles[-1][:half, :]], 0)
-    above = jnp.where(space_ref[0] == spaces - 1, jnp.zeros_like(above), above)
-    next_row = jnp.where(first, beside_ref[...], above)
-    windows = [windows_ref[i] for i in range(6)] + split_columns(0, next_row, stage)
-    pre_act = early_ref[...]
-    for index in range(6, 9):
-        pre_act = pre_act + dot(windows[index], w_ref[index], 1, 0)
+    tiles_at[chip] = early_ref[at + latent : at + 2 * latent, :lanes].astype(bf16)
+    mine, other = tiles_ref[...], other_tiles_ref[...]
+    for there, both in (
+        (spaces - 1, jnp.where(first, mine[:latent], other[:latent])),
+        (spaces - 2, jnp.where(first, other[:latent], mine[:latent])),
+        (1, jnp.where(first, other[latent:], mine[latent:])),
+    ):
+        band = jnp.where(first, both[:, :lanes], both[:, lanes:])
+        tiles_at[lax.rem(chip + there, spaces)] = band
+    pre_act = pre_act_ref[...]
     gating = jax.nn.sigmoid(pre_act)
-    hidden = (pre_act * gating).astype(bf16)
-    moments = dot(head_ref[...], hidden, 1, 1)
+    moments = dot(head, hidden_ref[...], 1, 1)
     mean_part = moments[:latent]
     logvar = moments[latent:]
-    upstream = jnp.concatenate(
-        [tiles_at[i][:, : cols // spaces].astype(f32) for i in range(spaces)], 1
-    )
-    sample = noise_ref[...].astype(f32)
+    upstream = jnp.concatenate([tiles_at[i].astype(f32) for i in range(spaces)], 1)
     spread = jnp.exp(0.5 * logvar)
     mean_grad = upstream + kl_weight * mean_part
     logvar_grad = 0.5 * upstream * sample * spread + 0.5 * kl_weight * (spread * spread - 1.0)
     moment_grad = jnp.concatenate([mean_grad, logvar_grad], 0).astype(bf16)
-    hidden_grad = dot(moment_grad, head_ref[...], 0, 0)
+    hidden_grad = dot(moment_grad, head, 0, 0)
     pre_grad = (hidden_grad * gating * (1.0 + pre_act * (1.0 - gating))).astype(bf16)
     pre_grad_ref[...] = pre_grad
-
-    def put(keep_ref, send_ref, s, at, even, odd):
-        here = slice(at, at + even.shape[0])
-        keep_ref[s, here, :] = jnp.where(first, even, odd)
-        send_ref[s, here, :] = jnp.where(first, odd, even).astype(bf16)
-
-    for index in range(9):
-        term = dot(windows[index], pre_grad, 0, 0)
-        refs = (keep_a, send_a) if index < HALVED else (keep_b, send_b)
-        at = share * (index if index < HALVED else index - HALVED)
-        for s in range(spaces):
-            row = 2 * share * s
-            put(*refs, s, at, term[row : row + share], term[row + share : row + 2 * share])
-    head_term = dot(hidden, moment_grad, 0, 1)
+    moment_grad_ref[...] = moment_grad
+
+
+def put_shares(first, keep_ref, send_ref, at, term):
+    spaces = keep_ref.shape[0]
+    share = term.shape[0] // (2 * spaces)
+    for s in range(spaces):
+        row = 2 * share * s
+        even, odd = term[row : row + share], term[row + share : row + 2 * share]
+        keep_ref[s, at : at + share, :] = jnp.where(first, even, odd)
+        send_ref[s, at : at + share, :] = jnp.where(first, odd, even).astype(bf16)
+
+
+def frame_terms_kernel(
+    core_ref, windows_ref, pre_grad_ref, hidden_ref, moment_grad_ref, keep_ref, send_ref
+):
+    cols, width = pre_grad_ref.shape
+    spaces = keep_ref.shape[0]
+    share = width // (2 * spaces)
+    first = core_ref[0] == 0
+    pre_grad = pre_grad_ref[...]
+    taps = windows_ref.shape[0]
+    for tap in range(taps):
+        put_shares(first, keep_ref, send_ref, tap * share, dot(windows_ref[tap], pre_grad, 0, 0))
+    head_term = dot(hidden_ref[...], moment_grad_ref[...], 0, 1)
     bias_term = dot(jnp.ones((TAIL, cols), bf16), pre_grad, 1, 0)
 
     def tail(row):
@@ -188,9 +220,22 @@
         pieces.append(jnp.zeros((TAIL, width - used), f32))
         return jnp.concatenate(pieces, 1)
 
+    tails = []
+    for s in range(2 * spaces):
+        tails.append(tail(share * s))
+    put_shares(first, keep_ref, send_ref, taps * share, jnp.concatenate(tails, 0))
+    rows, part = keep_ref.shape[1], cols // spaces
     for s in range(spaces):
-        row = 2 * share * s
-        put(keep_b, send_b, s, (9 - HALVED) * share, tail(row), tail(row + share))
+        send_ref[s, rows:, :] = pre_grad[part * s : part * (s + 1)]
+
+
+def early_terms_kernel(core_ref, windows_ref, pre_grad_ref, keep_ref, send_ref):
+    first = core_ref[0] == 0
+    pre_grad = pre_grad_ref[...]
+    share = pre_grad.shape[1] // (2 * keep_ref.shape[0])
+    for index in range(HALVED):
+        term = dot(windows_ref[index], pre_grad, 0, 0)
+        put_shares(first, keep_ref, send_ref, index * share, term)
 
 
 def halve_kernel(time_ref, keep_ref, got_ref, own_ref, send_ref):
@@ -208,15 +253,18 @@
         out[...] = (keep_ref[at] + got_ref[at].astype(f32)).astype(out.dtype)
 
 
-def pair_rim_kernel(core_ref, space_ref, keep_ref, got_ref, mine_ref, beside_ref, *outs):
+def pair_rim_kernel(core_ref, space_ref, keep_ref, got_ref, mine_ref, *outs):
+    *outs, beside_ref = outs
     spaces = len(outs)
     rows = keep_ref.shape[1]
     for k, out in enumerate(outs):
         at = lax.rem(space_ref[0] + k, spaces)
-        out[:rows, :] = (keep_ref[at] + got_ref[at].astype(f32)).astype(out.dtype)
+        out[:rows, :] = (keep_ref[at] + got_ref[at, :rows, :].astype(f32)).astype(out.dtype)
     half = mine_ref.shape[0] // 2
     first = core_ref[0] == 0
-    outs[1][rows:, :] = jnp.where(first, beside_ref[half:, :], mine_ref[:half, :])
+    beside = jnp.concatenate([got_ref[s, rows:, :] for s in range(spaces)], 0)
+    beside_ref[...] = beside
+    outs[1][rows:, :] = jnp.where(first, beside[half:], mine_ref[:half, :])
 
 
 def line_kernel(own_ref, *refs):
@@ -308,105 +356,121 @@
     share = channels // peers
     taps = conv_weight.reshape(9, channels, channels)
     tiles = jnp.transpose(latent_grad[0], (0, 2, 1))
-    if share % TAIL or not 2 <= spaces <= 4 or times != 2:
+    if share % TAIL or spaces != 4 or times != 2:
         return wide_body(activations, taps, conv_bias, head_weight, tiles, noise_sample)
     core_at = lax.axis_index("col").astype(jnp.int32).reshape(1)
     space_at = lax.axis_index("space").astype(jnp.int32).reshape(1)
     time_at = lax.axis_index("tm").astype(jnp.int32).reshape(1)
     swap = [(0, 1), (1, 0)]
-    hops = list(range(spaces - 1, 0, -1))
-    down = spaces - 1
     array = jax.ShapeDtypeStruct
 
     def over_space(pieces):
-        sent = {
-            k: lax.ppermute(pieces[k], "space", [(i, (i + k) % spaces) for i in range(spaces)])
-            for k in hops
-        }
-        return [sent[k] for k in range(1, spaces)]
+        return [
+            lax.ppermute(pieces[k], "space", [(i, (i + k) % spaces) for i in range(spaces)])
+            for k in range(1, spaces)
+        ]
 
     tile = tiles.shape[1:]
-    row, later, own_tiles, send_tiles = full_call(
+    got_tiles = lax.ppermute(tiles, "col", swap)
+    row, own_tiles = full_call(
         start_kernel,
-        (
-            array((double_cols, channels), bf16),
-            array((cols, channels), bf16),
-            array((spaces, *tile), bf16),
-            array((spaces, *tile), bf16),
-        ),
-        [pltpu.SemaphoreType.DMA((2 + 2 * spaces,))],
+        (array((double_cols, channels), bf16), array(tiles.shape, bf16)),
+        [pltpu.SemaphoreType.DMA((2,))],
         0,
         1 << 19,
-        "shh",
-    )(core_at, activations[0], tiles)
-    got_tiles = lax.ppermute(send_tiles, "col", swap)
-    got_later = lax.ppermute(later, "col", swap)
-    tile_sets = full_call(
+        "hh",
+    )(activations[0], tiles)
+    here, far, lower = full_call(
         tiles_kernel,
-        tuple(
-            array((cols + tile[0], channels) if k == down else (tile[0], LANES), bf16)
-            for k in range(spaces)
+        (
+            array((tile[0], LANES), bf16),
+            array((tile[0], LANES), bf16),
+            array((double_cols + tile[0], channels), bf16),
         ),
         [],
         0,
-        1 << 15,
-        "ssvvvv",
-    )(core_at, space_at, row, got_later, own_tiles, got_tiles)
-    far_tiles = over_space(tile_sets)
-    beside = lax.ppermute(row, "col", swap)
+        1 << 18,
+        "ssvvv",
+    )(core_at, space_at, row, own_tiles, got_tiles)
+    above = lax.ppermute(lower, line, [(i, (i - 1) % peers) for i in range(peers)])
+    hops = [(2 * i + c, 2 * ((i + 1 + c) % spaces) + c) for i in range(spaces) for c in range(2)]
+    far = lax.ppermute(far, line, hops)
     square = 2 * cols * channels * channels
-    windows, early, w_here, head_here, noise_here = full_call(
+    windows, early, w_here = full_call(
         early_kernel,
         (
             array((6, cols, channels), bf16),
-            array((cols, channels), f32),
+            array((cols + 4 * latent_dim, channels), f32),
             array(taps.shape, bf16),
-            array((2 * latent_dim, channels), bf16),
-            array((latent_dim, cols), bf16),
         ),
         [
             pltpu.VMEM((2, double_cols, channels), bf16),
             pltpu.VMEM((1, channels), f32),
+            pltpu.VMEM((2 * latent_dim, channels), bf16),
+            pltpu.VMEM((latent_dim, cols), bf16),
             pltpu.VMEM((2 * (channels // LANES), double_cols + 8, LANES), f32),
             pltpu.SemaphoreType.DMA((8,)),
         ],
         6 * square,
         5 << 20,
-        "hhhhh",
+        "hhhhhv",
     )(
         activations[0],
         taps,
         conv_bias.reshape(1, channels),
         head_weight.T,
         jnp.transpose(noise_sample[0, 0]),
+        here,
     )
-    early, *far_tiles = lax.optimization_barrier((early, *far_tiles))
-    fixed = lax.ppermute(far_tiles[-1], "col", swap)
+    early, far, above = lax.optimization_barrier((early, far, above))
     rows_a = HALVED * share
     rows_b = (9 - HALVED) * share + TAIL
     half = channels // 2
-    pre_grad, keep_a, send_a, keep_b, send_b = full_call(
-        terms_kernel,
+    pre_act, last_windows, hidden, came = full_call(
+        functools.partial(conv_kernel, spaces),
         (
+            array((cols, channels), f32),
+            array((3, cols, channels), bf16),
             array((cols, channels), bf16),
+            array((2 * tile[0], LANES), bf16),
+        ),
+        [pltpu.VMEM((channels // LANES, double_cols + 8, LANES), f32)],
+        3 * square,
+        2 << 20,
+        "ssvvvv",
+    )(core_at, space_at, early, w_here, far, above)
+    other_came = lax.ppermute(came, "col", swap)
+    pre_grad, moment_grad = full_call(
+        grad_kernel,
+        (array((cols, channels), bf16), array((2 * latent_dim, cols), bf16)),
+        [pltpu.VMEM((spaces, tile[0], 2 * tile[1]), bf16)],
+        square,
+        1 << 20,
+        "ssvvvvv",
+    )(core_at, space_at, early, pre_act, hidden, came, other_came)
+    keep_a, send_a = full_call(
+        early_terms_kernel,
+        (
             array((spaces, rows_a, channels), f32),
             array((spaces, rows_a, channels), bf16),
+        ),
+        [],
+        6 * square,
+        2 << 20,
+        "svv",
+    )(core_at, windows, pre_grad)
+    got_a = lax.ppermute(send_a, "col", swap)
+    keep_b, send_b = full_call(
+        frame_terms_kernel,
+        (
             array((spaces, rows_b, channels), f32),
-            array((spaces, rows_b, channels), bf16),
+            array((spaces, rows_b + cols // spaces, channels), bf16),
         ),
-        [
-            pltpu.VMEM((spaces, tile[0], LANES), bf16),
-            pltpu.VMEM((channels // LANES, double_cols + 8, LANES), f32),
-        ],
-        12 * square,
-        5 << 20,
-        "ss" + "v" * (7 + spaces),
-    )(
-        core_at, space_at, windows, early, w_here, head_here, noise_here, beside, fixed,
-        tile_sets[0], *far_tiles,
-    )
-    beside_grad = lax.ppermute(pre_grad, "col", swap)
-    got_a = lax.ppermute(send_a, "col", swap)
+        [],
+        cols,
+        cols,
+        "svvvv",
+    )(core_at, last_windows, pre_grad, hidden, moment_grad)
     got_b = lax.ppermute(send_b, "col", swap)
     own_a, cross_a = full_call(
         halve_kernel,
@@ -417,19 +481,21 @@
         "svv",
     )(time_at, keep_a, got_a)
     crossed_a = lax.ppermute(cross_a, "tm", swap)
-
     half_grad = cols // 2
-    pieces_b = full_call(
+    *pieces_b, beside_grad = full_call(
         pair_rim_kernel,
-        tuple(
-            array((rows_b + (half_grad if k == 1 else 0), channels), f32 if k == 0 else bf16)
-            for k in range(spaces)
+        (
+            *(
+                array((rows_b + (half_grad if k == 1 else 0), channels), f32 if k == 0 else bf16)
+                for k in range(spaces)
+            ),
+            array((cols, channels), bf16),
         ),
         [],
         spaces * rows_b * channels,
         1 << 20,
-        "ssvvvv",
-    )(core_at, space_at, keep_b, got_b, pre_grad, beside_grad)
+        "ssvvv",
+    )(core_at, space_at, keep_b, got_b, pre_grad)
     far_b = over_space(pieces_b)
     pieces_a = full_call(
         pair_kernel,
@@ -461,7 +527,8 @@
         9 * square,
         4 << 20,
         "ssvvvvv",
-    )(core_at, space_at, pre_grad, beside_grad, low, high, w_here)
+    )(core_at, space_at, pre_grad, beside_grad, low, high, taps)
+    other_a, x_grad = lax.optimization_barrier((other_a, x_grad))
     positions = frames * times * peers * cols
     kernel_grad, head_grad, bias_grad = full_call(
         functools.partial(final_kernel, 1.0 / math.sqrt(positions)),

time: 39.9 us -> 37.4 us (0.937)
  starting transfers between devices: 20.1 us -> 17.7 us
  Pallas kernels: 7.68 us -> 7.18 us
  waiting for transfers between devices: 11.2 us -> 11.6 us
    ppermute x9 -> x6, starting transfers between devices: 16 us -> 8.56 us  [over_space(): lax.ppermute(pieces[k], 'space', [(i, (i + k) % spaces) for i in range(sp...]
    ppermute x5 -> x4, starting transfers between devices: 0.79 us -> 5.34 us  [the longest x1 4.74 us: body(): lax.ppermute(lower, line, [(i, (i - 1) % peers) for i in range(peers)])]
    ppermute x5 -> x4, waiting for transfers between devices: 2.46 us -> 4.55 us  [the longest x1 3.31 us: body(): far = lax.ppermute(far, line, hops)]
    ppermute x9 -> x6, waiting for transfers between devices: 4.87 us -> 3.01 us  [over_space(): lax.ppermute(pieces[k], 'space', [(i, (i + k) % spaces) for i in range(sp...]
    ppermute x1, waiting for transfers between devices: 0.89 us -> 1.53 us  [body(): crossed_a = lax.ppermute(cross_a, 'tm', swap)]
    ppermute x1, waiting for transfers between devices: 1.28 us -> 0.73 us  [body(): got_a = lax.ppermute(send_a, 'col', swap)]
    pallas_call x11 -> x14, Pallas kernels: 7.68 us -> 7.18 us  [placed(): return call(*pinned)]
    ppermute x1, starting transfers between devices: 0.19 us -> 0.63 us  [body(): other_b = lax.ppermute(sum_b, 'tm', swap)]
  transfers between devices with their start and end apart: 20 -> 16, of which waited for: 10 -> 9; matrix products, arithmetic and copies ran while one was open for 0% -> 0% of each run, Pallas kernels for 9% -> 14%
where the time goes in v3:
time: 37.4 us; the launch traced here: 37.3 us
  starting transfers between devices  17.7 us (47%)
  waiting for transfers between devices  11.6 us (31%)
  Pallas kernels  7.18 us (19%)
  between operations  0.73 us (2%)
    ppermute x6, starting transfers between devices, over_space(): lax.ppermute(pieces[k], 'space', [(i, (i + k) % spaces) for i in range(sp...  8.56 us
    pallas_call x14, Pallas kernels, placed(): return call(*pinned)  7.18 us
    ppermute x1, starting transfers between devices, body(): lax.ppermute(lower, line, [(i, (i - 1) % peers) for i in range(peers)])  4.74 us
    ppermute x1, waiting for transfers between devices, body(): far = lax.ppermute(far, line, hops)  3.31 us
    ppermute x6, waiting for transfers between devices, over_space(): lax.ppermute(pieces[k], 'space', [(i, (i + k) % spaces) for i in range(sp...  3.01 us
    ppermute x1, waiting for transfers between devices, body(): other_a = lax.ppermute(sum_a, 'tm', swap)  1.82 us
    ppermute x1, starting transfers between devices, body(): crossed_a = lax.ppermute(cross_a, 'tm', swap)  1.56 us
    ppermute x1, waiting for transfers between devices, body(): crossed_a = lax.ppermute(cross_a, 'tm', swap)  1.53 us
  transfers between devices with their start and end apart: 16, of which 9 were waited for; matrix products, arithmetic and copies ran while one was open for 0% of the time, Pallas kernels for 14%

profile of v3, /device:TPU:0, one launch (start us, length us, event | category | flops | bytes accessed | tf_op | source)
XLA Modules:
  0.0 37.3 jit_solution(15887838928205947582)
XLA Ops:
  0.6 0.5 %collective-permute-start = (bf16[8,16,32]{2,1,0:T(8,128)(2,1)}, bf16[8,16,32]{2,1,0:T(8,128)(2,1)S(1)}, u32[]{:S(2)}, u32[]{:S(2)}) collective-permute-start(bf16[8,16,32]{2,1,0:T(8,128)(2,1)} %bitcast.21), channel_id=1, source_target_pairs={{0,1},{1,0},{2,3},{3,2},{4,5},{5,4},{6,7},{7,6},{8,9},{9,8},{10,11... | collective-permute-start | bytes 24584 | tf_op jit(solution)/shard_map/ppermute | solution.py:374
  1.1 1.0 %shard_map.93 = (bf16[512,256]{1,0:T(8,128)(2,1)S(1)}, bf16[8,16,32]{2,1,0:T(8,128)(2,1)S(1)}) custom-call(bf16[2,512,256]{2,1,0:T(8,128)(2,1)} %bitcast.18, bf16[8,16,32]{2,1,0:T(8,128)(2,1)} %bitcast.22), custom_call_target="tpu_custom_call" | custom-call | bytes 524288 | tf_op jit(solution)/shard_map/pallas_call | solution.py:46
  2.1 0.1 collective-permute-done.got_ref
  2.2 0.1 shard_map.94
  2.3 4.7 %collective-permute-start.2 = (bf16[528,256]{1,0:T(8,128)(2,1)S(1)}, bf16[528,256]{1,0:T(8,128)(2,1)S(1)}, u32[]{:S(2)}, u32[]{:S(2)}) collective-permute-start(bf16[528,256]{1,0:T(8,128)(2,1)S(1)} %get-tuple-element.49), channel_id=1, source_target_pairs={{0,13},{1,0},{4,1},{5,4},{8,5},{9,8},{12,9},{13,12},{2,15},{3,2},{... | collective-permute-start | bytes 811016 | tf_op jit(solution)/shard_map/ppermute | solution.py:395
  7.0 0.0 collective-permute-start.1
  7.1 2.1 %shard_map.95 = (bf16[6,256,256]{2,1,0:T(8,128)(2,1)S(1)}, f32[320,256]{1,0:T(8,128)S(1)}, bf16[9,256,256]{2,1,0:T(8,128)(2,1)S(1)}) custom-call(bf16[2,512,256]{2,1,0:T(8,128)(2,1)} %bitcast.19, bf16[9,256,256]{2,1,0:T(8,128)(2,1)} %bitcast.16, f32[1,256]{1,0:T(1,128)} %bitcast.25, bf16[32,256]{1,0:T(8,128)(2,1)} %bitcast.23, bf16[16,256]{1,0:T(8,128)(2,1)} %bitcast.24, ...), custom_call_target="tpu_custom_call" | custom-call | flops 201326592 | bytes 5242880 | tf_op jit(solution)/shard_map/pallas_call | solution.py:46
  9.1 3.3 %collective-permute-done.1.far_ref = bf16[16,128]{1,0:T(8,128)(2,1)S(1)} collective-permute-done((bf16[16,128]{1,0:T(8,128)(2,1)S(1)}, bf16[16,128]{1,0:T(8,128)(2,1)S(1)}, u32[]{:S(2)}, u32[]{:S(2)}) %collective-permute-start.1) | collective-permute-done | bytes 4128 | tf_op jit(solution)/shard_map/ppermute | solution.py:397
  12.5 0.0 collective-permute-done.2.above_ref
  12.5 0.3 shard_map.96
  12.8 0.1 collective-permute-start.3
  12.9 1.2 %collective-permute-done.3.other_tiles_ref = bf16[32,128]{1,0:T(8,128)(2,1)S(1)} collective-permute-done((bf16[32,128]{1,0:T(8,128)(2,1)S(1)}, bf16[32,128]{1,0:T(8,128)(2,1)S(1)}, u32[]{:S(2)}, u32[]{:S(2)}) %collective-permute-start.3) | collective-permute-done | bytes 8224 | tf_op jit(solution)/shard_map/ppermute | solution.py:442
  14.0 0.4 %shard_map.97 = (bf16[256,256]{1,0:T(8,128)(2,1)S(1)}, bf16[32,256]{1,0:T(8,128)(2,1)S(1)}) custom-call(s32[1]{0:T(128)} %bitcast.2.core_ref, s32[1]{0:T(128)} %bitcast.space_ref, f32[320,256]{1,0:T(8,128)S(1)} %get-tuple-element.50.early_ref, f32[256,256]{1,0:T(8,128)S(1)} %get-tuple-element.54.pre_act_ref, ...), custom_call_target="tpu_custom_call" | custom-call | flops 33554432 | bytes 1048576 | tf_op jit(solution)/shard_map/pallas_call | solution.py:46
  14.5 0.4 %shard_map.98 = (f32[4,192,256]{2,1,0:T(8,128)S(1)}, bf16[4,192,256]{2,1,0:T(8,128)(2,1)S(1)}) custom-call(s32[1]{0:T(128)} %bitcast.2.core_ref, bf16[6,256,256]{2,1,0:T(8,128)(2,1)S(1)} %get-tuple-element.46.windows_ref, bf16[256,256]{1,0:T(8,128)(2,1)S(1)} %get-tuple-element.57.pre_grad_ref.mine_ref), custom_call_target="tpu_custom_call" | custom-call | flops 201326592 | bytes 2097152 | tf_op jit(solution)/shard_map/pallas_call | solution.py:46
  14.9 0.2 collective-permute-start.4
  15.1 0.4 %shard_map.102 = (f32[4,104,256]{2,1,0:T(8,128)S(1)}, bf16[4,168,256]{2,1,0:T(8,128)(2,1)S(1)}) custom-call(s32[1]{0:T(128)} %bitcast.2.core_ref, bf16[3,256,256]{2,1,0:T(8,128)(2,1)S(1)} %get-tuple-element.66.windows_ref, bf16[256,256]{1,0:T(8,128)(2,1)S(1)} %get-tuple-element.57.pre_grad_ref.mine_ref, bf16[256,256]{1,0:T(8,128)(2,1)S(1)} %get-tuple-element.55.hidden_ref, ...), custom_call_target="tpu_custom_call" | custom-call | flops 256 | bytes 256 | tf_op jit(solution)/shard_map/pallas_call | solution.py:46
  15.5 0.4 %collective-permute-start.10 = (bf16[4,168,256]{2,1,0:T(8,128)(2,1)S(1)}, bf16[4,168,256]{2,1,0:T(8,128)(2,1)S(1)}, u32[]{:S(2)}, u32[]{:S(2)}) collective-permute-start(bf16[4,168,256]{2,1,0:T(8,128)(2,1)S(1)} %get-tuple-element.69), channel_id=1, source_target_pairs={{0,1},{1,0},{2,3},{3,2},{4,5},{5,4},{6,7},{7,6},{8,9},{9,8},{10,11... | collective-permute-start | bytes 1032200 | tf_op jit(solution)/shard_map/ppermute | solution.py:474
  15.9 0.7 %collective-permute-done.4.got_ref = bf16[4,192,256]{2,1,0:T(8,128)(2,1)S(1)} collective-permute-done((bf16[4,192,256]{2,1,0:T(8,128)(2,1)S(1)}, bf16[4,192,256]{2,1,0:T(8,128)(2,1)S(1)}, u32[]{:S(2)}, u32[]{:S(2)}) %collective-permute-start.4) | collective-permute-done | bytes 393248 | tf_op jit(solution)/shard_map/ppermute | solution.py:462
  16.7 0.1 shard_map.99
  16.8 0.0 copy-start
  16.8 1.6 %collective-permute-start.5 = (bf16[4,192,128]{2,1,0:T(8,128)(2,1)S(1)}, bf16[4,192,128]{2,1,0:T(8,128)(2,1)S(1)}, u32[]{:S(2)}, u32[]{:S(2)}) collective-permute-start(bf16[4,192,128]{2,1,0:T(8,128)(2,1)S(1)} %get-tuple-element.61), channel_id=1, source_target_pairs={{0,2},{2,0},{1,3},{3,1},{4,6},{6,4},{5,7},{7,5},{8,10},{10,8},{9,1... | collective-permute-start | bytes 589832 | tf_op jit(solution)/shard_map/ppermute | solution.py:483
  18.3 0.0 collective-permute-done.10.got_ref
  18.4 0.1 shard_map.103
  18.4 1.2 %collective-permute-start.11 = (bf16[232,256]{1,0:T(8,128)(2,1)S(1)}, bf16[232,256]{1,0:T(8,128)(2,1)S(1)}, u32[]{:S(2)}, u32[]{:S(2)}) collective-permute-start(bf16[232,256]{1,0:T(8,128)(2,1)S(1)} %get-tuple-element.72), channel_id=1, source_target_pairs={{0,4},{4,8},{8,12},{12,0},{1,5},{5,9},{9,13},{13,1},{2,6},{6,10},{... | collective-permute-start | bytes 356360 | tf_op jit(solution)/shard_map/ppermute | solution.py:369
  19.6 1.8 %collective-permute-start.12 = (bf16[104,256]{1,0:T(8,128)(2,1)S(1)}, bf16[104,256]{1,0:T(8,128)(2,1)S(1)}, u32[]{:S(2)}, u32[]{:S(2)}) collective-permute-start(bf16[104,256]{1,0:T(8,128)(2,1)S(1)} %get-tuple-element.73), channel_id=1, source_target_pairs={{0,8},{4,12},{8,0},{12,4},{1,9},{5,13},{9,1},{13,5},{2,10},{6,14},... | collective-permute-start | bytes 159752 | tf_op jit(solution)/shard_map/ppermute | solution.py:369
  21.4 0.9 %collective-permute-start.13 = (bf16[104,256]{1,0:T(8,128)(2,1)S(1)}, bf16[104,256]{1,0:T(8,128)(2,1)S(1)}, u32[]{:S(2)}, u32[]{:S(2)}) collective-permute-start(bf16[104,256]{1,0:T(8,128)(2,1)S(1)} %get-tuple-element.74), channel_id=1, source_target_pairs={{0,12},{4,0},{8,4},{12,8},{1,13},{5,1},{9,5},{13,9},{2,14},{6,2},{... | collective-permute-start | bytes 159752 | tf_op jit(solution)/shard_map/ppermute | solution.py:369
  22.3 1.5 %collective-permute-done.5.got_ref = bf16[4,192,128]{2,1,0:T(8,128)(2,1)S(1)} collective-permute-done((bf16[4,192,128]{2,1,0:T(8,128)(2,1)S(1)}, bf16[4,192,128]{2,1,0:T(8,128)(2,1)S(1)}, u32[]{:S(2)}, u32[]{:S(2)}) %collective-permute-start.5) | collective-permute-done | bytes 196640 | tf_op jit(solution)/shard_map/ppermute | solution.py:483
  23.9 1.2 %collective-permute-start.6 = (bf16[192,128]{1,0:T(8,128)(2,1)S(1)}, bf16[192,128]{1,0:T(8,128)(2,1)S(1)}, u32[]{:S(2)}, u32[]{:S(2)}) collective-permute-start(bf16[192,128]{1,0:T(8,128)(2,1)S(1)} %get-tuple-element.63), channel_id=1, source_target_pairs={{0,4},{4,8},{8,12},{12,0},{1,5},{5,9},{9,13},{13,1},{2,6},{6,10},{... | collective-permute-start | bytes 147464 | tf_op jit(solution)/shard_map/ppermute | solution.py:369
  25.0 2.0 %collective-permute-start.7 = (bf16[192,128]{1,0:T(8,128)(2,1)S(1)}, bf16[192,128]{1,0:T(8,128)(2,1)S(1)}, u32[]{:S(2)}, u32[]{:S(2)}) collective-permute-start(bf16[192,128]{1,0:T(8,128)(2,1)S(1)} %get-tuple-element.64), channel_id=1, source_target_pairs={{0,8},{4,12},{8,0},{12,4},{1,9},{5,13},{9,1},{13,5},{2,10},{6,14},... | collective-permute-start | bytes 147464 | tf_op jit(solution)/shard_map/ppermute | solution.py:369
  27.0 0.7 %collective-permute-done.12.refs_1_ = bf16[104,256]{1,0:T(8,128)(2,1)S(1)} collective-permute-done((bf16[104,256]{1,0:T(8,128)(2,1)S(1)}, bf16[104,256]{1,0:T(8,128)(2,1)S(1)}, u32[]{:S(2)}, u32[]{:S(2)}) %collective-permute-start.12) | collective-permute-done | bytes 53280 | tf_op jit(solution)/shard_map/ppermute | solution.py:369
  27.7 1.6 %collective-permute-start.8 = (bf16[192,128]{1,0:T(8,128)(2,1)S(1)}, bf16[192,128]{1,0:T(8,128)(2,1)S(1)}, u32[]{:S(2)}, u32[]{:S(2)}) collective-permute-start(bf16[192,128]{1,0:T(8,128)(2,1)S(1)} %get-tuple-element.65), channel_id=1, source_target_pairs={{0,12},{4,0},{8,4},{12,8},{1,13},{5,1},{9,5},{13,9},{2,14},{6,2},{... | collective-permute-start | bytes 147464 | tf_op jit(solution)/shard_map/ppermute | solution.py:369
  29.2 0.0 collective-permute-done.13.refs_2_
  29.3 0.0 collective-permute-done.11.refs_0_
  29.3 0.1 collective-permute-start.14
  29.4 0.6 %collective-permute-start.15 = (bf16[104,256]{1,0:T(8,128)(2,1)S(1)}, bf16[104,256]{1,0:T(8,128)(2,1)S(1)}, u32[]{:S(2)}, u32[]{:S(2)}) collective-permute-start(bf16[104,256]{1,0:T(8,128)(2,1)S(1)} %get-tuple-element.78.b_ref), channel_id=1, source_target_pairs={{0,2},{2,0},{1,3},{3,1},{4,6},{6,4},{5,7},{7,5},{8,10},{10,8},{9,1... | collective-permute-start | bytes 159752 | tf_op jit(solution)/shard_map/ppermute | solution.py:517
  30.0 0.0 collective-permute-done.6.refs_0_
  30.0 2.0 %collective-permute-done.7.refs_1_ = bf16[192,128]{1,0:T(8,128)(2,1)S(1)} collective-permute-done((bf16[192,128]{1,0:T(8,128)(2,1)S(1)}, bf16[192,128]{1,0:T(8,128)(2,1)S(1)}, u32[]{:S(2)}, u32[]{:S(2)}) %collective-permute-start.7) | collective-permute-done | bytes 49184 | tf_op jit(solution)/shard_map/ppermute | solution.py:369
  32.0 0.4 collective-permute-done.8.refs_2_
  32.4 0.9 %collective-permute-start.9 = (bf16[192,128]{1,0:T(8,128)(2,1)S(1)}, bf16[192,128]{1,0:T(8,128)(2,1)S(1)}, u32[]{:S(2)}, u32[]{:S(2)}) collective-permute-start(bf16[192,128]{1,0:T(8,128)(2,1)S(1)} %shard_map.101.a_ref), channel_id=1, source_target_pairs={{0,2},{2,0},{1,3},{3,1},{4,6},{6,4},{5,7},{7,5},{8,10},{10,8},{9,1... | collective-permute-start | bytes 147464 | tf_op jit(solution)/shard_map/ppermute | solution.py:522
  33.3 0.0 collective-permute-done.14.low_ref
  33.3 0.0 copy-done
  33.3 1.4 %shard_map.105 = bf16[2,512,256]{2,1,0:T(8,128)(2,1)} custom-call(s32[1]{0:T(128)} %bitcast.2.core_ref, s32[1]{0:T(128)} %bitcast.space_ref, bf16[256,256]{1,0:T(8,128)(2,1)S(1)} %get-tuple-element.57.pre_grad_ref.mine_ref, bf16[256,256]{1,0:T(8,128)(2,1)S(1)} %get-tuple-element.70.beside_ref, bf16[128,256]{1,0:T(8,128)(2,1)S(1)} %collective-permute-done.14.low_ref, ...), custom_call_target="tpu_custom_call" | custom-call | flops 301989888 | bytes 4194304 | tf_op jit(solution)/shard_map/pallas_call | solution.py:46
  34.7 1.8 %collective-permute-done.9.a_far_ref = bf16[192,128]{1,0:T(8,128)(2,1)S(1)} collective-permute-done((bf16[192,128]{1,0:T(8,128)(2,1)S(1)}, bf16[192,128]{1,0:T(8,128)(2,1)S(1)}, u32[]{:S(2)}, u32[]{:S(2)}) %collective-permute-start.9) | collective-permute-done | bytes 49184 | tf_op jit(solution)/shard_map/ppermute | solution.py:522
  36.5 0.0 collective-permute-done.15.b_far_ref
  36.5 0.8 %shard_map.106 = (f32[9,32,256]{2,1,0:T(8,128)}, f32[32,32]{1,0:T(8,128)}, f32[1,32]{1,0:T(1,128)}) custom-call(s32[1]{0:T(128)} %bitcast.1.time_ref, bf16[192,128]{1,0:T(8,128)(2,1)S(1)} %shard_map.101.a_ref, bf16[192,128]{1,0:T(8,128)(2,1)S(1)} %collective-permute-done.9.a_far_ref, bf16[104,256]{1,0:T(8,128)(2,1)S(1)} %get-tuple-element.78.b_ref, ...), custom_call_target="tpu_custom_call" | custom-call | flops 51200 | bytes 1048576 | tf_op jit(solution)/shard_map/pallas_call | solution.py:46
  (3 shorter events, 0.1 us)
Async XLA Ops:
  0.6 1.6 %collective-permute-start = (bf16[8,16,32]{2,1,0:T(8,128)(2,1)}, bf16[8,16,32]{2,1,0:T(8,128)(2,1)S(1)}, u32[]{:S(2)}, u32[]{:S(2)}) collective-permute-start(bf16[8,16,32]{2,1,0:T(8,128)(2,1)} %bitcast.21), channel_id=1, source_target_pairs={{0,1},{1,0},{2,3},{3,2},{4,5},{5,4},{6,7},{7,6},{8,9},{9,8},{10,11... | collective-permute-start | bytes 24584 | tf_op jit(solution)/shard_map/ppermute | solution.py:374
  2.3 10.2 %collective-permute-start.2 = (bf16[528,256]{1,0:T(8,128)(2,1)S(1)}, bf16[528,256]{1,0:T(8,128)(2,1)S(1)}, u32[]{:S(2)}, u32[]{:S(2)}) collective-permute-start(bf16[528,256]{1,0:T(8,128)(2,1)S(1)} %get-tuple-element.49), channel_id=1, source_target_pairs={{0,13},{1,0},{4,1},{5,4},{8,5},{9,8},{12,9},{13,12},{2,15},{3,2},{... | collective-permute-start | bytes 811016 | tf_op jit(solution)/shard_map/ppermute | solution.py:395
  7.0 5.4 %collective-permute-start.1 = (bf16[16,128]{1,0:T(8,128)(2,1)S(1)}, bf16[16,128]{1,0:T(8,128)(2,1)S(1)}, u32[]{:S(2)}, u32[]{:S(2)}) collective-permute-start(bf16[16,128]{1,0:T(8,128)(2,1)S(1)} %get-tuple-element.48), channel_id=1, source_target_pairs={{0,4},{1,9},{4,8},{5,13},{8,12},{9,1},{12,0},{13,5},{2,6},{3,11},{... | collective-permute-start | bytes 12296 | tf_op jit(solution)/shard_map/ppermute | solution.py:397
  12.8 1.2 %collective-permute-start.3 = (bf16[32,128]{1,0:T(8,128)(2,1)S(1)}, bf16[32,128]{1,0:T(8,128)(2,1)S(1)}, u32[]{:S(2)}, u32[]{:S(2)}) collective-permute-start(bf16[32,128]{1,0:T(8,128)(2,1)S(1)} %get-tuple-element.56.tiles_ref), channel_id=1, source_target_pairs={{0,1},{1,0},{2,3},{3,2},{4,5},{5,4},{6,7},{7,6},{8,9},{9,8},{10,11... | collective-permute-start | bytes 24584 | tf_op jit(solution)/shard_map/ppermute | solution.py:442
  14.9 1.8 %collective-permute-start.4 = (bf16[4,192,256]{2,1,0:T(8,128)(2,1)S(1)}, bf16[4,192,256]{2,1,0:T(8,128)(2,1)S(1)}, u32[]{:S(2)}, u32[]{:S(2)}) collective-permute-start(bf16[4,192,256]{2,1,0:T(8,128)(2,1)S(1)} %get-tuple-element.59), channel_id=1, source_target_pairs={{0,1},{1,0},{2,3},{3,2},{4,5},{5,4},{6,7},{7,6},{8,9},{9,8},{10,11... | collective-permute-start | bytes 1179656 | tf_op jit(solution)/shard_map/ppermute | solution.py:462
  15.5 2.8 %collective-permute-start.10 = (bf16[4,168,256]{2,1,0:T(8,128)(2,1)S(1)}, bf16[4,168,256]{2,1,0:T(8,128)(2,1)S(1)}, u32[]{:S(2)}, u32[]{:S(2)}) collective-permute-start(bf16[4,168,256]{2,1,0:T(8,128)(2,1)S(1)} %get-tuple-element.69), channel_id=1, source_target_pairs={{0,1},{1,0},{2,3},{3,2},{4,5},{5,4},{6,7},{7,6},{8,9},{9,8},{10,11... | collective-permute-start | bytes 1032200 | tf_op jit(solution)/shard_map/ppermute | solution.py:474
  16.8 16.5 %copy-start = (bf16[3,3,256,256]{3,2,1,0:T(8,128)(2,1)S(1)}, bf16[3,3,256,256]{3,2,1,0:T(8,128)(2,1)}, u32[]{:S(2)}) copy-start(bf16[3,3,256,256]{3,2,1,0:T(8,128)(2,1)} %param.7) | copy-start | bytes 3538948
  16.8 7.0 %collective-permute-start.5 = (bf16[4,192,128]{2,1,0:T(8,128)(2,1)S(1)}, bf16[4,192,128]{2,1,0:T(8,128)(2,1)S(1)}, u32[]{:S(2)}, u32[]{:S(2)}) collective-permute-start(bf16[4,192,128]{2,1,0:T(8,128)(2,1)S(1)} %get-tuple-element.61), channel_id=1, source_target_pairs={{0,2},{2,0},{1,3},{3,1},{4,6},{6,4},{5,7},{7,5},{8,10},{10,8},{9,1... | collective-permute-start | bytes 589832 | tf_op jit(solution)/shard_map/ppermute | solution.py:483
  18.4 10.8 %collective-permute-start.11 = (bf16[232,256]{1,0:T(8,128)(2,1)S(1)}, bf16[232,256]{1,0:T(8,128)(2,1)S(1)}, u32[]{:S(2)}, u32[]{:S(2)}) collective-permute-start(bf16[232,256]{1,0:T(8,128)(2,1)S(1)} %get-tuple-element.72), channel_id=1, source_target_pairs={{0,4},{4,8},{8,12},{12,0},{1,5},{5,9},{9,13},{13,1},{2,6},{6,10},{... | collective-permute-start | bytes 356360 | tf_op jit(solution)/shard_map/ppermute | solution.py:369
  19.6 8.1 %collective-permute-start.12 = (bf16[104,256]{1,0:T(8,128)(2,1)S(1)}, bf16[104,256]{1,0:T(8,128)(2,1)S(1)}, u32[]{:S(2)}, u32[]{:S(2)}) collective-permute-start(bf16[104,256]{1,0:T(8,128)(2,1)S(1)} %get-tuple-element.73), channel_id=1, source_target_pairs={{0,8},{4,12},{8,0},{12,4},{1,9},{5,13},{9,1},{13,5},{2,10},{6,14},... | collective-permute-start | bytes 159752 | tf_op jit(solution)/shard_map/ppermute | solution.py:369
  21.4 7.9 %collective-permute-start.13 = (bf16[104,256]{1,0:T(8,128)(2,1)S(1)}, bf16[104,256]{1,0:T(8,128)(2,1)S(1)}, u32[]{:S(2)}, u32[]{:S(2)}) collective-permute-start(bf16[104,256]{1,0:T(8,128)(2,1)S(1)} %get-tuple-element.74), channel_id=1, source_target_pairs={{0,12},{4,0},{8,4},{12,8},{1,13},{5,1},{9,5},{13,9},{2,14},{6,2},{... | collective-permute-start | bytes 159752 | tf_op jit(solution)/shard_map/ppermute | solution.py:369
  23.9 6.1 %collective-permute-start.6 = (bf16[192,128]{1,0:T(8,128)(2,1)S(1)}, bf16[192,128]{1,0:T(8,128)(2,1)S(1)}, u32[]{:S(2)}, u32[]{:S(2)}) collective-permute-start(bf16[192,128]{1,0:T(8,128)(2,1)S(1)} %get-tuple-element.63), channel_id=1, source_target_pairs={{0,4},{4,8},{8,12},{12,0},{1,5},{5,9},{9,13},{13,1},{2,6},{6,10},{... | collective-permute-start | bytes 147464 | tf_op jit(solution)/shard_map/ppermute | solution.py:369
  25.0 6.9 %collective-permute-start.7 = (bf16[192,128]{1,0:T(8,128)(2,1)S(1)}, bf16[192,128]{1,0:T(8,128)(2,1)S(1)}, u32[]{:S(2)}, u32[]{:S(2)}) collective-permute-start(bf16[192,128]{1,0:T(8,128)(2,1)S(1)} %get-tuple-element.64), channel_id=1, source_target_pairs={{0,8},{4,12},{8,0},{12,4},{1,9},{5,13},{9,1},{13,5},{2,10},{6,14},... | collective-permute-start | bytes 147464 | tf_op jit(solution)/shard_map/ppermute | solution.py:369
  27.7 4.6 %collective-permute-start.8 = (bf16[192,128]{1,0:T(8,128)(2,1)S(1)}, bf16[192,128]{1,0:T(8,128)(2,1)S(1)}, u32[]{:S(2)}, u32[]{:S(2)}) collective-permute-start(bf16[192,128]{1,0:T(8,128)(2,1)S(1)} %get-tuple-element.65), channel_id=1, source_target_pairs={{0,12},{4,0},{8,4},{12,8},{1,13},{5,1},{9,5},{13,9},{2,14},{6,2},{... | collective-permute-start | bytes 147464 | tf_op jit(solution)/shard_map/ppermute | solution.py:369
  29.3 4.0 %collective-permute-start.14 = (bf16[128,256]{1,0:T(8,128)(2,1)S(1)}, bf16[128,256]{1,0:T(8,128)(2,1)S(1)}, u32[]{:S(2)}, u32[]{:S(2)}) collective-permute-start(bf16[128,256]{1,0:T(8,128)(2,1)S(1)} %get-tuple-element.75.high_ref), channel_id=1, source_target_pairs={{0,1},{1,0},{2,3},{3,2},{4,5},{5,4},{6,7},{7,6},{8,9},{9,8},{10,11... | collective-permute-start | bytes 196616 | tf_op jit(solution)/shard_map/ppermute | solution.py:518
  29.4 7.1 %collective-permute-start.15 = (bf16[104,256]{1,0:T(8,128)(2,1)S(1)}, bf16[104,256]{1,0:T(8,128)(2,1)S(1)}, u32[]{:S(2)}, u32[]{:S(2)}) collective-permute-start(bf16[104,256]{1,0:T(8,128)(2,1)S(1)} %get-tuple-element.78.b_ref), channel_id=1, source_target_pairs={{0,2},{2,0},{1,3},{3,1},{4,6},{6,4},{5,7},{7,5},{8,10},{10,8},{9,1... | collective-permute-start | bytes 159752 | tf_op jit(solution)/shard_map/ppermute | solution.py:517
  32.4 4.2 %collective-permute-start.9 = (bf16[192,128]{1,0:T(8,128)(2,1)S(1)}, bf16[192,128]{1,0:T(8,128)(2,1)S(1)}, u32[]{:S(2)}, u32[]{:S(2)}) collective-permute-start(bf16[192,128]{1,0:T(8,128)(2,1)S(1)} %shard_map.101.a_ref), channel_id=1, source_target_pairs={{0,2},{2,0},{1,3},{3,1},{4,6},{6,4},{5,7},{7,5},{8,10},{10,8},{9,1... | collective-permute-start | bytes 147464 | tf_op jit(solution)/shard_map/ppermute | solution.py:522

commit v4 on v3

--- a/solution.py
+++ b/solution.py
@@ -103,7 +103,7 @@
 
 def early_kernel(
     act_ref, w_in, bias_in, head_in, noise_in, here_ref,
-    windows_ref, pre_act_ref, w_ref, act, bias, head, noise, stage, sems,
+    pre_act_ref, w_ref, act, bias, head, noise, stage, sems,
 ):
     pairs = [
         (act_ref.at[0], act.at[0]), (w_in.at[:3], w_ref.at[:3]),
@@ -122,7 +122,6 @@
         windows = split_columns(row, act[row], stage)
         copies[2 * row + 1].wait()
         for tap in range(3):
-            windows_ref[3 * row + tap] = windows[tap]
             pre_act = pre_act + dot(windows[tap], w_ref[3 * row + tap], 1, 0)
     pre_act_ref[:cols, :] = pre_act
     for copy in copies[5:]:
@@ -131,6 +130,26 @@
     for ref in (head, noise, here_ref):
         pre_act_ref[at : at + ref.shape[0], : ref.shape[1]] = ref[...].astype(f32)
         at += ref.shape[0]
+
+
+def select_kernel(chips, core_ref, act_in, beside_ref, windows_ref, act, stage, sem):
+    copy = pltpu.make_async_copy(act_in, act, sem)
+    copy.start()
+    rows, length, width = beside_ref.shape
+    kept = windows_ref.shape[2]
+    share = kept // chips
+    source = lax.broadcasted_iota(jnp.int32, (width, kept), 0)
+    target = lax.broadcasted_iota(jnp.int32, (width, kept), 1)
+    wanted = 2 * share * (target // share) + share * core_ref[0] + target % share
+    select = jnp.where(source == wanted, 1.0, 0.0).astype(bf16)
+    copy.wait()
+    cols = length // 2
+    for row in range(rows):
+        for at, ref in enumerate((act, beside_ref)):
+            picked = dot(ref[row], select, 1, 0)
+            windows = split_columns(rows * at + row, picked, stage)
+            for tap in range(3):
+                windows_ref[3 * row + tap, cols * at : cols * (at + 1), :] = windows[tap]
 
 
 def conv_kernel(
@@ -224,26 +243,24 @@
     for s in range(2 * spaces):
         tails.append(tail(share * s))
     put_shares(first, keep_ref, send_ref, taps * share, jnp.concatenate(tails, 0))
-    rows, part = keep_ref.shape[1], cols // spaces
-    for s in range(spaces):
-        send_ref[s, rows:, :] = pre_grad[part * s : part * (s + 1)]
-
-
-def early_terms_kernel(core_ref, windows_ref, pre_grad_ref, keep_ref, send_ref):
-    first = core_ref[0] == 0
-    pre_grad = pre_grad_ref[...]
-    share = pre_grad.shape[1] // (2 * keep_ref.shape[0])
+
+
+def chip_terms_kernel(
+    time_ref, windows_ref, pre_grad_ref, beside_ref, own_ref, send_ref
+):
+    first = time_ref[0] == 0
+    pre_grad = jnp.concatenate([pre_grad_ref[...], beside_ref[...]], 0)
+    spaces, _, half = own_ref.shape
+    share = windows_ref.shape[2] // spaces
     for index in range(HALVED):
         term = dot(windows_ref[index], pre_grad, 0, 0)
-        put_shares(first, keep_ref, send_ref, index * share, term)
-
-
-def halve_kernel(time_ref, keep_ref, got_ref, own_ref, send_ref):
-    half = own_ref.shape[2]
-    first = time_ref[0] == 0
-    total = keep_ref[...] + got_ref[...].astype(f32)
-    own_ref[...] = jnp.where(first, total[:, :, :half], total[:, :, half:])
-    send_ref[...] = jnp.where(first, total[:, :, half:], total[:, :, :half]).astype(bf16)
+        low, high = term[:, :half], term[:, half:]
+        mine = jnp.where(first, low, high)
+        other = jnp.where(first, high, low).astype(bf16)
+        here = slice(index * share, (index + 1) * share)
+        for s in range(spaces):
+            own_ref[s, here, :] = mine[s * share : (s + 1) * share]
+            send_ref[s, here, :] = other[s * share : (s + 1) * share]
 
 
 def pair_kernel(space_ref, keep_ref, got_ref, *outs):
@@ -253,18 +270,15 @@
         out[...] = (keep_ref[at] + got_ref[at].astype(f32)).astype(out.dtype)
 
 
-def pair_rim_kernel(core_ref, space_ref, keep_ref, got_ref, mine_ref, *outs):
-    *outs, beside_ref = outs
+def pair_rim_kernel(core_ref, space_ref, keep_ref, got_ref, mine_ref, beside_ref, *outs):
     spaces = len(outs)
     rows = keep_ref.shape[1]
     for k, out in enumerate(outs):
         at = lax.rem(space_ref[0] + k, spaces)
-        out[:rows, :] = (keep_ref[at] + got_ref[at, :rows, :].astype(f32)).astype(out.dtype)
+        out[:rows, :] = (keep_ref[at] + got_ref[at].astype(f32)).astype(out.dtype)
     half = mine_ref.shape[0] // 2
     first = core_ref[0] == 0
-    beside = jnp.concatenate([got_ref[s, rows:, :] for s in range(spaces)], 0)
-    beside_ref[...] = beside
-    outs[1][rows:, :] = jnp.where(first, beside[half:], mine_ref[:half, :])
+    outs[1][rows:, :] = jnp.where(first, beside_ref[half:, :], mine_ref[:half, :])
 
 
 def line_kernel(own_ref, *refs):
@@ -392,14 +406,14 @@
         1 << 18,
         "ssvvv",
     )(core_at, space_at, row, own_tiles, got_tiles)
+    late_rows, lower = lax.optimization_barrier((activations[0], lower))
     above = lax.ppermute(lower, line, [(i, (i - 1) % peers) for i in range(peers)])
     hops = [(2 * i + c, 2 * ((i + 1 + c) % spaces) + c) for i in range(spaces) for c in range(2)]
     far = lax.ppermute(far, line, hops)
     square = 2 * cols * channels * channels
-    windows, early, w_here = full_call(
+    early, w_here = full_call(
         early_kernel,
         (
-            array((6, cols, channels), bf16),
             array((cols + 4 * latent_dim, channels), f32),
             array(taps.shape, bf16),
         ),
@@ -411,7 +425,7 @@
             pltpu.VMEM((2 * (channels // LANES), double_cols + 8, LANES), f32),
             pltpu.SemaphoreType.DMA((8,)),
         ],
-        6 * square,
+        120 * square,
         5 << 20,
         "hhhhhv",
     )(
@@ -422,7 +436,20 @@
         jnp.transpose(noise_sample[0, 0]),
         here,
     )
-    early, far, above = lax.optimization_barrier((early, far, above))
+    beside = lax.ppermute(late_rows, "col", swap)
+    chip_windows = full_call(
+        functools.partial(select_kernel, spaces),
+        array((6, 2 * cols, channels // 2), bf16),
+        [
+            pltpu.VMEM((2, double_cols, channels), bf16),
+            pltpu.VMEM((4 * (channels // 2 // LANES), double_cols + 8, LANES), f32),
+            pltpu.SemaphoreType.DMA,
+        ],
+        4 * square,
+        2 << 20,
+        "shv",
+    )(core_at, activations[0], beside)
+    early, chip_windows, far, above = lax.optimization_barrier((early, chip_windows, far, above))
     rows_a = HALVED * share
     rows_b = (9 - HALVED) * share + TAIL
     half = channels // 2
@@ -448,23 +475,12 @@
         1 << 20,
         "ssvvvvv",
     )(core_at, space_at, early, pre_act, hidden, came, other_came)
-    keep_a, send_a = full_call(
-        early_terms_kernel,
-        (
-            array((spaces, rows_a, channels), f32),
-            array((spaces, rows_a, channels), bf16),
-        ),
-        [],
-        6 * square,
-        2 << 20,
-        "svv",
-    )(core_at, windows, pre_grad)
-    got_a = lax.ppermute(send_a, "col", swap)
+    beside_grad = lax.ppermute(pre_grad, "col", swap)
     keep_b, send_b = full_call(
         frame_terms_kernel,
         (
             array((spaces, rows_b, channels), f32),
-            array((spaces, rows_b + cols // spaces, channels), bf16),
+            array((spaces, rows_b, channels), bf16),
         ),
         [],
         cols,
@@ -473,29 +489,26 @@
     )(core_at, last_windows, pre_grad, hidden, moment_grad)
     got_b = lax.ppermute(send_b, "col", swap)
     own_a, cross_a = full_call(
-        halve_kernel,
+        chip_terms_kernel,
         (array((spaces, rows_a, half), f32), array((spaces, rows_a, half), bf16)),
         [],
-        spaces * rows_a * channels,
+        6 * square,
         2 << 20,
-        "svv",
-    )(time_at, keep_a, got_a)
+        "svvv",
+    )(time_at, chip_windows, pre_grad, beside_grad)
     crossed_a = lax.ppermute(cross_a, "tm", swap)
     half_grad = cols // 2
-    *pieces_b, beside_grad = full_call(
+    pieces_b = full_call(
         pair_rim_kernel,
-        (
-            *(
-                array((rows_b + (half_grad if k == 1 else 0), channels), f32 if k == 0 else bf16)
-                for k in range(spaces)
-            ),
-            array((cols, channels), bf16),
+        tuple(
+            array((rows_b + (half_grad if k == 1 else 0), channels), f32 if k == 0 else bf16)
+            for k in range(spaces)
         ),
         [],
         spaces * rows_b * channels,
         1 << 20,
-        "ssvvv",
-    )(core_at, space_at, keep_b, got_b, pre_grad)
+        "ssvvvv",
+    )(core_at, space_at, keep_b, got_b, pre_grad, beside_grad)
     far_b = over_space(pieces_b)
     pieces_a = full_call(
         pair_kernel,

time: 37.4 us -> 36.8 us (0.984)
  waiting for transfers between devices: 11.6 us -> 7.16 us
  starting transfers between devices: 17.7 us -> 20.1 us
  Pallas kernels: 7.18 us -> 8.6 us
    ppermute x1, waiting for transfers between devices: 3.31 us -> 0.01 us  [body(): far = lax.ppermute(far, line, hops)]
    ppermute x1, starting transfers between devices: 0.01 us -> 2.73 us  [body(): far = lax.ppermute(far, line, hops)]
    ppermute x1, starting transfers between devices: 4.74 us -> 2.03 us  [body(): lax.ppermute(lower, line, [(i, (i - 1) % peers) for i in range(peers)])]
    pallas_call x14, Pallas kernels: 7.18 us -> 8.6 us  [placed(): return call(*pinned)]
    ppermute x1, starting transfers between devices: 0.07 us -> 1.02 us  [body(): other_came = lax.ppermute(came, 'col', swap)]
    ppermute x6, starting transfers between devices: 8.56 us -> 9.39 us  [over_space(): lax.ppermute(pieces[k], 'space', [(i, (i + k) % spaces) for i in range(sp...]
    ppermute x1 -> x2, starting transfers between devices: 0.23 us -> 0.8 us  [the longest x1 0.41 us: body(): beside_grad = lax.ppermute(pre_grad, 'col', swap)]
    ppermute x6, waiting for transfers between devices: 3.01 us -> 2.47 us  [over_space(): lax.ppermute(pieces[k], 'space', [(i, (i + k) % spaces) for i in range(sp...]
  transfers between devices with their start and end apart: 16 -> 17, of which waited for: 9 -> 9; matrix products, arithmetic and copies ran while one was open for 0% -> 0% of each run, Pallas kernels for 14% -> 19%
where the time goes in v4:
time: 36.8 us; the launch traced here: 36.6 us
  starting transfers between devices  20.1 us (55%)
  Pallas kernels  8.6 us (23%)
  waiting for transfers between devices  7.16 us (19%)
  between operations  0.75 us (2%)
    ppermute x6, starting transfers between devices, over_space(): lax.ppermute(pieces[k], 'space', [(i, (i + k) % spaces) for i in range(sp...  9.39 us
    pallas_call x14, Pallas kernels, placed(): return call(*pinned)  8.6 us
    ppermute x1, starting transfers between devices, body(): far = lax.ppermute(far, line, hops)  2.73 us
    ppermute x6, waiting for transfers between devices, over_space(): lax.ppermute(pieces[k], 'space', [(i, (i + k) % spaces) for i in range(sp...  2.47 us
    ppermute x1, starting transfers between devices, body(): lax.ppermute(lower, line, [(i, (i - 1) % peers) for i in range(peers)])  2.03 us
    ppermute x1, waiting for transfers between devices, body(): other_a = lax.ppermute(sum_a, 'tm', swap)  1.57 us
    ppermute x1, starting transfers between devices, body(): crossed_a = lax.ppermute(cross_a, 'tm', swap)  1.56 us
    ppermute x1, waiting for transfers between devices, body(): crossed_a = lax.ppermute(cross_a, 'tm', swap)  1.53 us
  transfers between devices with their start and end apart: 17, of which 9 were waited for; matrix products, arithmetic and copies ran while one was open for 0% of the time, Pallas kernels for 19%

profile of v4, /device:TPU:0, one launch (start us, length us, event | category | flops | bytes accessed | tf_op | source)
XLA Modules:
  0.0 36.6 jit_solution(6880358983455847222)
XLA Ops:
  0.6 0.5 %collective-permute-start = (bf16[8,16,32]{2,1,0:T(8,128)(2,1)}, bf16[8,16,32]{2,1,0:T(8,128)(2,1)S(1)}, u32[]{:S(2)}, u32[]{:S(2)}) collective-permute-start(bf16[8,16,32]{2,1,0:T(8,128)(2,1)} %bitcast.23), channel_id=1, source_target_pairs={{0,1},{1,0},{2,3},{3,2},{4,5},{5,4},{6,7},{7,6},{8,9},{9,8},{10,11... | collective-permute-start | bytes 24584 | tf_op jit(solution)/shard_map/ppermute | solution.py:388
  1.1 1.0 %shard_map.93 = (bf16[512,256]{1,0:T(8,128)(2,1)S(1)}, bf16[8,16,32]{2,1,0:T(8,128)(2,1)S(1)}) custom-call(bf16[2,512,256]{2,1,0:T(8,128)(2,1)} %bitcast.18, bf16[8,16,32]{2,1,0:T(8,128)(2,1)} %bitcast.24), custom_call_target="tpu_custom_call" | custom-call | bytes 524288 | tf_op jit(solution)/shard_map/pallas_call | solution.py:46
  2.1 0.1 collective-permute-done.got_ref
  2.2 0.1 shard_map.94
  2.3 0.4 %collective-permute-start.1 = (bf16[2,512,256]{2,1,0:T(8,128)(2,1)}, bf16[2,512,256]{2,1,0:T(8,128)(2,1)S(1)}, u32[]{:S(2)}, u32[]{:S(2)}) collective-permute-start(bf16[2,512,256]{2,1,0:T(8,128)(2,1)} %bitcast.19), channel_id=1, source_target_pairs={{0,1},{1,0},{2,3},{3,2},{4,5},{5,4},{6,7},{7,6},{8,9},{9,8},{10,11... | collective-permute-start | bytes 1572872 | tf_op jit(solution)/shard_map/ppermute | solution.py:439
  2.7 2.7 %collective-permute-start.2 = (bf16[16,128]{1,0:T(8,128)(2,1)S(1)}, bf16[16,128]{1,0:T(8,128)(2,1)S(1)}, u32[]{:S(2)}, u32[]{:S(2)}) collective-permute-start(bf16[16,128]{1,0:T(8,128)(2,1)S(1)} %get-tuple-element.48), channel_id=1, source_target_pairs={{0,4},{1,9},{4,8},{5,13},{8,12},{9,1},{12,0},{13,5},{2,6},{3,11},{... | collective-permute-start | bytes 12296 | tf_op jit(solution)/shard_map/ppermute | solution.py:412
  5.4 2.0 %collective-permute-start.3 = (bf16[528,256]{1,0:T(8,128)(2,1)S(1)}, bf16[528,256]{1,0:T(8,128)(2,1)S(1)}, u32[]{:S(2)}, u32[]{:S(2)}) collective-permute-start(bf16[528,256]{1,0:T(8,128)(2,1)S(1)} %get-tuple-element.49), channel_id=1, source_target_pairs={{0,13},{1,0},{4,1},{5,4},{8,5},{9,8},{12,9},{13,12},{2,15},{3,2},{... | collective-permute-start | bytes 811016 | tf_op jit(solution)/shard_map/ppermute | solution.py:410
  7.5 2.0 %shard_map.95 = (f32[320,256]{1,0:T(8,128)S(1)}, bf16[9,256,256]{2,1,0:T(8,128)(2,1)S(1)}) custom-call(bf16[2,512,256]{2,1,0:T(8,128)(2,1)} %bitcast.20, bf16[9,256,256]{2,1,0:T(8,128)(2,1)} %bitcast.16, f32[1,256]{1,0:T(1,128)} %bitcast.28, bf16[32,256]{1,0:T(8,128)(2,1)} %bitcast.26, bf16[16,256]{1,0:T(8,128)(2,1)} %bitcast.27, ...), custom_call_target="tpu_custom_call" | custom-call | flops 4026531840 | bytes 5242880 | tf_op jit(solution)/shard_map/pallas_call | solution.py:46
  9.5 0.0 collective-permute-done.1.beside_ref
  9.5 1.6 %shard_map.96.windows_ref = bf16[6,512,128]{2,1,0:T(8,128)(2,1)S(1)} custom-call(s32[1]{0:T(128)} %bitcast.8.core_ref, bf16[2,512,256]{2,1,0:T(8,128)(2,1)} %bitcast.21, bf16[2,512,256]{2,1,0:T(8,128)(2,1)S(1)} %collective-permute-done.1.beside_ref), custom_call_target="tpu_custom_call" | custom-call | flops 134217728 | bytes 2097152 | tf_op jit(solution)/shard_map/pallas_call | solution.py:46
  11.1 0.0 collective-permute-done.2.far_ref
  11.1 0.3 collective-permute-done.3.above_ref
  11.4 0.3 shard_map.97
  11.8 1.0 %collective-permute-start.4 = (bf16[32,128]{1,0:T(8,128)(2,1)S(1)}, bf16[32,128]{1,0:T(8,128)(2,1)S(1)}, u32[]{:S(2)}, u32[]{:S(2)}) collective-permute-start(bf16[32,128]{1,0:T(8,128)(2,1)S(1)} %get-tuple-element.57.tiles_ref), channel_id=1, source_target_pairs={{0,1},{1,0},{2,3},{3,2},{4,5},{5,4},{6,7},{7,6},{8,9},{9,8},{10,11... | collective-permute-start | bytes 24584 | tf_op jit(solution)/shard_map/ppermute | solution.py:469
  12.8 0.8 %collective-permute-done.4.other_tiles_ref = bf16[32,128]{1,0:T(8,128)(2,1)S(1)} collective-permute-done((bf16[32,128]{1,0:T(8,128)(2,1)S(1)}, bf16[32,128]{1,0:T(8,128)(2,1)S(1)}, u32[]{:S(2)}, u32[]{:S(2)}) %collective-permute-start.4) | collective-permute-done | bytes 8224 | tf_op jit(solution)/shard_map/ppermute | solution.py:469
  13.6 0.4 %shard_map.98 = (bf16[256,256]{1,0:T(8,128)(2,1)S(1)}, bf16[32,256]{1,0:T(8,128)(2,1)S(1)}) custom-call(s32[1]{0:T(128)} %bitcast.8.core_ref, s32[1]{0:T(128)} %bitcast.space_ref, f32[320,256]{1,0:T(8,128)S(1)} %get-tuple-element.51.early_ref, f32[256,256]{1,0:T(8,128)S(1)} %get-tuple-element.55.pre_act_ref, ...), custom_call_target="tpu_custom_call" | custom-call | flops 33554432 | bytes 1048576 | tf_op jit(solution)/shard_map/pallas_call | solution.py:46
  14.1 0.4 %collective-permute-start.5 = (bf16[256,256]{1,0:T(8,128)(2,1)S(1)}, bf16[256,256]{1,0:T(8,128)(2,1)S(1)}, u32[]{:S(2)}, u32[]{:S(2)}) collective-permute-start(bf16[256,256]{1,0:T(8,128)(2,1)S(1)} %get-tuple-element.58.pre_grad_ref.mine_ref), channel_id=1, source_target_pairs={{0,1},{1,0},{2,3},{3,2},{4,5},{5,4},{6,7},{7,6},{8,9},{9,8},{10,11... | collective-permute-start | bytes 393224 | tf_op jit(solution)/shard_map/ppermute | solution.py:478
  14.5 0.4 %shard_map.102 = (f32[4,104,256]{2,1,0:T(8,128)S(1)}, bf16[4,104,256]{2,1,0:T(8,128)(2,1)S(1)}) custom-call(s32[1]{0:T(128)} %bitcast.8.core_ref, bf16[3,256,256]{2,1,0:T(8,128)(2,1)S(1)} %get-tuple-element.65.windows_ref, bf16[256,256]{1,0:T(8,128)(2,1)S(1)} %get-tuple-element.58.pre_grad_ref.mine_ref, bf16[256,256]{1,0:T(8,128)(2,1)S(1)} %get-tuple-element.56.hidden_ref, ...), custom_call_target="tpu_custom_call" | custom-call | flops 256 | bytes 256 | tf_op jit(solution)/shard_map/pallas_call | solution.py:46
  14.9 0.2 collective-permute-start.11
  15.1 0.4 collective-permute-done.5.beside_ref
  15.5 0.4 %shard_map.99 = (f32[4,192,128]{2,1,0:T(8,128)S(1)}, bf16[4,192,128]{2,1,0:T(8,128)(2,1)S(1)}) custom-call(s32[1]{0:T(128)} %bitcast.1.time_ref, bf16[6,512,128]{2,1,0:T(8,128)(2,1)S(1)} %shard_map.96.windows_ref, bf16[256,256]{1,0:T(8,128)(2,1)S(1)} %get-tuple-element.58.pre_grad_ref.mine_ref, bf16[256,256]{1,0:T(8,128)(2,1)S(1)} %collective-permute-done.5.beside_ref), custom_call_target="tpu_custom_call" | custom-call | flops 201326592 | bytes 2097152 | tf_op jit(solution)/shard_map/pallas_call | solution.py:46
  15.9 0.0 copy-start
  15.9 1.6 %collective-permute-start.6 = (bf16[4,192,128]{2,1,0:T(8,128)(2,1)S(1)}, bf16[4,192,128]{2,1,0:T(8,128)(2,1)S(1)}, u32[]{:S(2)}, u32[]{:S(2)}) collective-permute-start(bf16[4,192,128]{2,1,0:T(8,128)(2,1)S(1)} %get-tuple-element.60), channel_id=1, source_target_pairs={{0,2},{2,0},{1,3},{3,1},{4,6},{6,4},{5,7},{7,5},{8,10},{10,8},{9,1... | collective-permute-start | bytes 589832 | tf_op jit(solution)/shard_map/ppermute | solution.py:499
  17.5 0.0 collective-permute-done.11.got_ref
  17.5 0.1 shard_map.103
  17.5 1.6 %collective-permute-start.12 = (bf16[232,256]{1,0:T(8,128)(2,1)S(1)}, bf16[232,256]{1,0:T(8,128)(2,1)S(1)}, u32[]{:S(2)}, u32[]{:S(2)}) collective-permute-start(bf16[232,256]{1,0:T(8,128)(2,1)S(1)} %get-tuple-element.70), channel_id=1, source_target_pairs={{0,4},{4,8},{8,12},{12,0},{1,5},{5,9},{9,13},{13,1},{2,6},{6,10},{... | collective-permute-start | bytes 356360 | tf_op jit(solution)/shard_map/ppermute | solution.py:383
  19.1 2.1 %collective-permute-start.13 = (bf16[104,256]{1,0:T(8,128)(2,1)S(1)}, bf16[104,256]{1,0:T(8,128)(2,1)S(1)}, u32[]{:S(2)}, u32[]{:S(2)}) collective-permute-start(bf16[104,256]{1,0:T(8,128)(2,1)S(1)} %get-tuple-element.71), channel_id=1, source_target_pairs={{0,8},{4,12},{8,0},{12,4},{1,9},{5,13},{9,1},{13,5},{2,10},{6,14},... | collective-permute-start | bytes 159752 | tf_op jit(solution)/shard_map/ppermute | solution.py:383
  21.3 0.3 collective-permute-start.14
  21.6 1.5 %collective-permute-done.6.got_ref = bf16[4,192,128]{2,1,0:T(8,128)(2,1)S(1)} collective-permute-done((bf16[4,192,128]{2,1,0:T(8,128)(2,1)S(1)}, bf16[4,192,128]{2,1,0:T(8,128)(2,1)S(1)}, u32[]{:S(2)}, u32[]{:S(2)}) %collective-permute-start.6) | collective-permute-done | bytes 196640 | tf_op jit(solution)/shard_map/ppermute | solution.py:499
  23.2 1.6 %collective-permute-start.7 = (bf16[192,128]{1,0:T(8,128)(2,1)S(1)}, bf16[192,128]{1,0:T(8,128)(2,1)S(1)}, u32[]{:S(2)}, u32[]{:S(2)}) collective-permute-start(bf16[192,128]{1,0:T(8,128)(2,1)S(1)} %get-tuple-element.62), channel_id=1, source_target_pairs={{0,4},{4,8},{8,12},{12,0},{1,5},{5,9},{9,13},{13,1},{2,6},{6,10},{... | collective-permute-start | bytes 147464 | tf_op jit(solution)/shard_map/ppermute | solution.py:383
  24.8 2.1 %collective-permute-start.8 = (bf16[192,128]{1,0:T(8,128)(2,1)S(1)}, bf16[192,128]{1,0:T(8,128)(2,1)S(1)}, u32[]{:S(2)}, u32[]{:S(2)}) collective-permute-start(bf16[192,128]{1,0:T(8,128)(2,1)S(1)} %get-tuple-element.63), channel_id=1, source_target_pairs={{0,8},{4,12},{8,0},{12,4},{1,9},{5,13},{9,1},{13,5},{2,10},{6,14},... | collective-permute-start | bytes 147464 | tf_op jit(solution)/shard_map/ppermute | solution.py:383
  26.9 0.0 collective-permute-done.13.refs_1_
  26.9 1.6 %collective-permute-start.9 = (bf16[192,128]{1,0:T(8,128)(2,1)S(1)}, bf16[192,128]{1,0:T(8,128)(2,1)S(1)}, u32[]{:S(2)}, u32[]{:S(2)}) collective-permute-start(bf16[192,128]{1,0:T(8,128)(2,1)S(1)} %get-tuple-element.64), channel_id=1, source_target_pairs={{0,12},{4,0},{8,4},{12,8},{1,13},{5,1},{9,5},{13,9},{2,14},{6,2},{... | collective-permute-start | bytes 147464 | tf_op jit(solution)/shard_map/ppermute | solution.py:383
  28.5 0.0 collective-permute-done.14.refs_2_
  28.5 0.0 collective-permute-done.12.refs_0_
  28.5 0.1 collective-permute-start.15
  28.6 0.6 %collective-permute-start.16 = (bf16[104,256]{1,0:T(8,128)(2,1)S(1)}, bf16[104,256]{1,0:T(8,128)(2,1)S(1)}, u32[]{:S(2)}, u32[]{:S(2)}) collective-permute-start(bf16[104,256]{1,0:T(8,128)(2,1)S(1)} %get-tuple-element.76.b_ref), channel_id=1, source_target_pairs={{0,2},{2,0},{1,3},{3,1},{4,6},{6,4},{5,7},{7,5},{8,10},{10,8},{9,1... | collective-permute-start | bytes 159752 | tf_op jit(solution)/shard_map/ppermute | solution.py:530
  29.2 0.2 collective-permute-done.7.refs_0_
  29.5 1.8 %collective-permute-done.8.refs_1_ = bf16[192,128]{1,0:T(8,128)(2,1)S(1)} collective-permute-done((bf16[192,128]{1,0:T(8,128)(2,1)S(1)}, bf16[192,128]{1,0:T(8,128)(2,1)S(1)}, u32[]{:S(2)}, u32[]{:S(2)}) %collective-permute-start.8) | collective-permute-done | bytes 49184 | tf_op jit(solution)/shard_map/ppermute | solution.py:383
  31.2 0.4 %collective-permute-done.9.refs_2_ = bf16[192,128]{1,0:T(8,128)(2,1)S(1)} collective-permute-done((bf16[192,128]{1,0:T(8,128)(2,1)S(1)}, bf16[192,128]{1,0:T(8,128)(2,1)S(1)}, u32[]{:S(2)}, u32[]{:S(2)}) %collective-permute-start.9) | collective-permute-done | bytes 49184 | tf_op jit(solution)/shard_map/ppermute | solution.py:383
  31.7 1.2 %collective-permute-start.10 = (bf16[192,128]{1,0:T(8,128)(2,1)S(1)}, bf16[192,128]{1,0:T(8,128)(2,1)S(1)}, u32[]{:S(2)}, u32[]{:S(2)}) collective-permute-start(bf16[192,128]{1,0:T(8,128)(2,1)S(1)} %shard_map.101.a_ref), channel_id=1, source_target_pairs={{0,2},{2,0},{1,3},{3,1},{4,6},{6,4},{5,7},{7,5},{8,10},{10,8},{9,1... | collective-permute-start | bytes 147464 | tf_op jit(solution)/shard_map/ppermute | solution.py:535
  32.9 0.0 collective-permute-done.15.low_ref
  32.9 0.0 copy-done
  32.9 1.4 %shard_map.105 = bf16[2,512,256]{2,1,0:T(8,128)(2,1)} custom-call(s32[1]{0:T(128)} %bitcast.8.core_ref, s32[1]{0:T(128)} %bitcast.space_ref, bf16[256,256]{1,0:T(8,128)(2,1)S(1)} %get-tuple-element.58.pre_grad_ref.mine_ref, bf16[256,256]{1,0:T(8,128)(2,1)S(1)} %collective-permute-done.5.beside_ref, bf16[128,256]{1,0:T(8,128)(2,1)S(1)} %collective-permute-done.15.low_ref, ...), custom_call_target="tpu_custom_call" | custom-call | flops 301989888 | bytes 4194304 | tf_op jit(solution)/shard_map/pallas_call | solution.py:46
  34.3 1.6 %collective-permute-done.10.a_far_ref = bf16[192,128]{1,0:T(8,128)(2,1)S(1)} collective-permute-done((bf16[192,128]{1,0:T(8,128)(2,1)S(1)}, bf16[192,128]{1,0:T(8,128)(2,1)S(1)}, u32[]{:S(2)}, u32[]{:S(2)}) %collective-permute-start.10) | collective-permute-done | bytes 49184 | tf_op jit(solution)/shard_map/ppermute | solution.py:535
  35.9 0.0 collective-permute-done.16.b_far_ref
  35.9 0.8 %shard_map.106 = (f32[9,32,256]{2,1,0:T(8,128)}, f32[32,32]{1,0:T(8,128)}, f32[1,32]{1,0:T(1,128)}) custom-call(s32[1]{0:T(128)} %bitcast.1.time_ref, bf16[192,128]{1,0:T(8,128)(2,1)S(1)} %shard_map.101.a_ref, bf16[192,128]{1,0:T(8,128)(2,1)S(1)} %collective-permute-done.10.a_far_ref, bf16[104,256]{1,0:T(8,128)(2,1)S(1)} %get-tuple-element.76.b_ref, ...), custom_call_target="tpu_custom_call" | custom-call | flops 51200 | bytes 1048576 | tf_op jit(solution)/shard_map/pallas_call | solution.py:46
  (3 shorter events, 0.1 us)
Async XLA Ops:
  0.6 1.6 %collective-permute-start = (bf16[8,16,32]{2,1,0:T(8,128)(2,1)}, bf16[8,16,32]{2,1,0:T(8,128)(2,1)S(1)}, u32[]{:S(2)}, u32[]{:S(2)}) collective-permute-start(bf16[8,16,32]{2,1,0:T(8,128)(2,1)} %bitcast.23), channel_id=1, source_target_pairs={{0,1},{1,0},{2,3},{3,2},{4,5},{5,4},{6,7},{7,6},{8,9},{9,8},{10,11... | collective-permute-start | bytes 24584 | tf_op jit(solution)/shard_map/ppermute | solution.py:388
  2.3 7.2 %collective-permute-start.1 = (bf16[2,512,256]{2,1,0:T(8,128)(2,1)}, bf16[2,512,256]{2,1,0:T(8,128)(2,1)S(1)}, u32[]{:S(2)}, u32[]{:S(2)}) collective-permute-start(bf16[2,512,256]{2,1,0:T(8,128)(2,1)} %bitcast.19), channel_id=1, source_target_pairs={{0,1},{1,0},{2,3},{3,2},{4,5},{5,4},{6,7},{7,6},{8,9},{9,8},{10,11... | collective-permute-start | bytes 1572872 | tf_op jit(solution)/shard_map/ppermute | solution.py:439
  2.7 8.4 %collective-permute-start.2 = (bf16[16,128]{1,0:T(8,128)(2,1)S(1)}, bf16[16,128]{1,0:T(8,128)(2,1)S(1)}, u32[]{:S(2)}, u32[]{:S(2)}) collective-permute-start(bf16[16,128]{1,0:T(8,128)(2,1)S(1)} %get-tuple-element.48), channel_id=1, source_target_pairs={{0,4},{1,9},{4,8},{5,13},{8,12},{9,1},{12,0},{13,5},{2,6},{3,11},{... | collective-permute-start | bytes 12296 | tf_op jit(solution)/shard_map/ppermute | solution.py:412
  5.4 6.0 %collective-permute-start.3 = (bf16[528,256]{1,0:T(8,128)(2,1)S(1)}, bf16[528,256]{1,0:T(8,128)(2,1)S(1)}, u32[]{:S(2)}, u32[]{:S(2)}) collective-permute-start(bf16[528,256]{1,0:T(8,128)(2,1)S(1)} %get-tuple-element.49), channel_id=1, source_target_pairs={{0,13},{1,0},{4,1},{5,4},{8,5},{9,8},{12,9},{13,12},{2,15},{3,2},{... | collective-permute-start | bytes 811016 | tf_op jit(solution)/shard_map/ppermute | solution.py:410
  11.8 1.8 %collective-permute-start.4 = (bf16[32,128]{1,0:T(8,128)(2,1)S(1)}, bf16[32,128]{1,0:T(8,128)(2,1)S(1)}, u32[]{:S(2)}, u32[]{:S(2)}) collective-permute-start(bf16[32,128]{1,0:T(8,128)(2,1)S(1)} %get-tuple-element.57.tiles_ref), channel_id=1, source_target_pairs={{0,1},{1,0},{2,3},{3,2},{4,5},{5,4},{6,7},{7,6},{8,9},{9,8},{10,11... | collective-permute-start | bytes 24584 | tf_op jit(solution)/shard_map/ppermute | solution.py:469
  14.1 1.4 %collective-permute-start.5 = (bf16[256,256]{1,0:T(8,128)(2,1)S(1)}, bf16[256,256]{1,0:T(8,128)(2,1)S(1)}, u32[]{:S(2)}, u32[]{:S(2)}) collective-permute-start(bf16[256,256]{1,0:T(8,128)(2,1)S(1)} %get-tuple-element.58.pre_grad_ref.mine_ref), channel_id=1, source_target_pairs={{0,1},{1,0},{2,3},{3,2},{4,5},{5,4},{6,7},{7,6},{8,9},{9,8},{10,11... | collective-permute-start | bytes 393224 | tf_op jit(solution)/shard_map/ppermute | solution.py:478
  14.9 2.6 %collective-permute-start.11 = (bf16[4,104,256]{2,1,0:T(8,128)(2,1)S(1)}, bf16[4,104,256]{2,1,0:T(8,128)(2,1)S(1)}, u32[]{:S(2)}, u32[]{:S(2)}) collective-permute-start(bf16[4,104,256]{2,1,0:T(8,128)(2,1)S(1)} %get-tuple-element.68), channel_id=1, source_target_pairs={{0,1},{1,0},{2,3},{3,2},{4,5},{5,4},{6,7},{7,6},{8,9},{9,8},{10,11... | collective-permute-start | bytes 638984 | tf_op jit(solution)/shard_map/ppermute | solution.py:490
  15.9 17.0 %copy-start = (bf16[3,3,256,256]{3,2,1,0:T(8,128)(2,1)S(1)}, bf16[3,3,256,256]{3,2,1,0:T(8,128)(2,1)}, u32[]{:S(2)}) copy-start(bf16[3,3,256,256]{3,2,1,0:T(8,128)(2,1)} %param.7) | copy-start | bytes 3538948
  15.9 7.2 %collective-permute-start.6 = (bf16[4,192,128]{2,1,0:T(8,128)(2,1)S(1)}, bf16[4,192,128]{2,1,0:T(8,128)(2,1)S(1)}, u32[]{:S(2)}, u32[]{:S(2)}) collective-permute-start(bf16[4,192,128]{2,1,0:T(8,128)(2,1)S(1)} %get-tuple-element.60), channel_id=1, source_target_pairs={{0,2},{2,0},{1,3},{3,1},{4,6},{6,4},{5,7},{7,5},{8,10},{10,8},{9,1... | collective-permute-start | bytes 589832 | tf_op jit(solution)/shard_map/ppermute | solution.py:499
  17.5 11.0 %collective-permute-start.12 = (bf16[232,256]{1,0:T(8,128)(2,1)S(1)}, bf16[232,256]{1,0:T(8,128)(2,1)S(1)}, u32[]{:S(2)}, u32[]{:S(2)}) collective-permute-start(bf16[232,256]{1,0:T(8,128)(2,1)S(1)} %get-tuple-element.70), channel_id=1, source_target_pairs={{0,4},{4,8},{8,12},{12,0},{1,5},{5,9},{9,13},{13,1},{2,6},{6,10},{... | collective-permute-start | bytes 356360 | tf_op jit(solution)/shard_map/ppermute | solution.py:383
  19.1 7.8 %collective-permute-start.13 = (bf16[104,256]{1,0:T(8,128)(2,1)S(1)}, bf16[104,256]{1,0:T(8,128)(2,1)S(1)}, u32[]{:S(2)}, u32[]{:S(2)}) collective-permute-start(bf16[104,256]{1,0:T(8,128)(2,1)S(1)} %get-tuple-element.71), channel_id=1, source_target_pairs={{0,8},{4,12},{8,0},{12,4},{1,9},{5,13},{9,1},{13,5},{2,10},{6,14},... | collective-permute-start | bytes 159752 | tf_op jit(solution)/shard_map/ppermute | solution.py:383
  21.3 7.2 %collective-permute-start.14 = (bf16[104,256]{1,0:T(8,128)(2,1)S(1)}, bf16[104,256]{1,0:T(8,128)(2,1)S(1)}, u32[]{:S(2)}, u32[]{:S(2)}) collective-permute-start(bf16[104,256]{1,0:T(8,128)(2,1)S(1)} %get-tuple-element.72), channel_id=1, source_target_pairs={{0,12},{4,0},{8,4},{12,8},{1,13},{5,1},{9,5},{13,9},{2,14},{6,2},{... | collective-permute-start | bytes 159752 | tf_op jit(solution)/shard_map/ppermute | solution.py:383
  23.2 6.3 %collective-permute-start.7 = (bf16[192,128]{1,0:T(8,128)(2,1)S(1)}, bf16[192,128]{1,0:T(8,128)(2,1)S(1)}, u32[]{:S(2)}, u32[]{:S(2)}) collective-permute-start(bf16[192,128]{1,0:T(8,128)(2,1)S(1)} %get-tuple-element.62), channel_id=1, source_target_pairs={{0,4},{4,8},{8,12},{12,0},{1,5},{5,9},{9,13},{13,1},{2,6},{6,10},{... | collective-permute-start | bytes 147464 | tf_op jit(solution)/shard_map/ppermute | solution.py:383
  24.8 6.5 %collective-permute-start.8 = (bf16[192,128]{1,0:T(8,128)(2,1)S(1)}, bf16[192,128]{1,0:T(8,128)(2,1)S(1)}, u32[]{:S(2)}, u32[]{:S(2)}) collective-permute-start(bf16[192,128]{1,0:T(8,128)(2,1)S(1)} %get-tuple-element.63), channel_id=1, source_target_pairs={{0,8},{4,12},{8,0},{12,4},{1,9},{5,13},{9,1},{13,5},{2,10},{6,14},... | collective-permute-start | bytes 147464 | tf_op jit(solution)/shard_map/ppermute | solution.py:383
  26.9 4.7 %collective-permute-start.9 = (bf16[192,128]{1,0:T(8,128)(2,1)S(1)}, bf16[192,128]{1,0:T(8,128)(2,1)S(1)}, u32[]{:S(2)}, u32[]{:S(2)}) collective-permute-start(bf16[192,128]{1,0:T(8,128)(2,1)S(1)} %get-tuple-element.64), channel_id=1, source_target_pairs={{0,12},{4,0},{8,4},{12,8},{1,13},{5,1},{9,5},{13,9},{2,14},{6,2},{... | collective-permute-start | bytes 147464 | tf_op jit(solution)/shard_map/ppermute | solution.py:383
  28.5 4.3 %collective-permute-start.15 = (bf16[128,256]{1,0:T(8,128)(2,1)S(1)}, bf16[128,256]{1,0:T(8,128)(2,1)S(1)}, u32[]{:S(2)}, u32[]{:S(2)}) collective-permute-start(bf16[128,256]{1,0:T(8,128)(2,1)S(1)} %get-tuple-element.73.high_ref), channel_id=1, source_target_pairs={{0,1},{1,0},{2,3},{3,2},{4,5},{5,4},{6,7},{7,6},{8,9},{9,8},{10,11... | collective-permute-start | bytes 196616 | tf_op jit(solution)/shard_map/ppermute | solution.py:531
  28.6 7.2 %collective-permute-start.16 = (bf16[104,256]{1,0:T(8,128)(2,1)S(1)}, bf16[104,256]{1,0:T(8,128)(2,1)S(1)}, u32[]{:S(2)}, u32[]{:S(2)}) collective-permute-start(bf16[104,256]{1,0:T(8,128)(2,1)S(1)} %get-tuple-element.76.b_ref), channel_id=1, source_target_pairs={{0,2},{2,0},{1,3},{3,1},{4,6},{6,4},{5,7},{7,5},{8,10},{10,8},{9,1... | collective-permute-start | bytes 159752 | tf_op jit(solution)/shard_map/ppermute | solution.py:530
  31.7 4.2 %collective-permute-start.10 = (bf16[192,128]{1,0:T(8,128)(2,1)S(1)}, bf16[192,128]{1,0:T(8,128)(2,1)S(1)}, u32[]{:S(2)}, u32[]{:S(2)}) collective-permute-start(bf16[192,128]{1,0:T(8,128)(2,1)S(1)} %shard_map.101.a_ref), channel_id=1, source_target_pairs={{0,2},{2,0},{1,3},{3,1},{4,6},{6,4},{5,7},{7,5},{8,10},{10,8},{9,1... | collective-permute-start | bytes 147464 | tf_op jit(solution)/shard_map/ppermute | solution.py:535

commit v5 on v4

--- a/solution.py
+++ b/solution.py
@@ -49,20 +49,23 @@
 
 
 def start_kernel(act_ref, tiles_in, row_ref, tiles_ref, sems):
-    copies = [
-        pltpu.make_async_copy(tiles_in, tiles_ref, sems.at[0]),
-        pltpu.make_async_copy(act_ref.at[0], row_ref, sems.at[1]),
-    ]
+    copies = [pltpu.make_async_copy(tiles_in, tiles_ref, sems.at[0])]
+    pieces = sems.shape[0] - 1
+    length = row_ref.shape[0] // pieces
+    for i in range(pieces):
+        here = pl.ds(i * length, length)
+        copies.append(
+            pltpu.make_async_copy(act_ref.at[0, here], row_ref.at[here], sems.at[1 + i])
+        )
     for copy in copies:
         copy.start()
     for copy in copies:
         copy.wait()
 
 
-def tiles_kernel(core_ref, space_ref, row_ref, own_ref, got_ref, here_ref, far_ref, down_ref):
+def tiles_kernel(core_ref, space_ref, own_ref, got_ref, here_ref, far_ref, before_ref):
     spaces = own_ref.shape[0] // 2
     height, width = own_ref.shape[1:]
-    cols = row_ref.shape[0]
     core, chip = core_ref[0], space_ref[0]
     first = core == 0
 
@@ -70,18 +73,18 @@
         mine, other = own_ref[at], got_ref[at]
         return [jnp.where(first, mine, other), jnp.where(first, other, mine)]
 
-    def put(ref, top, pieces):
-        used = width * len(pieces)
-        if used < ref.shape[1]:
-            pieces = [*pieces, jnp.zeros((height, ref.shape[1] - used), bf16)]
-        ref[top:, :] = jnp.concatenate(pieces, 1)
-
-    put(here_ref, 0, side_by_side(2 * chip + core))
+    rest = [jnp.zeros((height, here_ref.shape[1] - 2 * width), bf16)]
+    here_ref[...] = jnp.concatenate(side_by_side(2 * chip + core) + rest, 1)
     there = 2 * lax.rem(chip + 1 + core, spaces)
-    put(far_ref, 0, side_by_side(there) + side_by_side(there + 1))
-    down_ref[:cols, :] = row_ref[...]
+    far_ref[...] = jnp.concatenate(side_by_side(there) + side_by_side(there + 1), 1)
     there = 2 * lax.rem(chip + spaces - 1, spaces)
-    put(down_ref, cols, side_by_side(there) + side_by_side(there + 1))
+    before_ref[...] = jnp.concatenate(side_by_side(there) + side_by_side(there + 1), 1)
+
+
+def join_kernel(far_ref, next_ref, out_ref):
+    height = far_ref.shape[0]
+    out_ref[:height, :] = far_ref[...]
+    out_ref[height:, :] = next_ref[...]
 
 
 def split_columns(row, source, stage):
@@ -102,8 +105,8 @@
 
 
 def early_kernel(
-    act_ref, w_in, bias_in, head_in, noise_in, here_ref,
-    pre_act_ref, w_ref, act, bias, head, noise, stage, sems,
+    act_ref, w_in, bias_in, head_in, noise_in, here_ref, before_ref,
+    pre_act_ref, w_ref, later_ref, act, bias, head, noise, stage, sems,
 ):
     pairs = [
         (act_ref.at[0], act.at[0]), (w_in.at[:3], w_ref.at[:3]),
@@ -113,6 +116,7 @@
     copies = [pltpu.make_async_copy(a, b, sems.at[i]) for i, (a, b) in enumerate(pairs)]
     for copy in copies:
         copy.start()
+    later_ref[...] = before_ref[...]
     copies[4].wait()
     cols = noise.shape[1]
     width = head.shape[1]
@@ -153,17 +157,13 @@
 
 
 def conv_kernel(
-    chips, core_ref, space_ref, early_ref, w_ref, far_ref, above_ref,
-    pre_act_ref, windows_ref, hidden_ref, tiles_ref, stage,
+    chips, core_ref, space_ref, early_ref, w_ref, above_ref,
+    pre_act_ref, windows_ref, hidden_ref, stage,
 ):
     cols = hidden_ref.shape[0]
-    height = far_ref.shape[0]
-    lanes = far_ref.shape[1]
     last = (core_ref[0] == 1) & (space_ref[0] == chips - 1)
-    row = above_ref[: 2 * cols, :]
+    row = above_ref[...]
     windows = split_columns(0, jnp.where(last, jnp.zeros_like(row), row), stage)
-    tiles_ref[:height, :] = far_ref[...]
-    tiles_ref[height:, :] = above_ref[2 * cols :, :lanes]
     pre_act = early_ref[:cols, :]
     for tap in range(3):
         windows_ref[tap] = windows[tap]
@@ -188,7 +188,7 @@
     for there, both in (
         (spaces - 1, jnp.where(first, mine[:latent], other[:latent])),
         (spaces - 2, jnp.where(first, other[:latent], mine[:latent])),
-        (1, jnp.where(first, other[latent:], mine[latent:])),
+        (1, jnp.where(first, mine[latent:], other[latent:])),
     ):
         band = jnp.where(first, both[:, :lanes], both[:, lanes:])
         tiles_at[lax.rem(chip + there, spaces)] = band
@@ -389,33 +389,25 @@
     row, own_tiles = full_call(
         start_kernel,
         (array((double_cols, channels), bf16), array(tiles.shape, bf16)),
-        [pltpu.SemaphoreType.DMA((2,))],
+        [pltpu.SemaphoreType.DMA((9,))],
         0,
         1 << 19,
         "hh",
     )(activations[0], tiles)
-    here, far, lower = full_call(
-        tiles_kernel,
-        (
-            array((tile[0], LANES), bf16),
-            array((tile[0], LANES), bf16),
-            array((double_cols + tile[0], channels), bf16),
-        ),
-        [],
-        0,
-        1 << 18,
-        "ssvvv",
-    )(core_at, space_at, row, own_tiles, got_tiles)
-    late_rows, lower = lax.optimization_barrier((activations[0], lower))
-    above = lax.ppermute(lower, line, [(i, (i - 1) % peers) for i in range(peers)])
+    here, far, before = full_call(
+        tiles_kernel, (array((tile[0], LANES), bf16),) * 3, [], 0, 1 << 16, "ssvv"
+    )(core_at, space_at, own_tiles, got_tiles)
+    late_rows, row, far = lax.optimization_barrier((activations[0], row, far))
+    above = lax.ppermute(row, line, [(i, (i - 1) % peers) for i in range(peers)])
     hops = [(2 * i + c, 2 * ((i + 1 + c) % spaces) + c) for i in range(spaces) for c in range(2)]
     far = lax.ppermute(far, line, hops)
     square = 2 * cols * channels * channels
-    early, w_here = full_call(
+    early, w_here, before = full_call(
         early_kernel,
         (
             array((cols + 4 * latent_dim, channels), f32),
             array(taps.shape, bf16),
+            array((tile[0], LANES), bf16),
         ),
         [
             pltpu.VMEM((2, double_cols, channels), bf16),
@@ -427,7 +419,7 @@
         ],
         120 * square,
         5 << 20,
-        "hhhhhv",
+        "hhhhhvv",
     )(
         activations[0],
         taps,
@@ -435,7 +427,10 @@
         head_weight.T,
         jnp.transpose(noise_sample[0, 0]),
         here,
+        before,
     )
+    back = [(2 * i + 1, 2 * ((i - 1) % spaces)) for i in range(spaces)]
+    after = lax.ppermute(before, line, back + [(2 * i, 2 * i + 1) for i in range(spaces)])
     beside = lax.ppermute(late_rows, "col", swap)
     chip_windows = full_call(
         functools.partial(select_kernel, spaces),
@@ -449,24 +444,27 @@
         2 << 20,
         "shv",
     )(core_at, activations[0], beside)
-    early, chip_windows, far, above = lax.optimization_barrier((early, chip_windows, far, above))
+    early, chip_windows, far, after = lax.optimization_barrier((early, chip_windows, far, after))
+    came = full_call(
+        join_kernel, array((2 * tile[0], LANES), bf16), [], 0, 1 << 14, "vv"
+    )(far, after)
+    other_came = lax.ppermute(came, "col", swap)
+    above, came = lax.optimization_barrier((above, came))
     rows_a = HALVED * share
     rows_b = (9 - HALVED) * share + TAIL
     half = channels // 2
-    pre_act, last_windows, hidden, came = full_call(
+    pre_act, last_windows, hidden = full_call(
         functools.partial(conv_kernel, spaces),
         (
             array((cols, channels), f32),
             array((3, cols, channels), bf16),
             array((cols, channels), bf16),
-            array((2 * tile[0], LANES), bf16),
         ),
         [pltpu.VMEM((channels // LANES, double_cols + 8, LANES), f32)],
         3 * square,
         2 << 20,
-        "ssvvvv",
-    )(core_at, space_at, early, w_here, far, above)
-    other_came = lax.ppermute(came, "col", swap)
+        "ssvvv",
+    )(core_at, space_at, early, w_here, above)
     pre_grad, moment_grad = full_call(
         grad_kernel,
         (array((cols, channels), bf16), array((2 * latent_dim, cols), bf16)),

time: 36.8 us -> 36.6 us (level)
  starting transfers between devices: 20.1 us -> 19.1 us
  waiting for transfers between devices: 7.16 us -> 7.94 us
    ppermute x1 -> x2, waiting for transfers between devices: 0.32 us -> 1.38 us  [the longest x1 1.38 us: body(): lax.ppermute(before, line, back + [(2 * i, 2 * i + 1) for i in range(spac...]
    ppermute x1, starting transfers between devices: 1.02 us -> 0.01 us  [body(): other_came = lax.ppermute(came, 'col', swap)]
    ppermute x1, waiting for transfers between devices: 1.53 us -> 0.75 us  [body(): crossed_a = lax.ppermute(cross_a, 'tm', swap)]
    ppermute x1, waiting for transfers between devices: 1.57 us -> 2 us  [body(): other_a = lax.ppermute(sum_a, 'tm', swap)]
    ppermute x1, starting transfers between devices: 1.16 us -> 0.72 us  [body(): other_a = lax.ppermute(sum_a, 'tm', swap)]
    ppermute x6, starting transfers between devices: 9.39 us -> 9.78 us  [over_space(): lax.ppermute(pieces[k], 'space', [(i, (i + k) % spaces) for i in range(sp...]
    ppermute x1 -> x2, starting transfers between devices: 2.03 us -> 2.09 us  [the longest x1 2.03 us: body(): lax.ppermute(row, line, [(i, (i - 1) % peers) for i in range(peers)])]
    pallas_call x14 -> x15, Pallas kernels: 8.6 us -> 8.59 us  [placed(): return call(*pinned)]
  transfers between devices with their start and end apart: 17 -> 18, of which waited for: 9 -> 9; matrix products, arithmetic and copies ran while one was open for 0% -> 0% of each run, Pallas kernels for 19% -> 20%
where the time goes in v5:
time: 36.6 us; the launch traced here: 36.4 us
  starting transfers between devices  19.1 us (52%)
  Pallas kernels  8.59 us (23%)
  waiting for transfers between devices  7.94 us (22%)
  between operations  0.76 us (2%)
    ppermute x6, starting transfers between devices, over_space(): lax.ppermute(pieces[k], 'space', [(i, (i + k) % spaces) for i in range(sp...  9.78 us
    pallas_call x15, Pallas kernels, placed(): return call(*pinned)  8.59 us
    ppermute x1, starting transfers between devices, body(): far = lax.ppermute(far, line, hops)  2.73 us
    ppermute x6, waiting for transfers between devices, over_space(): lax.ppermute(pieces[k], 'space', [(i, (i + k) % spaces) for i in range(sp...  2.5 us
    ppermute x1, starting transfers between devices, body(): lax.ppermute(row, line, [(i, (i - 1) % peers) for i in range(peers)])  2.03 us
    ppermute x1, waiting for transfers between devices, body(): other_a = lax.ppermute(sum_a, 'tm', swap)  2 us
    ppermute x1, starting transfers between devices, body(): crossed_a = lax.ppermute(cross_a, 'tm', swap)  1.55 us
    ppermute x1, waiting for transfers between devices, body(): lax.ppermute(before, line, back + [(2 * i, 2 * i + 1) for i in range(spac...  1.38 us
  transfers between devices with their start and end apart: 18, of which 9 were waited for; matrix products, arithmetic and copies ran while one was open for 0% of the time, Pallas kernels for 20%

profile of v5, /device:TPU:0, one launch (start us, length us, event | category | flops | bytes accessed | tf_op | source)
XLA Modules:
  0.0 36.4 jit_solution(13396654054519024031)
XLA Ops:
  0.6 0.5 %collective-permute-start = (bf16[8,16,32]{2,1,0:T(8,128)(2,1)}, bf16[8,16,32]{2,1,0:T(8,128)(2,1)S(1)}, u32[]{:S(2)}, u32[]{:S(2)}) collective-permute-start(bf16[8,16,32]{2,1,0:T(8,128)(2,1)} %bitcast.23), channel_id=1, source_target_pairs={{0,1},{1,0},{2,3},{3,2},{4,5},{5,4},{6,7},{7,6},{8,9},{9,8},{10,11... | collective-permute-start | bytes 24584 | tf_op jit(solution)/shard_map/ppermute | solution.py:388
  1.1 1.0 %shard_map.93 = (bf16[512,256]{1,0:T(8,128)(2,1)S(1)}, bf16[8,16,32]{2,1,0:T(8,128)(2,1)S(1)}) custom-call(bf16[2,512,256]{2,1,0:T(8,128)(2,1)} %bitcast.18, bf16[8,16,32]{2,1,0:T(8,128)(2,1)} %bitcast.24), custom_call_target="tpu_custom_call" | custom-call | bytes 524288 | tf_op jit(solution)/shard_map/pallas_call | solution.py:46
  2.1 0.1 collective-permute-done.got_ref
  2.2 0.1 shard_map.94
  2.3 0.4 %collective-permute-start.1 = (bf16[2,512,256]{2,1,0:T(8,128)(2,1)}, bf16[2,512,256]{2,1,0:T(8,128)(2,1)S(1)}, u32[]{:S(2)}, u32[]{:S(2)}) collective-permute-start(bf16[2,512,256]{2,1,0:T(8,128)(2,1)} %bitcast.19), channel_id=1, source_target_pairs={{0,1},{1,0},{2,3},{3,2},{4,5},{5,4},{6,7},{7,6},{8,9},{9,8},{10,11... | collective-permute-start | bytes 1572872 | tf_op jit(solution)/shard_map/ppermute | solution.py:434
  2.7 2.7 %collective-permute-start.2 = (bf16[16,128]{1,0:T(8,128)(2,1)S(1)}, bf16[16,128]{1,0:T(8,128)(2,1)S(1)}, u32[]{:S(2)}, u32[]{:S(2)}) collective-permute-start(bf16[16,128]{1,0:T(8,128)(2,1)S(1)} %get-tuple-element.52), channel_id=1, source_target_pairs={{0,4},{1,9},{4,8},{5,13},{8,12},{9,1},{12,0},{13,5},{2,6},{3,11},{... | collective-permute-start | bytes 12296 | tf_op jit(solution)/shard_map/ppermute | solution.py:403
  5.4 2.0 %collective-permute-start.4 = (bf16[512,256]{1,0:T(8,128)(2,1)S(1)}, bf16[512,256]{1,0:T(8,128)(2,1)S(1)}, u32[]{:S(2)}, u32[]{:S(2)}) collective-permute-start(bf16[512,256]{1,0:T(8,128)(2,1)S(1)} %get-tuple-element.57), channel_id=1, source_target_pairs={{0,13},{1,0},{4,1},{5,4},{8,5},{9,8},{12,9},{13,12},{2,15},{3,2},{... | collective-permute-start | bytes 786440 | tf_op jit(solution)/shard_map/ppermute | solution.py:401
  7.5 2.0 %shard_map.95 = (f32[320,256]{1,0:T(8,128)S(1)}, bf16[9,256,256]{2,1,0:T(8,128)(2,1)S(1)}, bf16[16,128]{1,0:T(8,128)(2,1)S(1)}) custom-call(bf16[2,512,256]{2,1,0:T(8,128)(2,1)} %bitcast.20, bf16[9,256,256]{2,1,0:T(8,128)(2,1)} %bitcast.16, f32[1,256]{1,0:T(1,128)} %bitcast.28, bf16[32,256]{1,0:T(8,128)(2,1)} %bitcast.26, bf16[16,256]{1,0:T(8,128)(2,1)} %bitcast.27, ...), custom_call_target="tpu_custom_call" | custom-call | flops 4026531840 | bytes 5242880 | tf_op jit(solution)/shard_map/pallas_call | solution.py:46
  9.5 0.1 collective-permute-start.3
  9.5 0.0 collective-permute-done.1.beside_ref
  9.6 1.6 %shard_map.96.windows_ref = bf16[6,512,128]{2,1,0:T(8,128)(2,1)S(1)} custom-call(s32[1]{0:T(128)} %bitcast.8.core_ref, bf16[2,512,256]{2,1,0:T(8,128)(2,1)} %bitcast.21, bf16[2,512,256]{2,1,0:T(8,128)(2,1)S(1)} %collective-permute-done.1.beside_ref), custom_call_target="tpu_custom_call" | custom-call | flops 134217728 | bytes 2097152 | tf_op jit(solution)/shard_map/pallas_call | solution.py:46
  11.2 0.0 collective-permute-done.2.far_ref
  11.2 1.4 %collective-permute-done.3.next_ref = bf16[16,128]{1,0:T(8,128)(2,1)S(1)} collective-permute-done((bf16[16,128]{1,0:T(8,128)(2,1)S(1)}, bf16[16,128]{1,0:T(8,128)(2,1)S(1)}, u32[]{:S(2)}, u32[]{:S(2)}) %collective-permute-start.3) | collective-permute-done | bytes 4128 | tf_op jit(solution)/shard_map/ppermute | solution.py:433
  12.6 0.0 collective-permute-start.5
  12.6 0.0 collective-permute-done.4.above_ref
  12.6 0.3 shard_map.98
  12.9 0.8 %collective-permute-done.5.other_tiles_ref = bf16[32,128]{1,0:T(8,128)(2,1)S(1)} collective-permute-done((bf16[32,128]{1,0:T(8,128)(2,1)S(1)}, bf16[32,128]{1,0:T(8,128)(2,1)S(1)}, u32[]{:S(2)}, u32[]{:S(2)}) %collective-permute-start.5) | collective-permute-done | bytes 8224 | tf_op jit(solution)/shard_map/ppermute | solution.py:451
  13.7 0.4 %shard_map.99 = (bf16[256,256]{1,0:T(8,128)(2,1)S(1)}, bf16[32,256]{1,0:T(8,128)(2,1)S(1)}) custom-call(s32[1]{0:T(128)} %bitcast.8.core_ref, s32[1]{0:T(128)} %bitcast.space_ref, f32[320,256]{1,0:T(8,128)S(1)} %get-tuple-element.55.early_ref, f32[256,256]{1,0:T(8,128)S(1)} %get-tuple-element.61.pre_act_ref, ...), custom_call_target="tpu_custom_call" | custom-call | flops 33554432 | bytes 1048576 | tf_op jit(solution)/shard_map/pallas_call | solution.py:46
  14.2 0.2 collective-permute-start.6
  14.4 0.4 %shard_map.103 = (f32[4,104,256]{2,1,0:T(8,128)S(1)}, bf16[4,104,256]{2,1,0:T(8,128)(2,1)S(1)}) custom-call(s32[1]{0:T(128)} %bitcast.8.core_ref, bf16[3,256,256]{2,1,0:T(8,128)(2,1)S(1)} %get-tuple-element.71.windows_ref, bf16[256,256]{1,0:T(8,128)(2,1)S(1)} %get-tuple-element.64.pre_grad_ref.mine_ref, bf16[256,256]{1,0:T(8,128)(2,1)S(1)} %get-tuple-element.62.hidden_ref, ...), custom_call_target="tpu_custom_call" | custom-call | flops 256 | bytes 256 | tf_op jit(solution)/shard_map/pallas_call | solution.py:46
  14.8 0.4 %collective-permute-start.12 = (bf16[4,104,256]{2,1,0:T(8,128)(2,1)S(1)}, bf16[4,104,256]{2,1,0:T(8,128)(2,1)S(1)}, u32[]{:S(2)}, u32[]{:S(2)}) collective-permute-start(bf16[4,104,256]{2,1,0:T(8,128)(2,1)S(1)} %get-tuple-element.74), channel_id=1, source_target_pairs={{0,1},{1,0},{2,3},{3,2},{4,5},{5,4},{6,7},{7,6},{8,9},{9,8},{10,11... | collective-permute-start | bytes 638984 | tf_op jit(solution)/shard_map/ppermute | solution.py:488
  15.2 0.4 collective-permute-done.6.beside_ref
  15.6 0.4 %shard_map.100 = (f32[4,192,128]{2,1,0:T(8,128)S(1)}, bf16[4,192,128]{2,1,0:T(8,128)(2,1)S(1)}) custom-call(s32[1]{0:T(128)} %bitcast.1.time_ref, bf16[6,512,128]{2,1,0:T(8,128)(2,1)S(1)} %shard_map.96.windows_ref, bf16[256,256]{1,0:T(8,128)(2,1)S(1)} %get-tuple-element.64.pre_grad_ref.mine_ref, bf16[256,256]{1,0:T(8,128)(2,1)S(1)} %collective-permute-done.6.beside_ref), custom_call_target="tpu_custom_call" | custom-call | flops 201326592 | bytes 2097152 | tf_op jit(solution)/shard_map/pallas_call | solution.py:46
  16.0 0.0 copy-start
  16.0 1.6 %collective-permute-start.7 = (bf16[4,192,128]{2,1,0:T(8,128)(2,1)S(1)}, bf16[4,192,128]{2,1,0:T(8,128)(2,1)S(1)}, u32[]{:S(2)}, u32[]{:S(2)}) collective-permute-start(bf16[4,192,128]{2,1,0:T(8,128)(2,1)S(1)} %get-tuple-element.66), channel_id=1, source_target_pairs={{0,2},{2,0},{1,3},{3,1},{4,6},{6,4},{5,7},{7,5},{8,10},{10,8},{9,1... | collective-permute-start | bytes 589832 | tf_op jit(solution)/shard_map/ppermute | solution.py:497
  17.6 0.0 collective-permute-done.12.got_ref
  17.6 0.1 shard_map.104
  17.6 0.8 %collective-permute-start.13 = (bf16[232,256]{1,0:T(8,128)(2,1)S(1)}, bf16[232,256]{1,0:T(8,128)(2,1)S(1)}, u32[]{:S(2)}, u32[]{:S(2)}) collective-permute-start(bf16[232,256]{1,0:T(8,128)(2,1)S(1)} %get-tuple-element.76), channel_id=1, source_target_pairs={{0,4},{4,8},{8,12},{12,0},{1,5},{5,9},{9,13},{13,1},{2,6},{6,10},{... | collective-permute-start | bytes 356360 | tf_op jit(solution)/shard_map/ppermute | solution.py:383
  18.5 2.1 %collective-permute-start.14 = (bf16[104,256]{1,0:T(8,128)(2,1)S(1)}, bf16[104,256]{1,0:T(8,128)(2,1)S(1)}, u32[]{:S(2)}, u32[]{:S(2)}) collective-permute-start(bf16[104,256]{1,0:T(8,128)(2,1)S(1)} %get-tuple-element.77), channel_id=1, source_target_pairs={{0,8},{4,12},{8,0},{12,4},{1,9},{5,13},{9,1},{13,5},{2,10},{6,14},... | collective-permute-start | bytes 159752 | tf_op jit(solution)/shard_map/ppermute | solution.py:383
  20.6 1.7 %collective-permute-start.15 = (bf16[104,256]{1,0:T(8,128)(2,1)S(1)}, bf16[104,256]{1,0:T(8,128)(2,1)S(1)}, u32[]{:S(2)}, u32[]{:S(2)}) collective-permute-start(bf16[104,256]{1,0:T(8,128)(2,1)S(1)} %get-tuple-element.78), channel_id=1, source_target_pairs={{0,12},{4,0},{8,4},{12,8},{1,13},{5,1},{9,5},{13,9},{2,14},{6,2},{... | collective-permute-start | bytes 159752 | tf_op jit(solution)/shard_map/ppermute | solution.py:383
  22.3 0.8 %collective-permute-done.7.got_ref = bf16[4,192,128]{2,1,0:T(8,128)(2,1)S(1)} collective-permute-done((bf16[4,192,128]{2,1,0:T(8,128)(2,1)S(1)}, bf16[4,192,128]{2,1,0:T(8,128)(2,1)S(1)}, u32[]{:S(2)}, u32[]{:S(2)}) %collective-permute-start.7) | collective-permute-done | bytes 196640 | tf_op jit(solution)/shard_map/ppermute | solution.py:497
  23.1 0.8 %collective-permute-start.8 = (bf16[192,128]{1,0:T(8,128)(2,1)S(1)}, bf16[192,128]{1,0:T(8,128)(2,1)S(1)}, u32[]{:S(2)}, u32[]{:S(2)}) collective-permute-start(bf16[192,128]{1,0:T(8,128)(2,1)S(1)} %get-tuple-element.68), channel_id=1, source_target_pairs={{0,4},{4,8},{8,12},{12,0},{1,5},{5,9},{9,13},{13,1},{2,6},{6,10},{... | collective-permute-start | bytes 147464 | tf_op jit(solution)/shard_map/ppermute | solution.py:383
  24.0 2.1 %collective-permute-start.9 = (bf16[192,128]{1,0:T(8,128)(2,1)S(1)}, bf16[192,128]{1,0:T(8,128)(2,1)S(1)}, u32[]{:S(2)}, u32[]{:S(2)}) collective-permute-start(bf16[192,128]{1,0:T(8,128)(2,1)S(1)} %get-tuple-element.69), channel_id=1, source_target_pairs={{0,8},{4,12},{8,0},{12,4},{1,9},{5,13},{9,1},{13,5},{2,10},{6,14},... | collective-permute-start | bytes 147464 | tf_op jit(solution)/shard_map/ppermute | solution.py:383
  26.0 0.9 %collective-permute-done.14.refs_1_ = bf16[104,256]{1,0:T(8,128)(2,1)S(1)} collective-permute-done((bf16[104,256]{1,0:T(8,128)(2,1)S(1)}, bf16[104,256]{1,0:T(8,128)(2,1)S(1)}, u32[]{:S(2)}, u32[]{:S(2)}) %collective-permute-start.14) | collective-permute-done | bytes 53280 | tf_op jit(solution)/shard_map/ppermute | solution.py:383
  27.0 2.2 %collective-permute-start.10 = (bf16[192,128]{1,0:T(8,128)(2,1)S(1)}, bf16[192,128]{1,0:T(8,128)(2,1)S(1)}, u32[]{:S(2)}, u32[]{:S(2)}) collective-permute-start(bf16[192,128]{1,0:T(8,128)(2,1)S(1)} %get-tuple-element.70), channel_id=1, source_target_pairs={{0,12},{4,0},{8,4},{12,8},{1,13},{5,1},{9,5},{13,9},{2,14},{6,2},{... | collective-permute-start | bytes 147464 | tf_op jit(solution)/shard_map/ppermute | solution.py:383
  29.2 0.0 collective-permute-done.15.refs_2_
  29.2 0.0 collective-permute-done.13.refs_0_
  29.2 0.1 collective-permute-start.16
  29.3 0.6 %collective-permute-start.17 = (bf16[104,256]{1,0:T(8,128)(2,1)S(1)}, bf16[104,256]{1,0:T(8,128)(2,1)S(1)}, u32[]{:S(2)}, u32[]{:S(2)}) collective-permute-start(bf16[104,256]{1,0:T(8,128)(2,1)S(1)} %get-tuple-element.82.b_ref), channel_id=1, source_target_pairs={{0,2},{2,0},{1,3},{3,1},{4,6},{6,4},{5,7},{7,5},{8,10},{10,8},{9,1... | collective-permute-start | bytes 159752 | tf_op jit(solution)/shard_map/ppermute | solution.py:528
  29.8 0.0 collective-permute-done.8.refs_0_
  29.8 1.5 %collective-permute-done.9.refs_1_ = bf16[192,128]{1,0:T(8,128)(2,1)S(1)} collective-permute-done((bf16[192,128]{1,0:T(8,128)(2,1)S(1)}, bf16[192,128]{1,0:T(8,128)(2,1)S(1)}, u32[]{:S(2)}, u32[]{:S(2)}) %collective-permute-start.9) | collective-permute-done | bytes 49184 | tf_op jit(solution)/shard_map/ppermute | solution.py:383
  31.3 0.1 collective-permute-done.10.refs_2_
  31.4 0.7 %collective-permute-start.11 = (bf16[192,128]{1,0:T(8,128)(2,1)S(1)}, bf16[192,128]{1,0:T(8,128)(2,1)S(1)}, u32[]{:S(2)}, u32[]{:S(2)}) collective-permute-start(bf16[192,128]{1,0:T(8,128)(2,1)S(1)} %shard_map.102.a_ref), channel_id=1, source_target_pairs={{0,2},{2,0},{1,3},{3,1},{4,6},{6,4},{5,7},{7,5},{8,10},{10,8},{9,1... | collective-permute-start | bytes 147464 | tf_op jit(solution)/shard_map/ppermute | solution.py:533
  32.2 0.0 collective-permute-done.16.low_ref
  32.2 0.0 copy-done
  32.2 1.4 %shard_map.106 = bf16[2,512,256]{2,1,0:T(8,128)(2,1)} custom-call(s32[1]{0:T(128)} %bitcast.8.core_ref, s32[1]{0:T(128)} %bitcast.space_ref, bf16[256,256]{1,0:T(8,128)(2,1)S(1)} %get-tuple-element.64.pre_grad_ref.mine_ref, bf16[256,256]{1,0:T(8,128)(2,1)S(1)} %collective-permute-done.6.beside_ref, bf16[128,256]{1,0:T(8,128)(2,1)S(1)} %collective-permute-done.16.low_ref, ...), custom_call_target="tpu_custom_call" | custom-call | flops 301989888 | bytes 4194304 | tf_op jit(solution)/shard_map/pallas_call | solution.py:46
  33.6 2.0 %collective-permute-done.11.a_far_ref = bf16[192,128]{1,0:T(8,128)(2,1)S(1)} collective-permute-done((bf16[192,128]{1,0:T(8,128)(2,1)S(1)}, bf16[192,128]{1,0:T(8,128)(2,1)S(1)}, u32[]{:S(2)}, u32[]{:S(2)}) %collective-permute-start.11) | collective-permute-done | bytes 49184 | tf_op jit(solution)/shard_map/ppermute | solution.py:533
  35.6 0.0 collective-permute-done.17.b_far_ref
  35.6 0.8 %shard_map.107 = (f32[9,32,256]{2,1,0:T(8,128)}, f32[32,32]{1,0:T(8,128)}, f32[1,32]{1,0:T(1,128)}) custom-call(s32[1]{0:T(128)} %bitcast.1.time_ref, bf16[192,128]{1,0:T(8,128)(2,1)S(1)} %shard_map.102.a_ref, bf16[192,128]{1,0:T(8,128)(2,1)S(1)} %collective-permute-done.11.a_far_ref, bf16[104,256]{1,0:T(8,128)(2,1)S(1)} %get-tuple-element.82.b_ref, ...), custom_call_target="tpu_custom_call" | custom-call | flops 51200 | bytes 1048576 | tf_op jit(solution)/shard_map/pallas_call | solution.py:46
  (4 shorter events, 0.1 us)
Async XLA Ops:
  0.6 1.6 %collective-permute-start = (bf16[8,16,32]{2,1,0:T(8,128)(2,1)}, bf16[8,16,32]{2,1,0:T(8,128)(2,1)S(1)}, u32[]{:S(2)}, u32[]{:S(2)}) collective-permute-start(bf16[8,16,32]{2,1,0:T(8,128)(2,1)} %bitcast.23), channel_id=1, source_target_pairs={{0,1},{1,0},{2,3},{3,2},{4,5},{5,4},{6,7},{7,6},{8,9},{9,8},{10,11... | collective-permute-start | bytes 24584 | tf_op jit(solution)/shard_map/ppermute | solution.py:388
  2.3 7.2 %collective-permute-start.1 = (bf16[2,512,256]{2,1,0:T(8,128)(2,1)}, bf16[2,512,256]{2,1,0:T(8,128)(2,1)S(1)}, u32[]{:S(2)}, u32[]{:S(2)}) collective-permute-start(bf16[2,512,256]{2,1,0:T(8,128)(2,1)} %bitcast.19), channel_id=1, source_target_pairs={{0,1},{1,0},{2,3},{3,2},{4,5},{5,4},{6,7},{7,6},{8,9},{9,8},{10,11... | collective-permute-start | bytes 1572872 | tf_op jit(solution)/shard_map/ppermute | solution.py:434
  2.7 8.5 %collective-permute-start.2 = (bf16[16,128]{1,0:T(8,128)(2,1)S(1)}, bf16[16,128]{1,0:T(8,128)(2,1)S(1)}, u32[]{:S(2)}, u32[]{:S(2)}) collective-permute-start(bf16[16,128]{1,0:T(8,128)(2,1)S(1)} %get-tuple-element.52), channel_id=1, source_target_pairs={{0,4},{1,9},{4,8},{5,13},{8,12},{9,1},{12,0},{13,5},{2,6},{3,11},{... | collective-permute-start | bytes 12296 | tf_op jit(solution)/shard_map/ppermute | solution.py:403
  5.4 7.2 %collective-permute-start.4 = (bf16[512,256]{1,0:T(8,128)(2,1)S(1)}, bf16[512,256]{1,0:T(8,128)(2,1)S(1)}, u32[]{:S(2)}, u32[]{:S(2)}) collective-permute-start(bf16[512,256]{1,0:T(8,128)(2,1)S(1)} %get-tuple-element.57), channel_id=1, source_target_pairs={{0,13},{1,0},{4,1},{5,4},{8,5},{9,8},{12,9},{13,12},{2,15},{3,2},{... | collective-permute-start | bytes 786440 | tf_op jit(solution)/shard_map/ppermute | solution.py:401
  9.5 3.1 %collective-permute-start.3 = (bf16[16,128]{1,0:T(8,128)(2,1)S(1)}, bf16[16,128]{1,0:T(8,128)(2,1)S(1)}, u32[]{:S(2)}, u32[]{:S(2)}) collective-permute-start(bf16[16,128]{1,0:T(8,128)(2,1)S(1)} %get-tuple-element.53), channel_id=1, source_target_pairs={{1,12},{5,0},{9,4},{13,8},{0,1},{4,5},{8,9},{12,13},{3,14},{7,2},{... | collective-permute-start | bytes 12296 | tf_op jit(solution)/shard_map/ppermute | solution.py:433
  12.6 1.2 %collective-permute-start.5 = (bf16[32,128]{1,0:T(8,128)(2,1)S(1)}, bf16[32,128]{1,0:T(8,128)(2,1)S(1)}, u32[]{:S(2)}, u32[]{:S(2)}) collective-permute-start(bf16[32,128]{1,0:T(8,128)(2,1)S(1)} %shard_map.97.tiles_ref), channel_id=1, source_target_pairs={{0,1},{1,0},{2,3},{3,2},{4,5},{5,4},{6,7},{7,6},{8,9},{9,8},{10,11... | collective-permute-start | bytes 24584 | tf_op jit(solution)/shard_map/ppermute | solution.py:451
  14.2 1.4 %collective-permute-start.6 = (bf16[256,256]{1,0:T(8,128)(2,1)S(1)}, bf16[256,256]{1,0:T(8,128)(2,1)S(1)}, u32[]{:S(2)}, u32[]{:S(2)}) collective-permute-start(bf16[256,256]{1,0:T(8,128)(2,1)S(1)} %get-tuple-element.64.pre_grad_ref.mine_ref), channel_id=1, source_target_pairs={{0,1},{1,0},{2,3},{3,2},{4,5},{5,4},{6,7},{7,6},{8,9},{9,8},{10,11... | collective-permute-start | bytes 393224 | tf_op jit(solution)/shard_map/ppermute | solution.py:476
  14.8 2.8 %collective-permute-start.12 = (bf16[4,104,256]{2,1,0:T(8,128)(2,1)S(1)}, bf16[4,104,256]{2,1,0:T(8,128)(2,1)S(1)}, u32[]{:S(2)}, u32[]{:S(2)}) collective-permute-start(bf16[4,104,256]{2,1,0:T(8,128)(2,1)S(1)} %get-tuple-element.74), channel_id=1, source_target_pairs={{0,1},{1,0},{2,3},{3,2},{4,5},{5,4},{6,7},{7,6},{8,9},{9,8},{10,11... | collective-permute-start | bytes 638984 | tf_op jit(solution)/shard_map/ppermute | solution.py:488
  16.0 16.2 %copy-start = (bf16[3,3,256,256]{3,2,1,0:T(8,128)(2,1)S(1)}, bf16[3,3,256,256]{3,2,1,0:T(8,128)(2,1)}, u32[]{:S(2)}) copy-start(bf16[3,3,256,256]{3,2,1,0:T(8,128)(2,1)} %param.7) | copy-start | bytes 3538948
  16.0 7.0 %collective-permute-start.7 = (bf16[4,192,128]{2,1,0:T(8,128)(2,1)S(1)}, bf16[4,192,128]{2,1,0:T(8,128)(2,1)S(1)}, u32[]{:S(2)}, u32[]{:S(2)}) collective-permute-start(bf16[4,192,128]{2,1,0:T(8,128)(2,1)S(1)} %get-tuple-element.66), channel_id=1, source_target_pairs={{0,2},{2,0},{1,3},{3,1},{4,6},{6,4},{5,7},{7,5},{8,10},{10,8},{9,1... | collective-permute-start | bytes 589832 | tf_op jit(solution)/shard_map/ppermute | solution.py:497
  17.6 11.5 %collective-permute-start.13 = (bf16[232,256]{1,0:T(8,128)(2,1)S(1)}, bf16[232,256]{1,0:T(8,128)(2,1)S(1)}, u32[]{:S(2)}, u32[]{:S(2)}) collective-permute-start(bf16[232,256]{1,0:T(8,128)(2,1)S(1)} %get-tuple-element.76), channel_id=1, source_target_pairs={{0,4},{4,8},{8,12},{12,0},{1,5},{5,9},{9,13},{13,1},{2,6},{6,10},{... | collective-permute-start | bytes 356360 | tf_op jit(solution)/shard_map/ppermute | solution.py:383
  18.5 8.5 %collective-permute-start.14 = (bf16[104,256]{1,0:T(8,128)(2,1)S(1)}, bf16[104,256]{1,0:T(8,128)(2,1)S(1)}, u32[]{:S(2)}, u32[]{:S(2)}) collective-permute-start(bf16[104,256]{1,0:T(8,128)(2,1)S(1)} %get-tuple-element.77), channel_id=1, source_target_pairs={{0,8},{4,12},{8,0},{12,4},{1,9},{5,13},{9,1},{13,5},{2,10},{6,14},... | collective-permute-start | bytes 159752 | tf_op jit(solution)/shard_map/ppermute | solution.py:383
  20.6 8.5 %collective-permute-start.15 = (bf16[104,256]{1,0:T(8,128)(2,1)S(1)}, bf16[104,256]{1,0:T(8,128)(2,1)S(1)}, u32[]{:S(2)}, u32[]{:S(2)}) collective-permute-start(bf16[104,256]{1,0:T(8,128)(2,1)S(1)} %get-tuple-element.78), channel_id=1, source_target_pairs={{0,12},{4,0},{8,4},{12,8},{1,13},{5,1},{9,5},{13,9},{2,14},{6,2},{... | collective-permute-start | bytes 159752 | tf_op jit(solution)/shard_map/ppermute | solution.py:383
  23.1 6.7 %collective-permute-start.8 = (bf16[192,128]{1,0:T(8,128)(2,1)S(1)}, bf16[192,128]{1,0:T(8,128)(2,1)S(1)}, u32[]{:S(2)}, u32[]{:S(2)}) collective-permute-start(bf16[192,128]{1,0:T(8,128)(2,1)S(1)} %get-tuple-element.68), channel_id=1, source_target_pairs={{0,4},{4,8},{8,12},{12,0},{1,5},{5,9},{9,13},{13,1},{2,6},{6,10},{... | collective-permute-start | bytes 147464 | tf_op jit(solution)/shard_map/ppermute | solution.py:383
  24.0 7.4 %collective-permute-start.9 = (bf16[192,128]{1,0:T(8,128)(2,1)S(1)}, bf16[192,128]{1,0:T(8,128)(2,1)S(1)}, u32[]{:S(2)}, u32[]{:S(2)}) collective-permute-start(bf16[192,128]{1,0:T(8,128)(2,1)S(1)} %get-tuple-element.69), channel_id=1, source_target_pairs={{0,8},{4,12},{8,0},{12,4},{1,9},{5,13},{9,1},{13,5},{2,10},{6,14},... | collective-permute-start | bytes 147464 | tf_op jit(solution)/shard_map/ppermute | solution.py:383
  27.0 4.5 %collective-permute-start.10 = (bf16[192,128]{1,0:T(8,128)(2,1)S(1)}, bf16[192,128]{1,0:T(8,128)(2,1)S(1)}, u32[]{:S(2)}, u32[]{:S(2)}) collective-permute-start(bf16[192,128]{1,0:T(8,128)(2,1)S(1)} %get-tuple-element.70), channel_id=1, source_target_pairs={{0,12},{4,0},{8,4},{12,8},{1,13},{5,1},{9,5},{13,9},{2,14},{6,2},{... | collective-permute-start | bytes 147464 | tf_op jit(solution)/shard_map/ppermute | solution.py:383
  29.2 3.0 %collective-permute-start.16 = (bf16[128,256]{1,0:T(8,128)(2,1)S(1)}, bf16[128,256]{1,0:T(8,128)(2,1)S(1)}, u32[]{:S(2)}, u32[]{:S(2)}) collective-permute-start(bf16[128,256]{1,0:T(8,128)(2,1)S(1)} %get-tuple-element.79.high_ref), channel_id=1, source_target_pairs={{0,1},{1,0},{2,3},{3,2},{4,5},{5,4},{6,7},{7,6},{8,9},{9,8},{10,11... | collective-permute-start | bytes 196616 | tf_op jit(solution)/shard_map/ppermute | solution.py:529
  29.3 6.3 %collective-permute-start.17 = (bf16[104,256]{1,0:T(8,128)(2,1)S(1)}, bf16[104,256]{1,0:T(8,128)(2,1)S(1)}, u32[]{:S(2)}, u32[]{:S(2)}) collective-permute-start(bf16[104,256]{1,0:T(8,128)(2,1)S(1)} %get-tuple-element.82.b_ref), channel_id=1, source_target_pairs={{0,2},{2,0},{1,3},{3,1},{4,6},{6,4},{5,7},{7,5},{8,10},{10,8},{9,1... | collective-permute-start | bytes 159752 | tf_op jit(solution)/shard_map/ppermute | solution.py:528
  31.4 4.2 %collective-permute-start.11 = (bf16[192,128]{1,0:T(8,128)(2,1)S(1)}, bf16[192,128]{1,0:T(8,128)(2,1)S(1)}, u32[]{:S(2)}, u32[]{:S(2)}) collective-permute-start(bf16[192,128]{1,0:T(8,128)(2,1)S(1)} %shard_map.102.a_ref), channel_id=1, source_target_pairs={{0,2},{2,0},{1,3},{3,1},{4,6},{6,4},{5,7},{7,5},{8,10},{10,8},{9,1... | collective-permute-start | bytes 147464 | tf_op jit(solution)/shard_map/ppermute | solution.py:533

commit v6 on v5

--- a/solution.py
+++ b/solution.py
@@ -104,41 +104,45 @@
     return windows
 
 
+def load_kernel(act_in, before_ref, act_ref, later_ref, sems):
+    rows = act_in.shape[0]
+    copies = [
+        pltpu.make_async_copy(act_in.at[i], act_ref.at[i], sems.at[i]) for i in range(rows)
+    ]
+    for copy in copies:
+        copy.start()
+    later_ref[...] = before_ref[...]
+    for copy in copies:
+        copy.wait()
+
+
 def early_kernel(
-    act_ref, w_in, bias_in, head_in, noise_in, here_ref, before_ref,
-    pre_act_ref, w_ref, later_ref, act, bias, head, noise, stage, sems,
+    bias_in, head_in, noise_in, w_in, act_ref, here_ref,
+    pre_act_ref, w_ref, bias, head, noise, stage, sems,
 ):
-    pairs = [
-        (act_ref.at[0], act.at[0]), (w_in.at[:3], w_ref.at[:3]),
-        (act_ref.at[1], act.at[1]), (w_in.at[3:6], w_ref.at[3:6]),
-        (bias_in, bias), (w_in.at[6:], w_ref.at[6:]), (head_in, head), (noise_in, noise),
-    ]
+    pairs = [(w_in.at[i : i + 3], w_ref.at[i : i + 3]) for i in (0, 3, 6)]
+    pairs += [(bias_in, bias), (head_in, head), (noise_in, noise)]
     copies = [pltpu.make_async_copy(a, b, sems.at[i]) for i, (a, b) in enumerate(pairs)]
     for copy in copies:
         copy.start()
-    later_ref[...] = before_ref[...]
-    copies[4].wait()
     cols = noise.shape[1]
-    width = head.shape[1]
-    pre_act = jnp.broadcast_to(bias[...], (cols, width))
+    pre_act = None
     for row in range(2):
-        copies[2 * row].wait()
-        windows = split_columns(row, act[row], stage)
-        copies[2 * row + 1].wait()
+        windows = split_columns(row, act_ref[row], stage)
+        copies[row].wait()
         for tap in range(3):
-            pre_act = pre_act + dot(windows[tap], w_ref[3 * row + tap], 1, 0)
-    pre_act_ref[:cols, :] = pre_act
-    for copy in copies[5:]:
+            term = dot(windows[tap], w_ref[3 * row + tap], 1, 0)
+            pre_act = term if pre_act is None else pre_act + term
+    for copy in copies[2:]:
         copy.wait()
+    pre_act_ref[:cols, :] = pre_act + bias[...]
     at = cols
     for ref in (head, noise, here_ref):
         pre_act_ref[at : at + ref.shape[0], : ref.shape[1]] = ref[...].astype(f32)
         at += ref.shape[0]
 
 
-def select_kernel(chips, core_ref, act_in, beside_ref, windows_ref, act, stage, sem):
-    copy = pltpu.make_async_copy(act_in, act, sem)
-    copy.start()
+def select_kernel(chips, core_ref, act_ref, beside_ref, windows_ref, stage):
     rows, length, width = beside_ref.shape
     kept = windows_ref.shape[2]
     share = kept // chips
@@ -146,10 +150,9 @@
     target = lax.broadcasted_iota(jnp.int32, (width, kept), 1)
     wanted = 2 * share * (target // share) + share * core_ref[0] + target % share
     select = jnp.where(source == wanted, 1.0, 0.0).astype(bf16)
-    copy.wait()
     cols = length // 2
     for row in range(rows):
-        for at, ref in enumerate((act, beside_ref)):
+        for at, ref in enumerate((act_ref, beside_ref)):
             picked = dot(ref[row], select, 1, 0)
             windows = split_columns(rows * at + row, picked, stage)
             for tap in range(3):
@@ -402,32 +405,37 @@
     hops = [(2 * i + c, 2 * ((i + 1 + c) % spaces) + c) for i in range(spaces) for c in range(2)]
     far = lax.ppermute(far, line, hops)
     square = 2 * cols * channels * channels
-    early, w_here, before = full_call(
-        early_kernel,
+    act_here, before = full_call(
+        load_kernel,
         (
-            array((cols + 4 * latent_dim, channels), f32),
-            array(taps.shape, bf16),
+            array((double_rows, double_cols, channels), bf16),
             array((tile[0], LANES), bf16),
         ),
+        [pltpu.SemaphoreType.DMA((double_rows,))],
+        60 * square,
+        2 << 20,
+        "hv",
+    )(activations[0], before)
+    early, w_here = full_call(
+        early_kernel,
+        (array((cols + 4 * latent_dim, channels), f32), array(taps.shape, bf16)),
         [
-            pltpu.VMEM((2, double_cols, channels), bf16),
             pltpu.VMEM((1, channels), f32),
             pltpu.VMEM((2 * latent_dim, channels), bf16),
             pltpu.VMEM((latent_dim, cols), bf16),
             pltpu.VMEM((2 * (channels // LANES), double_cols + 8, LANES), f32),
-            pltpu.SemaphoreType.DMA((8,)),
+            pltpu.SemaphoreType.DMA((6,)),
         ],
-        120 * square,
-        5 << 20,
-        "hhhhhvv",
+        60 * square,
+        3 << 20,
+        "hhhhvv",
     )(
-        activations[0],
-        taps,
         conv_bias.reshape(1, channels),
         head_weight.T,
         jnp.transpose(noise_sample[0, 0]),
+        taps,
+        act_here,
         here,
-        before,
     )
     back = [(2 * i + 1, 2 * ((i - 1) % spaces)) for i in range(spaces)]
     after = lax.ppermute(before, line, back + [(2 * i, 2 * i + 1) for i in range(spaces)])
@@ -435,15 +443,11 @@
     chip_windows = full_call(
         functools.partial(select_kernel, spaces),
         array((6, 2 * cols, channels // 2), bf16),
-        [
-            pltpu.VMEM((2, double_cols, channels), bf16),
-            pltpu.VMEM((4 * (channels // 2 // LANES), double_cols + 8, LANES), f32),
-            pltpu.SemaphoreType.DMA,
-        ],
+        [pltpu.VMEM((4 * (channels // 2 // LANES), double_cols + 8, LANES), f32)],
         4 * square,
         2 << 20,
-        "shv",
-    )(core_at, activations[0], beside)
+        "svv",
+    )(core_at, act_here, beside)
     early, chip_windows, far, after = lax.optimization_barrier((early, chip_windows, far, after))
     came = full_call(
         join_kernel, array((2 * tile[0], LANES), bf16), [], 0, 1 << 14, "vv"

time: 36.6 us -> 35.9 us (0.981)
  waiting for transfers between devices: 7.94 us -> 6.9 us
  starting transfers between devices: 19.1 us -> 19.6 us
    ppermute x1, waiting for transfers between devices: 1.38 us -> 0.65 us  [body(): lax.ppermute(before, line, back + [(2 * i, 2 * i + 1) for i in range(spac...]
    pallas_call x15 -> x16, Pallas kernels: 8.59 us -> 8.43 us  [placed(): return call(*pinned)]
where the time goes in v6:
time: 35.9 us; the launch traced here: 35.7 us
  starting transfers between devices  19.6 us (55%)
  Pallas kernels  8.43 us (23%)
  waiting for transfers between devices  6.9 us (19%)
  between operations  0.77 us (2%)
    ppermute x6, starting transfers between devices, over_space(): lax.ppermute(pieces[k], 'space', [(i, (i + k) % spaces) for i in range(sp...  10.1 us
    pallas_call x16, Pallas kernels, placed(): return call(*pinned)  8.43 us
    ppermute x1, starting transfers between devices, body(): far = lax.ppermute(far, line, hops)  2.73 us
    ppermute x6, waiting for transfers between devices, over_space(): lax.ppermute(pieces[k], 'space', [(i, (i + k) % spaces) for i in range(sp...  2.27 us
    ppermute x1, starting transfers between devices, body(): lax.ppermute(row, line, [(i, (i - 1) % peers) for i in range(peers)])  2.03 us
    ppermute x1, waiting for transfers between devices, body(): other_a = lax.ppermute(sum_a, 'tm', swap)  1.81 us
    ppermute x1, starting transfers between devices, body(): crossed_a = lax.ppermute(cross_a, 'tm', swap)  1.56 us
    ppermute x1, starting transfers between devices, body(): other_a = lax.ppermute(sum_a, 'tm', swap)  0.92 us
  transfers between devices with their start and end apart: 18, of which 9 were waited for; matrix products, arithmetic and copies ran while one was open for 0% of the time, Pallas kernels for 20%

profile of v6, /device:TPU:0, one launch (start us, length us, event | category | flops | bytes accessed | tf_op | source)
XLA Modules:
  0.0 35.7 jit_solution(11225223479771585809)
XLA Ops:
  0.6 0.5 %collective-permute-start = (bf16[8,16,32]{2,1,0:T(8,128)(2,1)}, bf16[8,16,32]{2,1,0:T(8,128)(2,1)S(1)}, u32[]{:S(2)}, u32[]{:S(2)}) collective-permute-start(bf16[8,16,32]{2,1,0:T(8,128)(2,1)} %bitcast.22), channel_id=1, source_target_pairs={{0,1},{1,0},{2,3},{3,2},{4,5},{5,4},{6,7},{7,6},{8,9},{9,8},{10,11... | collective-permute-start | bytes 24584 | tf_op jit(solution)/shard_map/ppermute | solution.py:391
  1.1 1.0 %shard_map.93 = (bf16[512,256]{1,0:T(8,128)(2,1)S(1)}, bf16[8,16,32]{2,1,0:T(8,128)(2,1)S(1)}) custom-call(bf16[2,512,256]{2,1,0:T(8,128)(2,1)} %bitcast.18, bf16[8,16,32]{2,1,0:T(8,128)(2,1)} %bitcast.23), custom_call_target="tpu_custom_call" | custom-call | bytes 524288 | tf_op jit(solution)/shard_map/pallas_call | solution.py:46
  2.1 0.1 collective-permute-done.got_ref
  2.2 0.1 shard_map.94
  2.3 0.4 %collective-permute-start.1 = (bf16[2,512,256]{2,1,0:T(8,128)(2,1)}, bf16[2,512,256]{2,1,0:T(8,128)(2,1)S(1)}, u32[]{:S(2)}, u32[]{:S(2)}) collective-permute-start(bf16[2,512,256]{2,1,0:T(8,128)(2,1)} %bitcast.19), channel_id=1, source_target_pairs={{0,1},{1,0},{2,3},{3,2},{4,5},{5,4},{6,7},{7,6},{8,9},{9,8},{10,11... | collective-permute-start | bytes 1572872 | tf_op jit(solution)/shard_map/ppermute | solution.py:442
  2.7 2.7 %collective-permute-start.2 = (bf16[16,128]{1,0:T(8,128)(2,1)S(1)}, bf16[16,128]{1,0:T(8,128)(2,1)S(1)}, u32[]{:S(2)}, u32[]{:S(2)}) collective-permute-start(bf16[16,128]{1,0:T(8,128)(2,1)S(1)} %get-tuple-element.54), channel_id=1, source_target_pairs={{0,4},{1,9},{4,8},{5,13},{8,12},{9,1},{12,0},{13,5},{2,6},{3,11},{... | collective-permute-start | bytes 12296 | tf_op jit(solution)/shard_map/ppermute | solution.py:406
  5.4 2.0 %collective-permute-start.4 = (bf16[512,256]{1,0:T(8,128)(2,1)S(1)}, bf16[512,256]{1,0:T(8,128)(2,1)S(1)}, u32[]{:S(2)}, u32[]{:S(2)}) collective-permute-start(bf16[512,256]{1,0:T(8,128)(2,1)S(1)} %get-tuple-element.59), channel_id=1, source_target_pairs={{0,13},{1,0},{4,1},{5,4},{8,5},{9,8},{12,9},{13,12},{2,15},{3,2},{... | collective-permute-start | bytes 786440 | tf_op jit(solution)/shard_map/ppermute | solution.py:404
  7.5 1.0 %shard_map.95 = (bf16[2,512,256]{2,1,0:T(8,128)(2,1)S(1)}, bf16[16,128]{1,0:T(8,128)(2,1)S(1)}) custom-call(bf16[2,512,256]{2,1,0:T(8,128)(2,1)} %bitcast.20, bf16[16,128]{1,0:T(8,128)(2,1)S(1)} %get-tuple-element.47.before_ref), custom_call_target="tpu_custom_call" | custom-call | flops 2013265920 | bytes 2097152 | tf_op jit(solution)/shard_map/pallas_call | solution.py:46
  8.5 0.1 collective-permute-start.3
  8.6 1.9 %shard_map.96 = (f32[320,256]{1,0:T(8,128)S(1)}, bf16[9,256,256]{2,1,0:T(8,128)(2,1)S(1)}) custom-call(f32[1,256]{1,0:T(1,128)} %bitcast.27, bf16[32,256]{1,0:T(8,128)(2,1)} %bitcast.25, bf16[16,256]{1,0:T(8,128)(2,1)} %bitcast.26, bf16[9,256,256]{2,1,0:T(8,128)(2,1)} %bitcast.16, bf16[2,512,256]{2,1,0:T(8,128)(2,1)S(1)} %get-tuple-element.48.act_ref, ...), custom_call_target="tpu_custom_call" | custom-call | flops 2013265920 | bytes 3145728 | tf_op jit(solution)/shard_map/pallas_call | solution.py:46
  10.5 0.0 collective-permute-done.1.beside_ref
  10.5 0.6 %shard_map.97.windows_ref = bf16[6,512,128]{2,1,0:T(8,128)(2,1)S(1)} custom-call(s32[1]{0:T(128)} %bitcast.8.core_ref, bf16[2,512,256]{2,1,0:T(8,128)(2,1)S(1)} %get-tuple-element.48.act_ref, bf16[2,512,256]{2,1,0:T(8,128)(2,1)S(1)} %collective-permute-done.1.beside_ref), custom_call_target="tpu_custom_call" | custom-call | flops 134217728 | bytes 2097152 | tf_op jit(solution)/shard_map/pallas_call | solution.py:46
  11.0 0.0 collective-permute-done.2.far_ref
  11.0 0.7 %collective-permute-done.3.next_ref = bf16[16,128]{1,0:T(8,128)(2,1)S(1)} collective-permute-done((bf16[16,128]{1,0:T(8,128)(2,1)S(1)}, bf16[16,128]{1,0:T(8,128)(2,1)S(1)}, u32[]{:S(2)}, u32[]{:S(2)}) %collective-permute-start.3) | collective-permute-done | bytes 4128 | tf_op jit(solution)/shard_map/ppermute | solution.py:441
  11.7 0.0 collective-permute-start.5
  11.7 0.0 collective-permute-done.4.above_ref
  11.7 0.3 shard_map.99
  12.0 0.8 %collective-permute-done.5.other_tiles_ref = bf16[32,128]{1,0:T(8,128)(2,1)S(1)} collective-permute-done((bf16[32,128]{1,0:T(8,128)(2,1)S(1)}, bf16[32,128]{1,0:T(8,128)(2,1)S(1)}, u32[]{:S(2)}, u32[]{:S(2)}) %collective-permute-start.5) | collective-permute-done | bytes 8224 | tf_op jit(solution)/shard_map/ppermute | solution.py:455
  12.9 0.4 %shard_map.100 = (bf16[256,256]{1,0:T(8,128)(2,1)S(1)}, bf16[32,256]{1,0:T(8,128)(2,1)S(1)}) custom-call(s32[1]{0:T(128)} %bitcast.8.core_ref, s32[1]{0:T(128)} %bitcast.space_ref, f32[320,256]{1,0:T(8,128)S(1)} %get-tuple-element.57.early_ref, f32[256,256]{1,0:T(8,128)S(1)} %get-tuple-element.63.pre_act_ref, ...), custom_call_target="tpu_custom_call" | custom-call | flops 33554432 | bytes 1048576 | tf_op jit(solution)/shard_map/pallas_call | solution.py:46
  13.3 0.2 collective-permute-start.6
  13.5 0.4 %shard_map.104 = (f32[4,104,256]{2,1,0:T(8,128)S(1)}, bf16[4,104,256]{2,1,0:T(8,128)(2,1)S(1)}) custom-call(s32[1]{0:T(128)} %bitcast.8.core_ref, bf16[3,256,256]{2,1,0:T(8,128)(2,1)S(1)} %get-tuple-element.73.windows_ref, bf16[256,256]{1,0:T(8,128)(2,1)S(1)} %get-tuple-element.66.pre_grad_ref.mine_ref, bf16[256,256]{1,0:T(8,128)(2,1)S(1)} %get-tuple-element.64.hidden_ref, ...), custom_call_target="tpu_custom_call" | custom-call | flops 256 | bytes 256 | tf_op jit(solution)/shard_map/pallas_call | solution.py:46
  14.0 0.4 %collective-permute-start.12 = (bf16[4,104,256]{2,1,0:T(8,128)(2,1)S(1)}, bf16[4,104,256]{2,1,0:T(8,128)(2,1)S(1)}, u32[]{:S(2)}, u32[]{:S(2)}) collective-permute-start(bf16[4,104,256]{2,1,0:T(8,128)(2,1)S(1)} %get-tuple-element.76), channel_id=1, source_target_pairs={{0,1},{1,0},{2,3},{3,2},{4,5},{5,4},{6,7},{7,6},{8,9},{9,8},{10,11... | collective-permute-start | bytes 638984 | tf_op jit(solution)/shard_map/ppermute | solution.py:492
  14.4 0.4 %collective-permute-done.6.beside_ref = bf16[256,256]{1,0:T(8,128)(2,1)S(1)} collective-permute-done((bf16[256,256]{1,0:T(8,128)(2,1)S(1)}, bf16[256,256]{1,0:T(8,128)(2,1)S(1)}, u32[]{:S(2)}, u32[]{:S(2)}) %collective-permute-start.6) | collective-permute-done | bytes 131104 | tf_op jit(solution)/shard_map/ppermute | solution.py:480
  14.7 0.4 %shard_map.101 = (f32[4,192,128]{2,1,0:T(8,128)S(1)}, bf16[4,192,128]{2,1,0:T(8,128)(2,1)S(1)}) custom-call(s32[1]{0:T(128)} %bitcast.1.time_ref, bf16[6,512,128]{2,1,0:T(8,128)(2,1)S(1)} %shard_map.97.windows_ref, bf16[256,256]{1,0:T(8,128)(2,1)S(1)} %get-tuple-element.66.pre_grad_ref.mine_ref, bf16[256,256]{1,0:T(8,128)(2,1)S(1)} %collective-permute-done.6.beside_ref), custom_call_target="tpu_custom_call" | custom-call | flops 201326592 | bytes 2097152 | tf_op jit(solution)/shard_map/pallas_call | solution.py:46
  15.1 0.0 copy-start
  15.2 1.6 %collective-permute-start.7 = (bf16[4,192,128]{2,1,0:T(8,128)(2,1)S(1)}, bf16[4,192,128]{2,1,0:T(8,128)(2,1)S(1)}, u32[]{:S(2)}, u32[]{:S(2)}) collective-permute-start(bf16[4,192,128]{2,1,0:T(8,128)(2,1)S(1)} %get-tuple-element.68), channel_id=1, source_target_pairs={{0,2},{2,0},{1,3},{3,1},{4,6},{6,4},{5,7},{7,5},{8,10},{10,8},{9,1... | collective-permute-start | bytes 589832 | tf_op jit(solution)/shard_map/ppermute | solution.py:501
  16.7 0.0 collective-permute-done.12.got_ref
  16.7 0.1 shard_map.105
  16.8 1.3 %collective-permute-start.13 = (bf16[232,256]{1,0:T(8,128)(2,1)S(1)}, bf16[232,256]{1,0:T(8,128)(2,1)S(1)}, u32[]{:S(2)}, u32[]{:S(2)}) collective-permute-start(bf16[232,256]{1,0:T(8,128)(2,1)S(1)} %get-tuple-element.78), channel_id=1, source_target_pairs={{0,4},{4,8},{8,12},{12,0},{1,5},{5,9},{9,13},{13,1},{2,6},{6,10},{... | collective-permute-start | bytes 356360 | tf_op jit(solution)/shard_map/ppermute | solution.py:386
  18.0 1.9 %collective-permute-start.14 = (bf16[104,256]{1,0:T(8,128)(2,1)S(1)}, bf16[104,256]{1,0:T(8,128)(2,1)S(1)}, u32[]{:S(2)}, u32[]{:S(2)}) collective-permute-start(bf16[104,256]{1,0:T(8,128)(2,1)S(1)} %get-tuple-element.79), channel_id=1, source_target_pairs={{0,8},{4,12},{8,0},{12,4},{1,9},{5,13},{9,1},{13,5},{2,10},{6,14},... | collective-permute-start | bytes 159752 | tf_op jit(solution)/shard_map/ppermute | solution.py:386
  20.0 1.3 %collective-permute-start.15 = (bf16[104,256]{1,0:T(8,128)(2,1)S(1)}, bf16[104,256]{1,0:T(8,128)(2,1)S(1)}, u32[]{:S(2)}, u32[]{:S(2)}) collective-permute-start(bf16[104,256]{1,0:T(8,128)(2,1)S(1)} %get-tuple-element.80), channel_id=1, source_target_pairs={{0,12},{4,0},{8,4},{12,8},{1,13},{5,1},{9,5},{13,9},{2,14},{6,2},{... | collective-permute-start | bytes 159752 | tf_op jit(solution)/shard_map/ppermute | solution.py:386
  21.3 0.9 %collective-permute-done.7.got_ref = bf16[4,192,128]{2,1,0:T(8,128)(2,1)S(1)} collective-permute-done((bf16[4,192,128]{2,1,0:T(8,128)(2,1)S(1)}, bf16[4,192,128]{2,1,0:T(8,128)(2,1)S(1)}, u32[]{:S(2)}, u32[]{:S(2)}) %collective-permute-start.7) | collective-permute-done | bytes 196640 | tf_op jit(solution)/shard_map/ppermute | solution.py:501
  22.2 1.4 %collective-permute-start.8 = (bf16[192,128]{1,0:T(8,128)(2,1)S(1)}, bf16[192,128]{1,0:T(8,128)(2,1)S(1)}, u32[]{:S(2)}, u32[]{:S(2)}) collective-permute-start(bf16[192,128]{1,0:T(8,128)(2,1)S(1)} %get-tuple-element.70), channel_id=1, source_target_pairs={{0,4},{4,8},{8,12},{12,0},{1,5},{5,9},{9,13},{13,1},{2,6},{6,10},{... | collective-permute-start | bytes 147464 | tf_op jit(solution)/shard_map/ppermute | solution.py:386
  23.7 2.0 %collective-permute-start.9 = (bf16[192,128]{1,0:T(8,128)(2,1)S(1)}, bf16[192,128]{1,0:T(8,128)(2,1)S(1)}, u32[]{:S(2)}, u32[]{:S(2)}) collective-permute-start(bf16[192,128]{1,0:T(8,128)(2,1)S(1)} %get-tuple-element.71), channel_id=1, source_target_pairs={{0,8},{4,12},{8,0},{12,4},{1,9},{5,13},{9,1},{13,5},{2,10},{6,14},... | collective-permute-start | bytes 147464 | tf_op jit(solution)/shard_map/ppermute | solution.py:386
  25.6 0.4 %collective-permute-done.14.refs_1_ = bf16[104,256]{1,0:T(8,128)(2,1)S(1)} collective-permute-done((bf16[104,256]{1,0:T(8,128)(2,1)S(1)}, bf16[104,256]{1,0:T(8,128)(2,1)S(1)}, u32[]{:S(2)}, u32[]{:S(2)}) %collective-permute-start.14) | collective-permute-done | bytes 53280 | tf_op jit(solution)/shard_map/ppermute | solution.py:386
  26.0 2.1 %collective-permute-start.10 = (bf16[192,128]{1,0:T(8,128)(2,1)S(1)}, bf16[192,128]{1,0:T(8,128)(2,1)S(1)}, u32[]{:S(2)}, u32[]{:S(2)}) collective-permute-start(bf16[192,128]{1,0:T(8,128)(2,1)S(1)} %get-tuple-element.72), channel_id=1, source_target_pairs={{0,12},{4,0},{8,4},{12,8},{1,13},{5,1},{9,5},{13,9},{2,14},{6,2},{... | collective-permute-start | bytes 147464 | tf_op jit(solution)/shard_map/ppermute | solution.py:386
  28.1 0.0 collective-permute-done.15.refs_2_
  28.1 0.0 collective-permute-done.13.refs_0_
  28.2 0.1 collective-permute-start.16
  28.2 0.6 %collective-permute-start.17 = (bf16[104,256]{1,0:T(8,128)(2,1)S(1)}, bf16[104,256]{1,0:T(8,128)(2,1)S(1)}, u32[]{:S(2)}, u32[]{:S(2)}) collective-permute-start(bf16[104,256]{1,0:T(8,128)(2,1)S(1)} %get-tuple-element.84.b_ref), channel_id=1, source_target_pairs={{0,2},{2,0},{1,3},{3,1},{4,6},{6,4},{5,7},{7,5},{8,10},{10,8},{9,1... | collective-permute-start | bytes 159752 | tf_op jit(solution)/shard_map/ppermute | solution.py:532
  28.9 0.0 collective-permute-done.8.refs_0_
  28.9 1.4 %collective-permute-done.9.refs_1_ = bf16[192,128]{1,0:T(8,128)(2,1)S(1)} collective-permute-done((bf16[192,128]{1,0:T(8,128)(2,1)S(1)}, bf16[192,128]{1,0:T(8,128)(2,1)S(1)}, u32[]{:S(2)}, u32[]{:S(2)}) %collective-permute-start.9) | collective-permute-done | bytes 49184 | tf_op jit(solution)/shard_map/ppermute | solution.py:386
  30.3 0.4 %collective-permute-done.10.refs_2_ = bf16[192,128]{1,0:T(8,128)(2,1)S(1)} collective-permute-done((bf16[192,128]{1,0:T(8,128)(2,1)S(1)}, bf16[192,128]{1,0:T(8,128)(2,1)S(1)}, u32[]{:S(2)}, u32[]{:S(2)}) %collective-permute-start.10) | collective-permute-done | bytes 49184 | tf_op jit(solution)/shard_map/ppermute | solution.py:386
  30.8 0.9 %collective-permute-start.11 = (bf16[192,128]{1,0:T(8,128)(2,1)S(1)}, bf16[192,128]{1,0:T(8,128)(2,1)S(1)}, u32[]{:S(2)}, u32[]{:S(2)}) collective-permute-start(bf16[192,128]{1,0:T(8,128)(2,1)S(1)} %shard_map.103.a_ref), channel_id=1, source_target_pairs={{0,2},{2,0},{1,3},{3,1},{4,6},{6,4},{5,7},{7,5},{8,10},{10,8},{9,1... | collective-permute-start | bytes 147464 | tf_op jit(solution)/shard_map/ppermute | solution.py:537
  31.7 0.0 collective-permute-done.16.low_ref
  31.7 0.0 copy-done
  31.7 1.4 %shard_map.107 = bf16[2,512,256]{2,1,0:T(8,128)(2,1)} custom-call(s32[1]{0:T(128)} %bitcast.8.core_ref, s32[1]{0:T(128)} %bitcast.space_ref, bf16[256,256]{1,0:T(8,128)(2,1)S(1)} %get-tuple-element.66.pre_grad_ref.mine_ref, bf16[256,256]{1,0:T(8,128)(2,1)S(1)} %collective-permute-done.6.beside_ref, bf16[128,256]{1,0:T(8,128)(2,1)S(1)} %collective-permute-done.16.low_ref, ...), custom_call_target="tpu_custom_call" | custom-call | flops 301989888 | bytes 4194304 | tf_op jit(solution)/shard_map/pallas_call | solution.py:46
  33.1 1.8 %collective-permute-done.11.a_far_ref = bf16[192,128]{1,0:T(8,128)(2,1)S(1)} collective-permute-done((bf16[192,128]{1,0:T(8,128)(2,1)S(1)}, bf16[192,128]{1,0:T(8,128)(2,1)S(1)}, u32[]{:S(2)}, u32[]{:S(2)}) %collective-permute-start.11) | collective-permute-done | bytes 49184 | tf_op jit(solution)/shard_map/ppermute | solution.py:537
  34.9 0.0 collective-permute-done.17.b_far_ref
  34.9 0.8 %shard_map.108 = (f32[9,32,256]{2,1,0:T(8,128)}, f32[32,32]{1,0:T(8,128)}, f32[1,32]{1,0:T(1,128)}) custom-call(s32[1]{0:T(128)} %bitcast.1.time_ref, bf16[192,128]{1,0:T(8,128)(2,1)S(1)} %shard_map.103.a_ref, bf16[192,128]{1,0:T(8,128)(2,1)S(1)} %collective-permute-done.11.a_far_ref, bf16[104,256]{1,0:T(8,128)(2,1)S(1)} %get-tuple-element.84.b_ref, ...), custom_call_target="tpu_custom_call" | custom-call | flops 51200 | bytes 1048576 | tf_op jit(solution)/shard_map/pallas_call | solution.py:46
  (4 shorter events, 0.1 us)
Async XLA Ops:
  0.6 1.6 %collective-permute-start = (bf16[8,16,32]{2,1,0:T(8,128)(2,1)}, bf16[8,16,32]{2,1,0:T(8,128)(2,1)S(1)}, u32[]{:S(2)}, u32[]{:S(2)}) collective-permute-start(bf16[8,16,32]{2,1,0:T(8,128)(2,1)} %bitcast.22), channel_id=1, source_target_pairs={{0,1},{1,0},{2,3},{3,2},{4,5},{5,4},{6,7},{7,6},{8,9},{9,8},{10,11... | collective-permute-start | bytes 24584 | tf_op jit(solution)/shard_map/ppermute | solution.py:391
  2.3 8.2 %collective-permute-start.1 = (bf16[2,512,256]{2,1,0:T(8,128)(2,1)}, bf16[2,512,256]{2,1,0:T(8,128)(2,1)S(1)}, u32[]{:S(2)}, u32[]{:S(2)}) collective-permute-start(bf16[2,512,256]{2,1,0:T(8,128)(2,1)} %bitcast.19), channel_id=1, source_target_pairs={{0,1},{1,0},{2,3},{3,2},{4,5},{5,4},{6,7},{7,6},{8,9},{9,8},{10,11... | collective-permute-start | bytes 1572872 | tf_op jit(solution)/shard_map/ppermute | solution.py:442
  2.7 8.3 %collective-permute-start.2 = (bf16[16,128]{1,0:T(8,128)(2,1)S(1)}, bf16[16,128]{1,0:T(8,128)(2,1)S(1)}, u32[]{:S(2)}, u32[]{:S(2)}) collective-permute-start(bf16[16,128]{1,0:T(8,128)(2,1)S(1)} %get-tuple-element.54), channel_id=1, source_target_pairs={{0,4},{1,9},{4,8},{5,13},{8,12},{9,1},{12,0},{13,5},{2,6},{3,11},{... | collective-permute-start | bytes 12296 | tf_op jit(solution)/shard_map/ppermute | solution.py:406
  5.4 6.3 %collective-permute-start.4 = (bf16[512,256]{1,0:T(8,128)(2,1)S(1)}, bf16[512,256]{1,0:T(8,128)(2,1)S(1)}, u32[]{:S(2)}, u32[]{:S(2)}) collective-permute-start(bf16[512,256]{1,0:T(8,128)(2,1)S(1)} %get-tuple-element.59), channel_id=1, source_target_pairs={{0,13},{1,0},{4,1},{5,4},{8,5},{9,8},{12,9},{13,12},{2,15},{3,2},{... | collective-permute-start | bytes 786440 | tf_op jit(solution)/shard_map/ppermute | solution.py:404
  8.5 3.2 %collective-permute-start.3 = (bf16[16,128]{1,0:T(8,128)(2,1)S(1)}, bf16[16,128]{1,0:T(8,128)(2,1)S(1)}, u32[]{:S(2)}, u32[]{:S(2)}) collective-permute-start(bf16[16,128]{1,0:T(8,128)(2,1)S(1)} %get-tuple-element.55), channel_id=1, source_target_pairs={{1,12},{5,0},{9,4},{13,8},{0,1},{4,5},{8,9},{12,13},{3,14},{7,2},{... | collective-permute-start | bytes 12296 | tf_op jit(solution)/shard_map/ppermute | solution.py:441
  11.7 1.2 %collective-permute-start.5 = (bf16[32,128]{1,0:T(8,128)(2,1)S(1)}, bf16[32,128]{1,0:T(8,128)(2,1)S(1)}, u32[]{:S(2)}, u32[]{:S(2)}) collective-permute-start(bf16[32,128]{1,0:T(8,128)(2,1)S(1)} %shard_map.98.tiles_ref), channel_id=1, source_target_pairs={{0,1},{1,0},{2,3},{3,2},{4,5},{5,4},{6,7},{7,6},{8,9},{9,8},{10,11... | collective-permute-start | bytes 24584 | tf_op jit(solution)/shard_map/ppermute | solution.py:455
  13.3 1.4 %collective-permute-start.6 = (bf16[256,256]{1,0:T(8,128)(2,1)S(1)}, bf16[256,256]{1,0:T(8,128)(2,1)S(1)}, u32[]{:S(2)}, u32[]{:S(2)}) collective-permute-start(bf16[256,256]{1,0:T(8,128)(2,1)S(1)} %get-tuple-element.66.pre_grad_ref.mine_ref), channel_id=1, source_target_pairs={{0,1},{1,0},{2,3},{3,2},{4,5},{5,4},{6,7},{7,6},{8,9},{9,8},{10,11... | collective-permute-start | bytes 393224 | tf_op jit(solution)/shard_map/ppermute | solution.py:480
  14.0 2.8 %collective-permute-start.12 = (bf16[4,104,256]{2,1,0:T(8,128)(2,1)S(1)}, bf16[4,104,256]{2,1,0:T(8,128)(2,1)S(1)}, u32[]{:S(2)}, u32[]{:S(2)}) collective-permute-start(bf16[4,104,256]{2,1,0:T(8,128)(2,1)S(1)} %get-tuple-element.76), channel_id=1, source_target_pairs={{0,1},{1,0},{2,3},{3,2},{4,5},{5,4},{6,7},{7,6},{8,9},{9,8},{10,11... | collective-permute-start | bytes 638984 | tf_op jit(solution)/shard_map/ppermute | solution.py:492
  15.1 16.6 %copy-start = (bf16[3,3,256,256]{3,2,1,0:T(8,128)(2,1)S(1)}, bf16[3,3,256,256]{3,2,1,0:T(8,128)(2,1)}, u32[]{:S(2)}) copy-start(bf16[3,3,256,256]{3,2,1,0:T(8,128)(2,1)} %param.7) | copy-start | bytes 3538948
  15.2 7.0 %collective-permute-start.7 = (bf16[4,192,128]{2,1,0:T(8,128)(2,1)S(1)}, bf16[4,192,128]{2,1,0:T(8,128)(2,1)S(1)}, u32[]{:S(2)}, u32[]{:S(2)}) collective-permute-start(bf16[4,192,128]{2,1,0:T(8,128)(2,1)S(1)} %get-tuple-element.68), channel_id=1, source_target_pairs={{0,2},{2,0},{1,3},{3,1},{4,6},{6,4},{5,7},{7,5},{8,10},{10,8},{9,1... | collective-permute-start | bytes 589832 | tf_op jit(solution)/shard_map/ppermute | solution.py:501
  16.8 11.4 %collective-permute-start.13 = (bf16[232,256]{1,0:T(8,128)(2,1)S(1)}, bf16[232,256]{1,0:T(8,128)(2,1)S(1)}, u32[]{:S(2)}, u32[]{:S(2)}) collective-permute-start(bf16[232,256]{1,0:T(8,128)(2,1)S(1)} %get-tuple-element.78), channel_id=1, source_target_pairs={{0,4},{4,8},{8,12},{12,0},{1,5},{5,9},{9,13},{13,1},{2,6},{6,10},{... | collective-permute-start | bytes 356360 | tf_op jit(solution)/shard_map/ppermute | solution.py:386
  18.0 8.0 %collective-permute-start.14 = (bf16[104,256]{1,0:T(8,128)(2,1)S(1)}, bf16[104,256]{1,0:T(8,128)(2,1)S(1)}, u32[]{:S(2)}, u32[]{:S(2)}) collective-permute-start(bf16[104,256]{1,0:T(8,128)(2,1)S(1)} %get-tuple-element.79), channel_id=1, source_target_pairs={{0,8},{4,12},{8,0},{12,4},{1,9},{5,13},{9,1},{13,5},{2,10},{6,14},... | collective-permute-start | bytes 159752 | tf_op jit(solution)/shard_map/ppermute | solution.py:386
  20.0 8.1 %collective-permute-start.15 = (bf16[104,256]{1,0:T(8,128)(2,1)S(1)}, bf16[104,256]{1,0:T(8,128)(2,1)S(1)}, u32[]{:S(2)}, u32[]{:S(2)}) collective-permute-start(bf16[104,256]{1,0:T(8,128)(2,1)S(1)} %get-tuple-element.80), channel_id=1, source_target_pairs={{0,12},{4,0},{8,4},{12,8},{1,13},{5,1},{9,5},{13,9},{2,14},{6,2},{... | collective-permute-start | bytes 159752 | tf_op jit(solution)/shard_map/ppermute | solution.py:386
  22.2 6.6 %collective-permute-start.8 = (bf16[192,128]{1,0:T(8,128)(2,1)S(1)}, bf16[192,128]{1,0:T(8,128)(2,1)S(1)}, u32[]{:S(2)}, u32[]{:S(2)}) collective-permute-start(bf16[192,128]{1,0:T(8,128)(2,1)S(1)} %get-tuple-element.70), channel_id=1, source_target_pairs={{0,4},{4,8},{8,12},{12,0},{1,5},{5,9},{9,13},{13,1},{2,6},{6,10},{... | collective-permute-start | bytes 147464 | tf_op jit(solution)/shard_map/ppermute | solution.py:386
  23.7 6.6 %collective-permute-start.9 = (bf16[192,128]{1,0:T(8,128)(2,1)S(1)}, bf16[192,128]{1,0:T(8,128)(2,1)S(1)}, u32[]{:S(2)}, u32[]{:S(2)}) collective-permute-start(bf16[192,128]{1,0:T(8,128)(2,1)S(1)} %get-tuple-element.71), channel_id=1, source_target_pairs={{0,8},{4,12},{8,0},{12,4},{1,9},{5,13},{9,1},{13,5},{2,10},{6,14},... | collective-permute-start | bytes 147464 | tf_op jit(solution)/shard_map/ppermute | solution.py:386
  26.0 4.7 %collective-permute-start.10 = (bf16[192,128]{1,0:T(8,128)(2,1)S(1)}, bf16[192,128]{1,0:T(8,128)(2,1)S(1)}, u32[]{:S(2)}, u32[]{:S(2)}) collective-permute-start(bf16[192,128]{1,0:T(8,128)(2,1)S(1)} %get-tuple-element.72), channel_id=1, source_target_pairs={{0,12},{4,0},{8,4},{12,8},{1,13},{5,1},{9,5},{13,9},{2,14},{6,2},{... | collective-permute-start | bytes 147464 | tf_op jit(solution)/shard_map/ppermute | solution.py:386
  28.2 3.5 %collective-permute-start.16 = (bf16[128,256]{1,0:T(8,128)(2,1)S(1)}, bf16[128,256]{1,0:T(8,128)(2,1)S(1)}, u32[]{:S(2)}, u32[]{:S(2)}) collective-permute-start(bf16[128,256]{1,0:T(8,128)(2,1)S(1)} %get-tuple-element.81.high_ref), channel_id=1, source_target_pairs={{0,1},{1,0},{2,3},{3,2},{4,5},{5,4},{6,7},{7,6},{8,9},{9,8},{10,11... | collective-permute-start | bytes 196616 | tf_op jit(solution)/shard_map/ppermute | solution.py:533
  28.2 6.7 %collective-permute-start.17 = (bf16[104,256]{1,0:T(8,128)(2,1)S(1)}, bf16[104,256]{1,0:T(8,128)(2,1)S(1)}, u32[]{:S(2)}, u32[]{:S(2)}) collective-permute-start(bf16[104,256]{1,0:T(8,128)(2,1)S(1)} %get-tuple-element.84.b_ref), channel_id=1, source_target_pairs={{0,2},{2,0},{1,3},{3,1},{4,6},{6,4},{5,7},{7,5},{8,10},{10,8},{9,1... | collective-permute-start | bytes 159752 | tf_op jit(solution)/shard_map/ppermute | solution.py:532
  30.8 4.2 %collective-permute-start.11 = (bf16[192,128]{1,0:T(8,128)(2,1)S(1)}, bf16[192,128]{1,0:T(8,128)(2,1)S(1)}, u32[]{:S(2)}, u32[]{:S(2)}) collective-permute-start(bf16[192,128]{1,0:T(8,128)(2,1)S(1)} %shard_map.103.a_ref), channel_id=1, source_target_pairs={{0,2},{2,0},{1,3},{3,1},{4,6},{6,4},{5,7},{7,5},{8,10},{10,8},{9,1... | collective-permute-start | bytes 147464 | tf_op jit(solution)/shard_map/ppermute | solution.py:537

commit v7 on v6

--- a/solution.py
+++ b/solution.py
@@ -400,7 +400,7 @@
     here, far, before = full_call(
         tiles_kernel, (array((tile[0], LANES), bf16),) * 3, [], 0, 1 << 16, "ssvv"
     )(core_at, space_at, own_tiles, got_tiles)
-    late_rows, row, far = lax.optimization_barrier((activations[0], row, far))
+    row, far = lax.optimization_barrier((row, far))
     above = lax.ppermute(row, line, [(i, (i - 1) % peers) for i in range(peers)])
     hops = [(2 * i + c, 2 * ((i + 1 + c) % spaces) + c) for i in range(spaces) for c in range(2)]
     far = lax.ppermute(far, line, hops)
@@ -426,7 +426,7 @@
             pltpu.VMEM((2 * (channels // LANES), double_cols + 8, LANES), f32),
             pltpu.SemaphoreType.DMA((6,)),
         ],
-        60 * square,
+        300 * square,
         3 << 20,
         "hhhhvv",
     )(
@@ -439,7 +439,7 @@
     )
     back = [(2 * i + 1, 2 * ((i - 1) % spaces)) for i in range(spaces)]
     after = lax.ppermute(before, line, back + [(2 * i, 2 * i + 1) for i in range(spaces)])
-    beside = lax.ppermute(late_rows, "col", swap)
+    beside = lax.ppermute(act_here, "col", swap)
     chip_windows = full_call(
         functools.partial(select_kernel, spaces),
         array((6, 2 * cols, channels // 2), bf16),

time: 35.9 us -> 35.6 us (level)
  waiting for transfers between devices: 6.9 us -> 6.18 us
  starting transfers between devices: 19.6 us -> 20 us
    ppermute x1, waiting for transfers between devices: 0.65 us -> 0.11 us  [body(): lax.ppermute(before, line, back + [(2 * i, 2 * i + 1) for i in range(spac...]
where the time goes in v7:
time: 35.6 us; the launch traced here: 35.4 us
  starting transfers between devices  20 us (56%)
  Pallas kernels  8.42 us (24%)
  waiting for transfers between devices  6.18 us (17%)
  between operations  0.77 us (2%)
    ppermute x6, starting transfers between devices, over_space(): lax.ppermute(pieces[k], 'space', [(i, (i + k) % spaces) for i in range(sp...  10 us
    pallas_call x16, Pallas kernels, placed(): return call(*pinned)  8.42 us
    ppermute x1, starting transfers between devices, body(): far = lax.ppermute(far, line, hops)  2.94 us
    ppermute x6, waiting for transfers between devices, over_space(): lax.ppermute(pieces[k], 'space', [(i, (i + k) % spaces) for i in range(sp...  2.23 us
    ppermute x1, starting transfers between devices, body(): lax.ppermute(row, line, [(i, (i - 1) % peers) for i in range(peers)])  1.86 us
    ppermute x1, waiting for transfers between devices, body(): other_a = lax.ppermute(sum_a, 'tm', swap)  1.75 us
    ppermute x1, starting transfers between devices, body(): crossed_a = lax.ppermute(cross_a, 'tm', swap)  1.56 us
    ppermute x1, starting transfers between devices, body(): other_a = lax.ppermute(sum_a, 'tm', swap)  0.98 us
  transfers between devices with their start and end apart: 18, of which 9 were waited for; matrix products, arithmetic and copies ran while one was open for 0% of the time, Pallas kernels for 20%

profile of v7, /device:TPU:0, one launch (start us, length us, event | category | flops | bytes accessed | tf_op | source)
XLA Modules:
  0.0 35.4 jit_solution(17050961774703497319)
XLA Ops:
  0.6 0.5 %collective-permute-start = (bf16[8,16,32]{2,1,0:T(8,128)(2,1)}, bf16[8,16,32]{2,1,0:T(8,128)(2,1)S(1)}, u32[]{:S(2)}, u32[]{:S(2)}) collective-permute-start(bf16[8,16,32]{2,1,0:T(8,128)(2,1)} %bitcast.21), channel_id=1, source_target_pairs={{0,1},{1,0},{2,3},{3,2},{4,5},{5,4},{6,7},{7,6},{8,9},{9,8},{10,11... | collective-permute-start | bytes 24584 | tf_op jit(solution)/shard_map/ppermute | solution.py:391
  1.1 1.0 %shard_map.93 = (bf16[512,256]{1,0:T(8,128)(2,1)S(1)}, bf16[8,16,32]{2,1,0:T(8,128)(2,1)S(1)}) custom-call(bf16[2,512,256]{2,1,0:T(8,128)(2,1)} %bitcast.18, bf16[8,16,32]{2,1,0:T(8,128)(2,1)} %bitcast.22), custom_call_target="tpu_custom_call" | custom-call | bytes 524288 | tf_op jit(solution)/shard_map/pallas_call | solution.py:46
  2.1 0.1 collective-permute-done.got_ref
  2.2 0.1 shard_map.94
  2.3 2.9 %collective-permute-start.2 = (bf16[16,128]{1,0:T(8,128)(2,1)S(1)}, bf16[16,128]{1,0:T(8,128)(2,1)S(1)}, u32[]{:S(2)}, u32[]{:S(2)}) collective-permute-start(bf16[16,128]{1,0:T(8,128)(2,1)S(1)} %get-tuple-element.52), channel_id=1, source_target_pairs={{0,4},{1,9},{4,8},{5,13},{8,12},{9,1},{12,0},{13,5},{2,6},{3,11},{... | collective-permute-start | bytes 12296 | tf_op jit(solution)/shard_map/ppermute | solution.py:406
  5.2 1.9 %collective-permute-start.4 = (bf16[512,256]{1,0:T(8,128)(2,1)S(1)}, bf16[512,256]{1,0:T(8,128)(2,1)S(1)}, u32[]{:S(2)}, u32[]{:S(2)}) collective-permute-start(bf16[512,256]{1,0:T(8,128)(2,1)S(1)} %get-tuple-element.57), channel_id=1, source_target_pairs={{0,13},{1,0},{4,1},{5,4},{8,5},{9,8},{12,9},{13,12},{2,15},{3,2},{... | collective-permute-start | bytes 786440 | tf_op jit(solution)/shard_map/ppermute | solution.py:404
  7.1 1.0 %shard_map.95 = (bf16[2,512,256]{2,1,0:T(8,128)(2,1)S(1)}, bf16[16,128]{1,0:T(8,128)(2,1)S(1)}) custom-call(bf16[2,512,256]{2,1,0:T(8,128)(2,1)} %bitcast.19, bf16[16,128]{1,0:T(8,128)(2,1)S(1)} %get-tuple-element.46.before_ref), custom_call_target="tpu_custom_call" | custom-call | flops 2013265920 | bytes 2097152 | tf_op jit(solution)/shard_map/pallas_call | solution.py:46
  8.2 0.1 collective-permute-start.3
  8.2 0.6 %collective-permute-start.1 = (bf16[2,512,256]{2,1,0:T(8,128)(2,1)S(1)}, bf16[2,512,256]{2,1,0:T(8,128)(2,1)S(1)}, u32[]{:S(2)}, u32[]{:S(2)}) collective-permute-start(bf16[2,512,256]{2,1,0:T(8,128)(2,1)S(1)} %get-tuple-element.47.act_ref), channel_id=1, source_target_pairs={{0,1},{1,0},{2,3},{3,2},{4,5},{5,4},{6,7},{7,6},{8,9},{9,8},{10,11... | collective-permute-start | bytes 1572872 | tf_op jit(solution)/shard_map/ppermute | solution.py:442
  8.8 1.9 %shard_map.96 = (f32[320,256]{1,0:T(8,128)S(1)}, bf16[9,256,256]{2,1,0:T(8,128)(2,1)S(1)}) custom-call(f32[1,256]{1,0:T(1,128)} %bitcast.26, bf16[32,256]{1,0:T(8,128)(2,1)} %bitcast.24, bf16[16,256]{1,0:T(8,128)(2,1)} %bitcast.25, bf16[9,256,256]{2,1,0:T(8,128)(2,1)} %bitcast.16, bf16[2,512,256]{2,1,0:T(8,128)(2,1)S(1)} %get-tuple-element.47.act_ref, ...), custom_call_target="tpu_custom_call" | custom-call | flops 10066329600 | bytes 3145728 | tf_op jit(solution)/shard_map/pallas_call | solution.py:46
  10.6 0.0 collective-permute-done.1.beside_ref
  10.7 0.6 %shard_map.97.windows_ref = bf16[6,512,128]{2,1,0:T(8,128)(2,1)S(1)} custom-call(s32[1]{0:T(128)} %bitcast.8.core_ref, bf16[2,512,256]{2,1,0:T(8,128)(2,1)S(1)} %get-tuple-element.47.act_ref, bf16[2,512,256]{2,1,0:T(8,128)(2,1)S(1)} %collective-permute-done.1.beside_ref), custom_call_target="tpu_custom_call" | custom-call | flops 134217728 | bytes 2097152 | tf_op jit(solution)/shard_map/pallas_call | solution.py:46
  11.2 0.0 collective-permute-done.2.far_ref
  11.2 0.1 collective-permute-done.3.next_ref
  11.3 0.0 collective-permute-start.5
  11.3 0.0 collective-permute-done.4.above_ref
  11.4 0.3 shard_map.99
  11.7 0.8 %collective-permute-done.5.other_tiles_ref = bf16[32,128]{1,0:T(8,128)(2,1)S(1)} collective-permute-done((bf16[32,128]{1,0:T(8,128)(2,1)S(1)}, bf16[32,128]{1,0:T(8,128)(2,1)S(1)}, u32[]{:S(2)}, u32[]{:S(2)}) %collective-permute-start.5) | collective-permute-done | bytes 8224 | tf_op jit(solution)/shard_map/ppermute | solution.py:455
  12.5 0.4 %shard_map.100 = (bf16[256,256]{1,0:T(8,128)(2,1)S(1)}, bf16[32,256]{1,0:T(8,128)(2,1)S(1)}) custom-call(s32[1]{0:T(128)} %bitcast.8.core_ref, s32[1]{0:T(128)} %bitcast.space_ref, f32[320,256]{1,0:T(8,128)S(1)} %get-tuple-element.55.early_ref, f32[256,256]{1,0:T(8,128)S(1)} %get-tuple-element.61.pre_act_ref, ...), custom_call_target="tpu_custom_call" | custom-call | flops 33554432 | bytes 1048576 | tf_op jit(solution)/shard_map/pallas_call | solution.py:46
  13.0 0.2 collective-permute-start.6
  13.2 0.4 %shard_map.104 = (f32[4,104,256]{2,1,0:T(8,128)S(1)}, bf16[4,104,256]{2,1,0:T(8,128)(2,1)S(1)}) custom-call(s32[1]{0:T(128)} %bitcast.8.core_ref, bf16[3,256,256]{2,1,0:T(8,128)(2,1)S(1)} %get-tuple-element.71.windows_ref, bf16[256,256]{1,0:T(8,128)(2,1)S(1)} %get-tuple-element.64.pre_grad_ref.mine_ref, bf16[256,256]{1,0:T(8,128)(2,1)S(1)} %get-tuple-element.62.hidden_ref, ...), custom_call_target="tpu_custom_call" | custom-call | flops 256 | bytes 256 | tf_op jit(solution)/shard_map/pallas_call | solution.py:46
  13.6 0.4 %collective-permute-start.12 = (bf16[4,104,256]{2,1,0:T(8,128)(2,1)S(1)}, bf16[4,104,256]{2,1,0:T(8,128)(2,1)S(1)}, u32[]{:S(2)}, u32[]{:S(2)}) collective-permute-start(bf16[4,104,256]{2,1,0:T(8,128)(2,1)S(1)} %get-tuple-element.74), channel_id=1, source_target_pairs={{0,1},{1,0},{2,3},{3,2},{4,5},{5,4},{6,7},{7,6},{8,9},{9,8},{10,11... | collective-permute-start | bytes 638984 | tf_op jit(solution)/shard_map/ppermute | solution.py:492
  14.0 0.4 %collective-permute-done.6.beside_ref = bf16[256,256]{1,0:T(8,128)(2,1)S(1)} collective-permute-done((bf16[256,256]{1,0:T(8,128)(2,1)S(1)}, bf16[256,256]{1,0:T(8,128)(2,1)S(1)}, u32[]{:S(2)}, u32[]{:S(2)}) %collective-permute-start.6) | collective-permute-done | bytes 131104 | tf_op jit(solution)/shard_map/ppermute | solution.py:480
  14.4 0.4 %shard_map.101 = (f32[4,192,128]{2,1,0:T(8,128)S(1)}, bf16[4,192,128]{2,1,0:T(8,128)(2,1)S(1)}) custom-call(s32[1]{0:T(128)} %bitcast.1.time_ref, bf16[6,512,128]{2,1,0:T(8,128)(2,1)S(1)} %shard_map.97.windows_ref, bf16[256,256]{1,0:T(8,128)(2,1)S(1)} %get-tuple-element.64.pre_grad_ref.mine_ref, bf16[256,256]{1,0:T(8,128)(2,1)S(1)} %collective-permute-done.6.beside_ref), custom_call_target="tpu_custom_call" | custom-call | flops 201326592 | bytes 2097152 | tf_op jit(solution)/shard_map/pallas_call | solution.py:46
  14.8 0.0 copy-start
  14.8 1.6 %collective-permute-start.7 = (bf16[4,192,128]{2,1,0:T(8,128)(2,1)S(1)}, bf16[4,192,128]{2,1,0:T(8,128)(2,1)S(1)}, u32[]{:S(2)}, u32[]{:S(2)}) collective-permute-start(bf16[4,192,128]{2,1,0:T(8,128)(2,1)S(1)} %get-tuple-element.66), channel_id=1, source_target_pairs={{0,2},{2,0},{1,3},{3,1},{4,6},{6,4},{5,7},{7,5},{8,10},{10,8},{9,1... | collective-permute-start | bytes 589832 | tf_op jit(solution)/shard_map/ppermute | solution.py:501
  16.4 0.0 collective-permute-done.12.got_ref
  16.4 0.1 shard_map.105
  16.4 1.6 %collective-permute-start.13 = (bf16[232,256]{1,0:T(8,128)(2,1)S(1)}, bf16[232,256]{1,0:T(8,128)(2,1)S(1)}, u32[]{:S(2)}, u32[]{:S(2)}) collective-permute-start(bf16[232,256]{1,0:T(8,128)(2,1)S(1)} %get-tuple-element.76), channel_id=1, source_target_pairs={{0,4},{4,8},{8,12},{12,0},{1,5},{5,9},{9,13},{13,1},{2,6},{6,10},{... | collective-permute-start | bytes 356360 | tf_op jit(solution)/shard_map/ppermute | solution.py:386
  18.0 1.7 %collective-permute-start.14 = (bf16[104,256]{1,0:T(8,128)(2,1)S(1)}, bf16[104,256]{1,0:T(8,128)(2,1)S(1)}, u32[]{:S(2)}, u32[]{:S(2)}) collective-permute-start(bf16[104,256]{1,0:T(8,128)(2,1)S(1)} %get-tuple-element.77), channel_id=1, source_target_pairs={{0,8},{4,12},{8,0},{12,4},{1,9},{5,13},{9,1},{13,5},{2,10},{6,14},... | collective-permute-start | bytes 159752 | tf_op jit(solution)/shard_map/ppermute | solution.py:386
  19.7 1.3 %collective-permute-start.15 = (bf16[104,256]{1,0:T(8,128)(2,1)S(1)}, bf16[104,256]{1,0:T(8,128)(2,1)S(1)}, u32[]{:S(2)}, u32[]{:S(2)}) collective-permute-start(bf16[104,256]{1,0:T(8,128)(2,1)S(1)} %get-tuple-element.78), channel_id=1, source_target_pairs={{0,12},{4,0},{8,4},{12,8},{1,13},{5,1},{9,5},{13,9},{2,14},{6,2},{... | collective-permute-start | bytes 159752 | tf_op jit(solution)/shard_map/ppermute | solution.py:386
  21.1 0.8 %collective-permute-done.7.got_ref = bf16[4,192,128]{2,1,0:T(8,128)(2,1)S(1)} collective-permute-done((bf16[4,192,128]{2,1,0:T(8,128)(2,1)S(1)}, bf16[4,192,128]{2,1,0:T(8,128)(2,1)S(1)}, u32[]{:S(2)}, u32[]{:S(2)}) %collective-permute-start.7) | collective-permute-done | bytes 196640 | tf_op jit(solution)/shard_map/ppermute | solution.py:501
  21.9 1.6 %collective-permute-start.8 = (bf16[192,128]{1,0:T(8,128)(2,1)S(1)}, bf16[192,128]{1,0:T(8,128)(2,1)S(1)}, u32[]{:S(2)}, u32[]{:S(2)}) collective-permute-start(bf16[192,128]{1,0:T(8,128)(2,1)S(1)} %get-tuple-element.68), channel_id=1, source_target_pairs={{0,4},{4,8},{8,12},{12,0},{1,5},{5,9},{9,13},{13,1},{2,6},{6,10},{... | collective-permute-start | bytes 147464 | tf_op jit(solution)/shard_map/ppermute | solution.py:386
  23.5 1.8 %collective-permute-start.9 = (bf16[192,128]{1,0:T(8,128)(2,1)S(1)}, bf16[192,128]{1,0:T(8,128)(2,1)S(1)}, u32[]{:S(2)}, u32[]{:S(2)}) collective-permute-start(bf16[192,128]{1,0:T(8,128)(2,1)S(1)} %get-tuple-element.69), channel_id=1, source_target_pairs={{0,8},{4,12},{8,0},{12,4},{1,9},{5,13},{9,1},{13,5},{2,10},{6,14},... | collective-permute-start | bytes 147464 | tf_op jit(solution)/shard_map/ppermute | solution.py:386
  25.3 0.4 %collective-permute-done.14.refs_1_ = bf16[104,256]{1,0:T(8,128)(2,1)S(1)} collective-permute-done((bf16[104,256]{1,0:T(8,128)(2,1)S(1)}, bf16[104,256]{1,0:T(8,128)(2,1)S(1)}, u32[]{:S(2)}, u32[]{:S(2)}) %collective-permute-start.14) | collective-permute-done | bytes 53280 | tf_op jit(solution)/shard_map/ppermute | solution.py:386
  25.7 2.0 %collective-permute-start.10 = (bf16[192,128]{1,0:T(8,128)(2,1)S(1)}, bf16[192,128]{1,0:T(8,128)(2,1)S(1)}, u32[]{:S(2)}, u32[]{:S(2)}) collective-permute-start(bf16[192,128]{1,0:T(8,128)(2,1)S(1)} %get-tuple-element.70), channel_id=1, source_target_pairs={{0,12},{4,0},{8,4},{12,8},{1,13},{5,1},{9,5},{13,9},{2,14},{6,2},{... | collective-permute-start | bytes 147464 | tf_op jit(solution)/shard_map/ppermute | solution.py:386
  27.7 0.0 collective-permute-done.15.refs_2_
  27.7 0.0 collective-permute-done.13.refs_0_
  27.7 0.1 collective-permute-start.16
  27.8 0.8 %collective-permute-start.17 = (bf16[104,256]{1,0:T(8,128)(2,1)S(1)}, bf16[104,256]{1,0:T(8,128)(2,1)S(1)}, u32[]{:S(2)}, u32[]{:S(2)}) collective-permute-start(bf16[104,256]{1,0:T(8,128)(2,1)S(1)} %get-tuple-element.82.b_ref), channel_id=1, source_target_pairs={{0,2},{2,0},{1,3},{3,1},{4,6},{6,4},{5,7},{7,5},{8,10},{10,8},{9,1... | collective-permute-start | bytes 159752 | tf_op jit(solution)/shard_map/ppermute | solution.py:532
  28.6 0.0 collective-permute-done.8.refs_0_
  28.6 1.4 %collective-permute-done.9.refs_1_ = bf16[192,128]{1,0:T(8,128)(2,1)S(1)} collective-permute-done((bf16[192,128]{1,0:T(8,128)(2,1)S(1)}, bf16[192,128]{1,0:T(8,128)(2,1)S(1)}, u32[]{:S(2)}, u32[]{:S(2)}) %collective-permute-start.9) | collective-permute-done | bytes 49184 | tf_op jit(solution)/shard_map/ppermute | solution.py:386
  30.0 0.4 %collective-permute-done.10.refs_2_ = bf16[192,128]{1,0:T(8,128)(2,1)S(1)} collective-permute-done((bf16[192,128]{1,0:T(8,128)(2,1)S(1)}, bf16[192,128]{1,0:T(8,128)(2,1)S(1)}, u32[]{:S(2)}, u32[]{:S(2)}) %collective-permute-start.10) | collective-permute-done | bytes 49184 | tf_op jit(solution)/shard_map/ppermute | solution.py:386
  30.4 1.0 %collective-permute-start.11 = (bf16[192,128]{1,0:T(8,128)(2,1)S(1)}, bf16[192,128]{1,0:T(8,128)(2,1)S(1)}, u32[]{:S(2)}, u32[]{:S(2)}) collective-permute-start(bf16[192,128]{1,0:T(8,128)(2,1)S(1)} %shard_map.103.a_ref), channel_id=1, source_target_pairs={{0,2},{2,0},{1,3},{3,1},{4,6},{6,4},{5,7},{7,5},{8,10},{10,8},{9,1... | collective-permute-start | bytes 147464 | tf_op jit(solution)/shard_map/ppermute | solution.py:537
  31.4 0.0 collective-permute-done.16.low_ref
  31.4 0.0 copy-done
  31.4 1.4 %shard_map.107 = bf16[2,512,256]{2,1,0:T(8,128)(2,1)} custom-call(s32[1]{0:T(128)} %bitcast.8.core_ref, s32[1]{0:T(128)} %bitcast.space_ref, bf16[256,256]{1,0:T(8,128)(2,1)S(1)} %get-tuple-element.64.pre_grad_ref.mine_ref, bf16[256,256]{1,0:T(8,128)(2,1)S(1)} %collective-permute-done.6.beside_ref, bf16[128,256]{1,0:T(8,128)(2,1)S(1)} %collective-permute-done.16.low_ref, ...), custom_call_target="tpu_custom_call" | custom-call | flops 301989888 | bytes 4194304 | tf_op jit(solution)/shard_map/pallas_call | solution.py:46
  32.8 1.8 %collective-permute-done.11.a_far_ref = bf16[192,128]{1,0:T(8,128)(2,1)S(1)} collective-permute-done((bf16[192,128]{1,0:T(8,128)(2,1)S(1)}, bf16[192,128]{1,0:T(8,128)(2,1)S(1)}, u32[]{:S(2)}, u32[]{:S(2)}) %collective-permute-start.11) | collective-permute-done | bytes 49184 | tf_op jit(solution)/shard_map/ppermute | solution.py:537
  34.6 0.0 collective-permute-done.17.b_far_ref
  34.6 0.8 %shard_map.108 = (f32[9,32,256]{2,1,0:T(8,128)}, f32[32,32]{1,0:T(8,128)}, f32[1,32]{1,0:T(1,128)}) custom-call(s32[1]{0:T(128)} %bitcast.1.time_ref, bf16[192,128]{1,0:T(8,128)(2,1)S(1)} %shard_map.103.a_ref, bf16[192,128]{1,0:T(8,128)(2,1)S(1)} %collective-permute-done.11.a_far_ref, bf16[104,256]{1,0:T(8,128)(2,1)S(1)} %get-tuple-element.82.b_ref, ...), custom_call_target="tpu_custom_call" | custom-call | flops 51200 | bytes 1048576 | tf_op jit(solution)/shard_map/pallas_call | solution.py:46
  (4 shorter events, 0.1 us)
Async XLA Ops:
  0.6 1.6 %collective-permute-start = (bf16[8,16,32]{2,1,0:T(8,128)(2,1)}, bf16[8,16,32]{2,1,0:T(8,128)(2,1)S(1)}, u32[]{:S(2)}, u32[]{:S(2)}) collective-permute-start(bf16[8,16,32]{2,1,0:T(8,128)(2,1)} %bitcast.21), channel_id=1, source_target_pairs={{0,1},{1,0},{2,3},{3,2},{4,5},{5,4},{6,7},{7,6},{8,9},{9,8},{10,11... | collective-permute-start | bytes 24584 | tf_op jit(solution)/shard_map/ppermute | solution.py:391
  2.3 8.9 %collective-permute-start.2 = (bf16[16,128]{1,0:T(8,128)(2,1)S(1)}, bf16[16,128]{1,0:T(8,128)(2,1)S(1)}, u32[]{:S(2)}, u32[]{:S(2)}) collective-permute-start(bf16[16,128]{1,0:T(8,128)(2,1)S(1)} %get-tuple-element.52), channel_id=1, source_target_pairs={{0,4},{1,9},{4,8},{5,13},{8,12},{9,1},{12,0},{13,5},{2,6},{3,11},{... | collective-permute-start | bytes 12296 | tf_op jit(solution)/shard_map/ppermute | solution.py:406
  5.2 6.1 %collective-permute-start.4 = (bf16[512,256]{1,0:T(8,128)(2,1)S(1)}, bf16[512,256]{1,0:T(8,128)(2,1)S(1)}, u32[]{:S(2)}, u32[]{:S(2)}) collective-permute-start(bf16[512,256]{1,0:T(8,128)(2,1)S(1)} %get-tuple-element.57), channel_id=1, source_target_pairs={{0,13},{1,0},{4,1},{5,4},{8,5},{9,8},{12,9},{13,12},{2,15},{3,2},{... | collective-permute-start | bytes 786440 | tf_op jit(solution)/shard_map/ppermute | solution.py:404
  8.2 3.2 %collective-permute-start.3 = (bf16[16,128]{1,0:T(8,128)(2,1)S(1)}, bf16[16,128]{1,0:T(8,128)(2,1)S(1)}, u32[]{:S(2)}, u32[]{:S(2)}) collective-permute-start(bf16[16,128]{1,0:T(8,128)(2,1)S(1)} %get-tuple-element.53), channel_id=1, source_target_pairs={{1,12},{5,0},{9,4},{13,8},{0,1},{4,5},{8,9},{12,13},{3,14},{7,2},{... | collective-permute-start | bytes 12296 | tf_op jit(solution)/shard_map/ppermute | solution.py:441
  8.2 2.4 %collective-permute-start.1 = (bf16[2,512,256]{2,1,0:T(8,128)(2,1)S(1)}, bf16[2,512,256]{2,1,0:T(8,128)(2,1)S(1)}, u32[]{:S(2)}, u32[]{:S(2)}) collective-permute-start(bf16[2,512,256]{2,1,0:T(8,128)(2,1)S(1)} %get-tuple-element.47.act_ref), channel_id=1, source_target_pairs={{0,1},{1,0},{2,3},{3,2},{4,5},{5,4},{6,7},{7,6},{8,9},{9,8},{10,11... | collective-permute-start | bytes 1572872 | tf_op jit(solution)/shard_map/ppermute | solution.py:442
  11.3 1.2 %collective-permute-start.5 = (bf16[32,128]{1,0:T(8,128)(2,1)S(1)}, bf16[32,128]{1,0:T(8,128)(2,1)S(1)}, u32[]{:S(2)}, u32[]{:S(2)}) collective-permute-start(bf16[32,128]{1,0:T(8,128)(2,1)S(1)} %shard_map.98.tiles_ref), channel_id=1, source_target_pairs={{0,1},{1,0},{2,3},{3,2},{4,5},{5,4},{6,7},{7,6},{8,9},{9,8},{10,11... | collective-permute-start | bytes 24584 | tf_op jit(solution)/shard_map/ppermute | solution.py:455
  13.0 1.4 %collective-permute-start.6 = (bf16[256,256]{1,0:T(8,128)(2,1)S(1)}, bf16[256,256]{1,0:T(8,128)(2,1)S(1)}, u32[]{:S(2)}, u32[]{:S(2)}) collective-permute-start(bf16[256,256]{1,0:T(8,128)(2,1)S(1)} %get-tuple-element.64.pre_grad_ref.mine_ref), channel_id=1, source_target_pairs={{0,1},{1,0},{2,3},{3,2},{4,5},{5,4},{6,7},{7,6},{8,9},{9,8},{10,11... | collective-permute-start | bytes 393224 | tf_op jit(solution)/shard_map/ppermute | solution.py:480
  13.6 2.8 %collective-permute-start.12 = (bf16[4,104,256]{2,1,0:T(8,128)(2,1)S(1)}, bf16[4,104,256]{2,1,0:T(8,128)(2,1)S(1)}, u32[]{:S(2)}, u32[]{:S(2)}) collective-permute-start(bf16[4,104,256]{2,1,0:T(8,128)(2,1)S(1)} %get-tuple-element.74), channel_id=1, source_target_pairs={{0,1},{1,0},{2,3},{3,2},{4,5},{5,4},{6,7},{7,6},{8,9},{9,8},{10,11... | collective-permute-start | bytes 638984 | tf_op jit(solution)/shard_map/ppermute | solution.py:492
  14.8 16.6 %copy-start = (bf16[3,3,256,256]{3,2,1,0:T(8,128)(2,1)S(1)}, bf16[3,3,256,256]{3,2,1,0:T(8,128)(2,1)}, u32[]{:S(2)}) copy-start(bf16[3,3,256,256]{3,2,1,0:T(8,128)(2,1)} %param.7) | copy-start | bytes 3538948
  14.8 7.0 %collective-permute-start.7 = (bf16[4,192,128]{2,1,0:T(8,128)(2,1)S(1)}, bf16[4,192,128]{2,1,0:T(8,128)(2,1)S(1)}, u32[]{:S(2)}, u32[]{:S(2)}) collective-permute-start(bf16[4,192,128]{2,1,0:T(8,128)(2,1)S(1)} %get-tuple-element.66), channel_id=1, source_target_pairs={{0,2},{2,0},{1,3},{3,1},{4,6},{6,4},{5,7},{7,5},{8,10},{10,8},{9,1... | collective-permute-start | bytes 589832 | tf_op jit(solution)/shard_map/ppermute | solution.py:501
  16.4 11.2 %collective-permute-start.13 = (bf16[232,256]{1,0:T(8,128)(2,1)S(1)}, bf16[232,256]{1,0:T(8,128)(2,1)S(1)}, u32[]{:S(2)}, u32[]{:S(2)}) collective-permute-start(bf16[232,256]{1,0:T(8,128)(2,1)S(1)} %get-tuple-element.76), channel_id=1, source_target_pairs={{0,4},{4,8},{8,12},{12,0},{1,5},{5,9},{9,13},{13,1},{2,6},{6,10},{... | collective-permute-start | bytes 356360 | tf_op jit(solution)/shard_map/ppermute | solution.py:386
  18.0 7.6 %collective-permute-start.14 = (bf16[104,256]{1,0:T(8,128)(2,1)S(1)}, bf16[104,256]{1,0:T(8,128)(2,1)S(1)}, u32[]{:S(2)}, u32[]{:S(2)}) collective-permute-start(bf16[104,256]{1,0:T(8,128)(2,1)S(1)} %get-tuple-element.77), channel_id=1, source_target_pairs={{0,8},{4,12},{8,0},{12,4},{1,9},{5,13},{9,1},{13,5},{2,10},{6,14},... | collective-permute-start | bytes 159752 | tf_op jit(solution)/shard_map/ppermute | solution.py:386
  19.7 7.9 %collective-permute-start.15 = (bf16[104,256]{1,0:T(8,128)(2,1)S(1)}, bf16[104,256]{1,0:T(8,128)(2,1)S(1)}, u32[]{:S(2)}, u32[]{:S(2)}) collective-permute-start(bf16[104,256]{1,0:T(8,128)(2,1)S(1)} %get-tuple-element.78), channel_id=1, source_target_pairs={{0,12},{4,0},{8,4},{12,8},{1,13},{5,1},{9,5},{13,9},{2,14},{6,2},{... | collective-permute-start | bytes 159752 | tf_op jit(solution)/shard_map/ppermute | solution.py:386
  21.9 6.7 %collective-permute-start.8 = (bf16[192,128]{1,0:T(8,128)(2,1)S(1)}, bf16[192,128]{1,0:T(8,128)(2,1)S(1)}, u32[]{:S(2)}, u32[]{:S(2)}) collective-permute-start(bf16[192,128]{1,0:T(8,128)(2,1)S(1)} %get-tuple-element.68), channel_id=1, source_target_pairs={{0,4},{4,8},{8,12},{12,0},{1,5},{5,9},{9,13},{13,1},{2,6},{6,10},{... | collective-permute-start | bytes 147464 | tf_op jit(solution)/shard_map/ppermute | solution.py:386
  23.5 6.5 %collective-permute-start.9 = (bf16[192,128]{1,0:T(8,128)(2,1)S(1)}, bf16[192,128]{1,0:T(8,128)(2,1)S(1)}, u32[]{:S(2)}, u32[]{:S(2)}) collective-permute-start(bf16[192,128]{1,0:T(8,128)(2,1)S(1)} %get-tuple-element.69), channel_id=1, source_target_pairs={{0,8},{4,12},{8,0},{12,4},{1,9},{5,13},{9,1},{13,5},{2,10},{6,14},... | collective-permute-start | bytes 147464 | tf_op jit(solution)/shard_map/ppermute | solution.py:386
  25.7 4.7 %collective-permute-start.10 = (bf16[192,128]{1,0:T(8,128)(2,1)S(1)}, bf16[192,128]{1,0:T(8,128)(2,1)S(1)}, u32[]{:S(2)}, u32[]{:S(2)}) collective-permute-start(bf16[192,128]{1,0:T(8,128)(2,1)S(1)} %get-tuple-element.70), channel_id=1, source_target_pairs={{0,12},{4,0},{8,4},{12,8},{1,13},{5,1},{9,5},{13,9},{2,14},{6,2},{... | collective-permute-start | bytes 147464 | tf_op jit(solution)/shard_map/ppermute | solution.py:386
  27.7 3.7 %collective-permute-start.16 = (bf16[128,256]{1,0:T(8,128)(2,1)S(1)}, bf16[128,256]{1,0:T(8,128)(2,1)S(1)}, u32[]{:S(2)}, u32[]{:S(2)}) collective-permute-start(bf16[128,256]{1,0:T(8,128)(2,1)S(1)} %get-tuple-element.79.high_ref), channel_id=1, source_target_pairs={{0,1},{1,0},{2,3},{3,2},{4,5},{5,4},{6,7},{7,6},{8,9},{9,8},{10,11... | collective-permute-start | bytes 196616 | tf_op jit(solution)/shard_map/ppermute | solution.py:533
  27.8 6.8 %collective-permute-start.17 = (bf16[104,256]{1,0:T(8,128)(2,1)S(1)}, bf16[104,256]{1,0:T(8,128)(2,1)S(1)}, u32[]{:S(2)}, u32[]{:S(2)}) collective-permute-start(bf16[104,256]{1,0:T(8,128)(2,1)S(1)} %get-tuple-element.82.b_ref), channel_id=1, source_target_pairs={{0,2},{2,0},{1,3},{3,1},{4,6},{6,4},{5,7},{7,5},{8,10},{10,8},{9,1... | collective-permute-start | bytes 159752 | tf_op jit(solution)/shard_map/ppermute | solution.py:532
  30.4 4.2 %collective-permute-start.11 = (bf16[192,128]{1,0:T(8,128)(2,1)S(1)}, bf16[192,128]{1,0:T(8,128)(2,1)S(1)}, u32[]{:S(2)}, u32[]{:S(2)}) collective-permute-start(bf16[192,128]{1,0:T(8,128)(2,1)S(1)} %shard_map.103.a_ref), channel_id=1, source_target_pairs={{0,2},{2,0},{1,3},{3,1},{4,6},{6,4},{5,7},{7,5},{8,10},{10,8},{9,1... | collective-permute-start | bytes 147464 | tf_op jit(solution)/shard_map/ppermute | solution.py:537

commit v8 on v7

--- a/solution.py
+++ b/solution.py
@@ -48,15 +48,12 @@
     return placed
 
 
-def start_kernel(act_ref, tiles_in, row_ref, tiles_ref, sems):
-    copies = [pltpu.make_async_copy(tiles_in, tiles_ref, sems.at[0])]
-    pieces = sems.shape[0] - 1
-    length = row_ref.shape[0] // pieces
-    for i in range(pieces):
-        here = pl.ds(i * length, length)
-        copies.append(
-            pltpu.make_async_copy(act_ref.at[0, here], row_ref.at[here], sems.at[1 + i])
-        )
+def start_kernel(act_ref, tiles_in, row_ref, second_ref, tiles_ref, sems):
+    copies = [
+        pltpu.make_async_copy(tiles_in, tiles_ref, sems.at[0]),
+        pltpu.make_async_copy(act_ref.at[0], row_ref, sems.at[1]),
+        pltpu.make_async_copy(act_ref.at[1], second_ref, sems.at[2]),
+    ]
     for copy in copies:
         copy.start()
     for copy in copies:
@@ -104,16 +101,10 @@
     return windows
 
 
-def load_kernel(act_in, before_ref, act_ref, later_ref, sems):
-    rows = act_in.shape[0]
-    copies = [
-        pltpu.make_async_copy(act_in.at[i], act_ref.at[i], sems.at[i]) for i in range(rows)
-    ]
-    for copy in copies:
-        copy.start()
+def load_kernel(row_ref, second_ref, before_ref, act_ref, later_ref):
+    act_ref[0] = row_ref[...]
+    act_ref[1] = second_ref[...]
     later_ref[...] = before_ref[...]
-    for copy in copies:
-        copy.wait()
 
 
 def early_kernel(
@@ -389,10 +380,10 @@
 
     tile = tiles.shape[1:]
     got_tiles = lax.ppermute(tiles, "col", swap)
-    row, own_tiles = full_call(
+    row, second, own_tiles = full_call(
         start_kernel,
-        (array((double_cols, channels), bf16), array(tiles.shape, bf16)),
-        [pltpu.SemaphoreType.DMA((9,))],
+        (array((double_cols, channels), bf16),) * 2 + (array(tiles.shape, bf16),),
+        [pltpu.SemaphoreType.DMA((3,))],
         0,
         1 << 19,
         "hh",
@@ -411,11 +402,11 @@
             array((double_rows, double_cols, channels), bf16),
             array((tile[0], LANES), bf16),
         ),
-        [pltpu.SemaphoreType.DMA((double_rows,))],
+        [],
         60 * square,
         2 << 20,
-        "hv",
-    )(activations[0], before)
+        "vvv",
+    )(row, second, before)
     early, w_here = full_call(
         early_kernel,
         (array((cols + 4 * latent_dim, channels), f32), array(taps.shape, bf16)),

time: 35.6 us -> 35.2 us (0.989)
  Pallas kernels: 8.42 us -> 7.53 us
  waiting for transfers between devices: 6.18 us -> 6.86 us
    pallas_call x16, Pallas kernels: 8.42 us -> 7.53 us  [placed(): return call(*pinned)]
    ppermute x1, waiting for transfers between devices: 0.84 us -> 0.16 us  [body(): other_came = lax.ppermute(came, 'col', swap)]
    ppermute x1, waiting for transfers between devices: 0.01 us -> 0.67 us  [body(): lax.ppermute(row, line, [(i, (i - 1) % peers) for i in range(peers)])]
    ppermute x1, starting transfers between devices: 0.23 us -> 0.9 us  [body(): beside_grad = lax.ppermute(pre_grad, 'col', swap)]
    ppermute x1, waiting for transfers between devices: 0.79 us -> 1.41 us  [body(): crossed_a = lax.ppermute(cross_a, 'tm', swap)]
    ppermute x6, starting transfers between devices: 10 us -> 9.49 us  [over_space(): lax.ppermute(pieces[k], 'space', [(i, (i + k) % spaces) for i in range(sp...]
  transfers between devices with their start and end apart: 18 -> 18, of which waited for: 9 -> 8; matrix products, arithmetic and copies ran while one was open for 0% -> 0% of each run, Pallas kernels for 20% -> 18%
where the time goes in v8:
time: 35.2 us; the launch traced here: 35 us
  starting transfers between devices  19.8 us (56%)
  Pallas kernels  7.53 us (21%)
  waiting for transfers between devices  6.86 us (19%)
  between operations  0.77 us (2%)
    ppermute x6, starting transfers between devices, over_space(): lax.ppermute(pieces[k], 'space', [(i, (i + k) % spaces) for i in range(sp...  9.49 us
    pallas_call x16, Pallas kernels, placed(): return call(*pinned)  7.53 us
    ppermute x1, starting transfers between devices, body(): far = lax.ppermute(far, line, hops)  2.91 us
    ppermute x6, waiting for transfers between devices, over_space(): lax.ppermute(pieces[k], 'space', [(i, (i + k) % spaces) for i in range(sp...  2.52 us
    ppermute x1, starting transfers between devices, body(): lax.ppermute(row, line, [(i, (i - 1) % peers) for i in range(peers)])  1.89 us
    ppermute x1, waiting for transfers between devices, body(): other_a = lax.ppermute(sum_a, 'tm', swap)  1.59 us
    ppermute x1, starting transfers between devices, body(): crossed_a = lax.ppermute(cross_a, 'tm', swap)  1.57 us
    ppermute x1, waiting for transfers between devices, body(): crossed_a = lax.ppermute(cross_a, 'tm', swap)  1.41 us
  transfers between devices with their start and end apart: 18, of which 8 were waited for; matrix products, arithmetic and copies ran while one was open for 0% of the time, Pallas kernels for 18%

profile of v8, /device:TPU:0, one launch (start us, length us, event | category | flops | bytes accessed | tf_op | source)
XLA Modules:
  0.0 35.0 jit_solution(5495565874500573563)
XLA Ops:
  0.6 0.5 %collective-permute-start = (bf16[8,16,32]{2,1,0:T(8,128)(2,1)}, bf16[8,16,32]{2,1,0:T(8,128)(2,1)S(1)}, u32[]{:S(2)}, u32[]{:S(2)}) collective-permute-start(bf16[8,16,32]{2,1,0:T(8,128)(2,1)} %bitcast.20), channel_id=1, source_target_pairs={{0,1},{1,0},{2,3},{3,2},{4,5},{5,4},{6,7},{7,6},{8,9},{9,8},{10,11... | collective-permute-start | bytes 24584 | tf_op jit(solution)/shard_map/ppermute | solution.py:382
  1.1 1.1 %shard_map.93 = (bf16[512,256]{1,0:T(8,128)(2,1)S(1)}, bf16[512,256]{1,0:T(8,128)(2,1)S(1)}, bf16[8,16,32]{2,1,0:T(8,128)(2,1)S(1)}) custom-call(bf16[2,512,256]{2,1,0:T(8,128)(2,1)} %bitcast.18, bf16[8,16,32]{2,1,0:T(8,128)(2,1)} %bitcast.21), custom_call_target="tpu_custom_call" | custom-call | bytes 524288 | tf_op jit(solution)/shard_map/pallas_call | solution.py:46
  2.2 0.0 collective-permute-done.got_ref
  2.2 0.1 shard_map.94
  2.3 2.9 %collective-permute-start.2 = (bf16[16,128]{1,0:T(8,128)(2,1)S(1)}, bf16[16,128]{1,0:T(8,128)(2,1)S(1)}, u32[]{:S(2)}, u32[]{:S(2)}) collective-permute-start(bf16[16,128]{1,0:T(8,128)(2,1)S(1)} %get-tuple-element.55), channel_id=1, source_target_pairs={{0,4},{1,9},{4,8},{5,13},{8,12},{9,1},{12,0},{13,5},{2,6},{3,11},{... | collective-permute-start | bytes 12296 | tf_op jit(solution)/shard_map/ppermute | solution.py:397
  5.2 1.9 %collective-permute-start.4 = (bf16[512,256]{1,0:T(8,128)(2,1)S(1)}, bf16[512,256]{1,0:T(8,128)(2,1)S(1)}, u32[]{:S(2)}, u32[]{:S(2)}) collective-permute-start(bf16[512,256]{1,0:T(8,128)(2,1)S(1)} %get-tuple-element.49.row_ref), channel_id=1, source_target_pairs={{0,13},{1,0},{4,1},{5,4},{8,5},{9,8},{12,9},{13,12},{2,15},{3,2},{... | collective-permute-start | bytes 786440 | tf_op jit(solution)/shard_map/ppermute | solution.py:395
  7.2 0.1 collective-permute-start.3
  7.2 0.6 %collective-permute-start.1 = (bf16[2,512,256]{2,1,0:T(8,128)(2,1)S(1)}, bf16[2,512,256]{2,1,0:T(8,128)(2,1)S(1)}, u32[]{:S(2)}, u32[]{:S(2)}) collective-permute-start(bf16[2,512,256]{2,1,0:T(8,128)(2,1)S(1)} %get-tuple-element.52.act_ref), channel_id=1, source_target_pairs={{0,1},{1,0},{2,3},{3,2},{4,5},{5,4},{6,7},{7,6},{8,9},{9,8},{10,11... | collective-permute-start | bytes 1572872 | tf_op jit(solution)/shard_map/ppermute | solution.py:433
  7.8 1.9 %shard_map.96 = (f32[320,256]{1,0:T(8,128)S(1)}, bf16[9,256,256]{2,1,0:T(8,128)(2,1)S(1)}) custom-call(f32[1,256]{1,0:T(1,128)} %bitcast.25, bf16[32,256]{1,0:T(8,128)(2,1)} %bitcast.23, bf16[16,256]{1,0:T(8,128)(2,1)} %bitcast.24, bf16[9,256,256]{2,1,0:T(8,128)(2,1)} %bitcast.16, bf16[2,512,256]{2,1,0:T(8,128)(2,1)S(1)} %get-tuple-element.52.act_ref, ...), custom_call_target="tpu_custom_call" | custom-call | flops 10066329600 | bytes 3145728 | tf_op jit(solution)/shard_map/pallas_call | solution.py:46
  9.7 0.0 collective-permute-done.1.beside_ref
  9.7 0.6 %shard_map.97.windows_ref = bf16[6,512,128]{2,1,0:T(8,128)(2,1)S(1)} custom-call(s32[1]{0:T(128)} %bitcast.10.core_ref, bf16[2,512,256]{2,1,0:T(8,128)(2,1)S(1)} %get-tuple-element.52.act_ref, bf16[2,512,256]{2,1,0:T(8,128)(2,1)S(1)} %collective-permute-done.1.beside_ref), custom_call_target="tpu_custom_call" | custom-call | flops 134217728 | bytes 2097152 | tf_op jit(solution)/shard_map/pallas_call | solution.py:46
  10.2 0.0 collective-permute-done.2.far_ref
  10.3 0.0 collective-permute-done.3.next_ref
  10.3 0.1 collective-permute-start.5
  10.4 0.7 %collective-permute-done.4.above_ref = bf16[512,256]{1,0:T(8,128)(2,1)S(1)} collective-permute-done((bf16[512,256]{1,0:T(8,128)(2,1)S(1)}, bf16[512,256]{1,0:T(8,128)(2,1)S(1)}, u32[]{:S(2)}, u32[]{:S(2)}) %collective-permute-start.4) | collective-permute-done | bytes 262176 | tf_op jit(solution)/shard_map/ppermute | solution.py:395
  11.0 0.3 shard_map.99
  11.4 0.2 collective-permute-done.5.other_tiles_ref
  11.5 0.4 %shard_map.100 = (bf16[256,256]{1,0:T(8,128)(2,1)S(1)}, bf16[32,256]{1,0:T(8,128)(2,1)S(1)}) custom-call(s32[1]{0:T(128)} %bitcast.10.core_ref, s32[1]{0:T(128)} %bitcast.space_ref, f32[320,256]{1,0:T(8,128)S(1)} %get-tuple-element.58.early_ref, f32[256,256]{1,0:T(8,128)S(1)} %get-tuple-element.63.pre_act_ref, ...), custom_call_target="tpu_custom_call" | custom-call | flops 33554432 | bytes 1048576 | tf_op jit(solution)/shard_map/pallas_call | solution.py:46
  12.0 0.9 %collective-permute-start.6 = (bf16[256,256]{1,0:T(8,128)(2,1)S(1)}, bf16[256,256]{1,0:T(8,128)(2,1)S(1)}, u32[]{:S(2)}, u32[]{:S(2)}) collective-permute-start(bf16[256,256]{1,0:T(8,128)(2,1)S(1)} %get-tuple-element.66.pre_grad_ref.mine_ref), channel_id=1, source_target_pairs={{0,1},{1,0},{2,3},{3,2},{4,5},{5,4},{6,7},{7,6},{8,9},{9,8},{10,11... | collective-permute-start | bytes 393224 | tf_op jit(solution)/shard_map/ppermute | solution.py:471
  12.8 0.4 %shard_map.104 = (f32[4,104,256]{2,1,0:T(8,128)S(1)}, bf16[4,104,256]{2,1,0:T(8,128)(2,1)S(1)}) custom-call(s32[1]{0:T(128)} %bitcast.10.core_ref, bf16[3,256,256]{2,1,0:T(8,128)(2,1)S(1)} %get-tuple-element.73.windows_ref, bf16[256,256]{1,0:T(8,128)(2,1)S(1)} %get-tuple-element.66.pre_grad_ref.mine_ref, bf16[256,256]{1,0:T(8,128)(2,1)S(1)} %get-tuple-element.64.hidden_ref, ...), custom_call_target="tpu_custom_call" | custom-call | flops 256 | bytes 256 | tf_op jit(solution)/shard_map/pallas_call | solution.py:46
  13.3 0.1 collective-permute-start.12
  13.3 0.5 %collective-permute-done.6.beside_ref = bf16[256,256]{1,0:T(8,128)(2,1)S(1)} collective-permute-done((bf16[256,256]{1,0:T(8,128)(2,1)S(1)}, bf16[256,256]{1,0:T(8,128)(2,1)S(1)}, u32[]{:S(2)}, u32[]{:S(2)}) %collective-permute-start.6) | collective-permute-done | bytes 131104 | tf_op jit(solution)/shard_map/ppermute | solution.py:471
  13.8 0.4 %shard_map.101 = (f32[4,192,128]{2,1,0:T(8,128)S(1)}, bf16[4,192,128]{2,1,0:T(8,128)(2,1)S(1)}) custom-call(s32[1]{0:T(128)} %bitcast.1.time_ref, bf16[6,512,128]{2,1,0:T(8,128)(2,1)S(1)} %shard_map.97.windows_ref, bf16[256,256]{1,0:T(8,128)(2,1)S(1)} %get-tuple-element.66.pre_grad_ref.mine_ref, bf16[256,256]{1,0:T(8,128)(2,1)S(1)} %collective-permute-done.6.beside_ref), custom_call_target="tpu_custom_call" | custom-call | flops 201326592 | bytes 2097152 | tf_op jit(solution)/shard_map/pallas_call | solution.py:46
  14.3 0.0 copy-start
  14.3 1.6 %collective-permute-start.7 = (bf16[4,192,128]{2,1,0:T(8,128)(2,1)S(1)}, bf16[4,192,128]{2,1,0:T(8,128)(2,1)S(1)}, u32[]{:S(2)}, u32[]{:S(2)}) collective-permute-start(bf16[4,192,128]{2,1,0:T(8,128)(2,1)S(1)} %get-tuple-element.68), channel_id=1, source_target_pairs={{0,2},{2,0},{1,3},{3,1},{4,6},{6,4},{5,7},{7,5},{8,10},{10,8},{9,1... | collective-permute-start | bytes 589832 | tf_op jit(solution)/shard_map/ppermute | solution.py:492
  15.8 0.0 collective-permute-done.12.got_ref
  15.8 0.1 shard_map.105
  15.9 1.6 %collective-permute-start.13 = (bf16[232,256]{1,0:T(8,128)(2,1)S(1)}, bf16[232,256]{1,0:T(8,128)(2,1)S(1)}, u32[]{:S(2)}, u32[]{:S(2)}) collective-permute-start(bf16[232,256]{1,0:T(8,128)(2,1)S(1)} %get-tuple-element.78), channel_id=1, source_target_pairs={{0,4},{4,8},{8,12},{12,0},{1,5},{5,9},{9,13},{13,1},{2,6},{6,10},{... | collective-permute-start | bytes 356360 | tf_op jit(solution)/shard_map/ppermute | solution.py:377
  17.5 2.1 %collective-permute-start.14 = (bf16[104,256]{1,0:T(8,128)(2,1)S(1)}, bf16[104,256]{1,0:T(8,128)(2,1)S(1)}, u32[]{:S(2)}, u32[]{:S(2)}) collective-permute-start(bf16[104,256]{1,0:T(8,128)(2,1)S(1)} %get-tuple-element.79), channel_id=1, source_target_pairs={{0,8},{4,12},{8,0},{12,4},{1,9},{5,13},{9,1},{13,5},{2,10},{6,14},... | collective-permute-start | bytes 159752 | tf_op jit(solution)/shard_map/ppermute | solution.py:377
  19.6 0.5 %collective-permute-start.15 = (bf16[104,256]{1,0:T(8,128)(2,1)S(1)}, bf16[104,256]{1,0:T(8,128)(2,1)S(1)}, u32[]{:S(2)}, u32[]{:S(2)}) collective-permute-start(bf16[104,256]{1,0:T(8,128)(2,1)S(1)} %get-tuple-element.80), channel_id=1, source_target_pairs={{0,12},{4,0},{8,4},{12,8},{1,13},{5,1},{9,5},{13,9},{2,14},{6,2},{... | collective-permute-start | bytes 159752 | tf_op jit(solution)/shard_map/ppermute | solution.py:377
  20.1 1.4 %collective-permute-done.7.got_ref = bf16[4,192,128]{2,1,0:T(8,128)(2,1)S(1)} collective-permute-done((bf16[4,192,128]{2,1,0:T(8,128)(2,1)S(1)}, bf16[4,192,128]{2,1,0:T(8,128)(2,1)S(1)}, u32[]{:S(2)}, u32[]{:S(2)}) %collective-permute-start.7) | collective-permute-done | bytes 196640 | tf_op jit(solution)/shard_map/ppermute | solution.py:492
  21.6 1.6 %collective-permute-start.8 = (bf16[192,128]{1,0:T(8,128)(2,1)S(1)}, bf16[192,128]{1,0:T(8,128)(2,1)S(1)}, u32[]{:S(2)}, u32[]{:S(2)}) collective-permute-start(bf16[192,128]{1,0:T(8,128)(2,1)S(1)} %get-tuple-element.70), channel_id=1, source_target_pairs={{0,4},{4,8},{8,12},{12,0},{1,5},{5,9},{9,13},{13,1},{2,6},{6,10},{... | collective-permute-start | bytes 147464 | tf_op jit(solution)/shard_map/ppermute | solution.py:377
  23.1 2.1 %collective-permute-start.9 = (bf16[192,128]{1,0:T(8,128)(2,1)S(1)}, bf16[192,128]{1,0:T(8,128)(2,1)S(1)}, u32[]{:S(2)}, u32[]{:S(2)}) collective-permute-start(bf16[192,128]{1,0:T(8,128)(2,1)S(1)} %get-tuple-element.71), channel_id=1, source_target_pairs={{0,8},{4,12},{8,0},{12,4},{1,9},{5,13},{9,1},{13,5},{2,10},{6,14},... | collective-permute-start | bytes 147464 | tf_op jit(solution)/shard_map/ppermute | solution.py:377
  25.3 0.0 collective-permute-done.14.refs_1_
  25.3 1.6 %collective-permute-start.10 = (bf16[192,128]{1,0:T(8,128)(2,1)S(1)}, bf16[192,128]{1,0:T(8,128)(2,1)S(1)}, u32[]{:S(2)}, u32[]{:S(2)}) collective-permute-start(bf16[192,128]{1,0:T(8,128)(2,1)S(1)} %get-tuple-element.72), channel_id=1, source_target_pairs={{0,12},{4,0},{8,4},{12,8},{1,13},{5,1},{9,5},{13,9},{2,14},{6,2},{... | collective-permute-start | bytes 147464 | tf_op jit(solution)/shard_map/ppermute | solution.py:377
  26.9 0.0 collective-permute-done.15.refs_2_
  26.9 0.0 collective-permute-done.13.refs_0_
  26.9 0.1 collective-permute-start.16
  27.0 0.6 %collective-permute-start.17 = (bf16[104,256]{1,0:T(8,128)(2,1)S(1)}, bf16[104,256]{1,0:T(8,128)(2,1)S(1)}, u32[]{:S(2)}, u32[]{:S(2)}) collective-permute-start(bf16[104,256]{1,0:T(8,128)(2,1)S(1)} %get-tuple-element.84.b_ref), channel_id=1, source_target_pairs={{0,2},{2,0},{1,3},{3,1},{4,6},{6,4},{5,7},{7,5},{8,10},{10,8},{9,1... | collective-permute-start | bytes 159752 | tf_op jit(solution)/shard_map/ppermute | solution.py:523
  27.6 0.4 %collective-permute-done.8.refs_0_ = bf16[192,128]{1,0:T(8,128)(2,1)S(1)} collective-permute-done((bf16[192,128]{1,0:T(8,128)(2,1)S(1)}, bf16[192,128]{1,0:T(8,128)(2,1)S(1)}, u32[]{:S(2)}, u32[]{:S(2)}) %collective-permute-start.8) | collective-permute-done | bytes 49184 | tf_op jit(solution)/shard_map/ppermute | solution.py:377
  28.0 1.7 %collective-permute-done.9.refs_1_ = bf16[192,128]{1,0:T(8,128)(2,1)S(1)} collective-permute-done((bf16[192,128]{1,0:T(8,128)(2,1)S(1)}, bf16[192,128]{1,0:T(8,128)(2,1)S(1)}, u32[]{:S(2)}, u32[]{:S(2)}) %collective-permute-start.9) | collective-permute-done | bytes 49184 | tf_op jit(solution)/shard_map/ppermute | solution.py:377
  29.6 0.4 %collective-permute-done.10.refs_2_ = bf16[192,128]{1,0:T(8,128)(2,1)S(1)} collective-permute-done((bf16[192,128]{1,0:T(8,128)(2,1)S(1)}, bf16[192,128]{1,0:T(8,128)(2,1)S(1)}, u32[]{:S(2)}, u32[]{:S(2)}) %collective-permute-start.10) | collective-permute-done | bytes 49184 | tf_op jit(solution)/shard_map/ppermute | solution.py:377
  30.1 1.1 %collective-permute-start.11 = (bf16[192,128]{1,0:T(8,128)(2,1)S(1)}, bf16[192,128]{1,0:T(8,128)(2,1)S(1)}, u32[]{:S(2)}, u32[]{:S(2)}) collective-permute-start(bf16[192,128]{1,0:T(8,128)(2,1)S(1)} %shard_map.103.a_ref), channel_id=1, source_target_pairs={{0,2},{2,0},{1,3},{3,1},{4,6},{6,4},{5,7},{7,5},{8,10},{10,8},{9,1... | collective-permute-start | bytes 147464 | tf_op jit(solution)/shard_map/ppermute | solution.py:528
  31.2 0.0 collective-permute-done.16.low_ref
  31.2 0.0 copy-done
  31.2 1.4 %shard_map.107 = bf16[2,512,256]{2,1,0:T(8,128)(2,1)} custom-call(s32[1]{0:T(128)} %bitcast.10.core_ref, s32[1]{0:T(128)} %bitcast.space_ref, bf16[256,256]{1,0:T(8,128)(2,1)S(1)} %get-tuple-element.66.pre_grad_ref.mine_ref, bf16[256,256]{1,0:T(8,128)(2,1)S(1)} %collective-permute-done.6.beside_ref, bf16[128,256]{1,0:T(8,128)(2,1)S(1)} %collective-permute-done.16.low_ref, ...), custom_call_target="tpu_custom_call" | custom-call | flops 301989888 | bytes 4194304 | tf_op jit(solution)/shard_map/pallas_call | solution.py:46
  32.7 1.6 %collective-permute-done.11.a_far_ref = bf16[192,128]{1,0:T(8,128)(2,1)S(1)} collective-permute-done((bf16[192,128]{1,0:T(8,128)(2,1)S(1)}, bf16[192,128]{1,0:T(8,128)(2,1)S(1)}, u32[]{:S(2)}, u32[]{:S(2)}) %collective-permute-start.11) | collective-permute-done | bytes 49184 | tf_op jit(solution)/shard_map/ppermute | solution.py:528
  34.2 0.0 collective-permute-done.17.b_far_ref
  34.3 0.8 %shard_map.108 = (f32[9,32,256]{2,1,0:T(8,128)}, f32[32,32]{1,0:T(8,128)}, f32[1,32]{1,0:T(1,128)}) custom-call(s32[1]{0:T(128)} %bitcast.1.time_ref, bf16[192,128]{1,0:T(8,128)(2,1)S(1)} %shard_map.103.a_ref, bf16[192,128]{1,0:T(8,128)(2,1)S(1)} %collective-permute-done.11.a_far_ref, bf16[104,256]{1,0:T(8,128)(2,1)S(1)} %get-tuple-element.84.b_ref, ...), custom_call_target="tpu_custom_call" | custom-call | flops 51200 | bytes 1048576 | tf_op jit(solution)/shard_map/pallas_call | solution.py:46
  (5 shorter events, 0.1 us)
Async XLA Ops:
  0.6 1.6 %collective-permute-start = (bf16[8,16,32]{2,1,0:T(8,128)(2,1)}, bf16[8,16,32]{2,1,0:T(8,128)(2,1)S(1)}, u32[]{:S(2)}, u32[]{:S(2)}) collective-permute-start(bf16[8,16,32]{2,1,0:T(8,128)(2,1)} %bitcast.20), channel_id=1, source_target_pairs={{0,1},{1,0},{2,3},{3,2},{4,5},{5,4},{6,7},{7,6},{8,9},{9,8},{10,11... | collective-permute-start | bytes 24584 | tf_op jit(solution)/shard_map/ppermute | solution.py:382
  2.3 7.9 %collective-permute-start.2 = (bf16[16,128]{1,0:T(8,128)(2,1)S(1)}, bf16[16,128]{1,0:T(8,128)(2,1)S(1)}, u32[]{:S(2)}, u32[]{:S(2)}) collective-permute-start(bf16[16,128]{1,0:T(8,128)(2,1)S(1)} %get-tuple-element.55), channel_id=1, source_target_pairs={{0,4},{1,9},{4,8},{5,13},{8,12},{9,1},{12,0},{13,5},{2,6},{3,11},{... | collective-permute-start | bytes 12296 | tf_op jit(solution)/shard_map/ppermute | solution.py:397
  5.2 5.8 %collective-permute-start.4 = (bf16[512,256]{1,0:T(8,128)(2,1)S(1)}, bf16[512,256]{1,0:T(8,128)(2,1)S(1)}, u32[]{:S(2)}, u32[]{:S(2)}) collective-permute-start(bf16[512,256]{1,0:T(8,128)(2,1)S(1)} %get-tuple-element.49.row_ref), channel_id=1, source_target_pairs={{0,13},{1,0},{4,1},{5,4},{8,5},{9,8},{12,9},{13,12},{2,15},{3,2},{... | collective-permute-start | bytes 786440 | tf_op jit(solution)/shard_map/ppermute | solution.py:395
  7.2 3.1 %collective-permute-start.3 = (bf16[16,128]{1,0:T(8,128)(2,1)S(1)}, bf16[16,128]{1,0:T(8,128)(2,1)S(1)}, u32[]{:S(2)}, u32[]{:S(2)}) collective-permute-start(bf16[16,128]{1,0:T(8,128)(2,1)S(1)} %get-tuple-element.56), channel_id=1, source_target_pairs={{1,12},{5,0},{9,4},{13,8},{0,1},{4,5},{8,9},{12,13},{3,14},{7,2},{... | collective-permute-start | bytes 12296 | tf_op jit(solution)/shard_map/ppermute | solution.py:432
  7.2 2.4 %collective-permute-start.1 = (bf16[2,512,256]{2,1,0:T(8,128)(2,1)S(1)}, bf16[2,512,256]{2,1,0:T(8,128)(2,1)S(1)}, u32[]{:S(2)}, u32[]{:S(2)}) collective-permute-start(bf16[2,512,256]{2,1,0:T(8,128)(2,1)S(1)} %get-tuple-element.52.act_ref), channel_id=1, source_target_pairs={{0,1},{1,0},{2,3},{3,2},{4,5},{5,4},{6,7},{7,6},{8,9},{9,8},{10,11... | collective-permute-start | bytes 1572872 | tf_op jit(solution)/shard_map/ppermute | solution.py:433
  10.3 1.2 %collective-permute-start.5 = (bf16[32,128]{1,0:T(8,128)(2,1)S(1)}, bf16[32,128]{1,0:T(8,128)(2,1)S(1)}, u32[]{:S(2)}, u32[]{:S(2)}) collective-permute-start(bf16[32,128]{1,0:T(8,128)(2,1)S(1)} %shard_map.98.tiles_ref), channel_id=1, source_target_pairs={{0,1},{1,0},{2,3},{3,2},{4,5},{5,4},{6,7},{7,6},{8,9},{9,8},{10,11... | collective-permute-start | bytes 24584 | tf_op jit(solution)/shard_map/ppermute | solution.py:446
  12.0 1.9 %collective-permute-start.6 = (bf16[256,256]{1,0:T(8,128)(2,1)S(1)}, bf16[256,256]{1,0:T(8,128)(2,1)S(1)}, u32[]{:S(2)}, u32[]{:S(2)}) collective-permute-start(bf16[256,256]{1,0:T(8,128)(2,1)S(1)} %get-tuple-element.66.pre_grad_ref.mine_ref), channel_id=1, source_target_pairs={{0,1},{1,0},{2,3},{3,2},{4,5},{5,4},{6,7},{7,6},{8,9},{9,8},{10,11... | collective-permute-start | bytes 393224 | tf_op jit(solution)/shard_map/ppermute | solution.py:471
  13.3 2.6 %collective-permute-start.12 = (bf16[4,104,256]{2,1,0:T(8,128)(2,1)S(1)}, bf16[4,104,256]{2,1,0:T(8,128)(2,1)S(1)}, u32[]{:S(2)}, u32[]{:S(2)}) collective-permute-start(bf16[4,104,256]{2,1,0:T(8,128)(2,1)S(1)} %get-tuple-element.76), channel_id=1, source_target_pairs={{0,1},{1,0},{2,3},{3,2},{4,5},{5,4},{6,7},{7,6},{8,9},{9,8},{10,11... | collective-permute-start | bytes 638984 | tf_op jit(solution)/shard_map/ppermute | solution.py:483
  14.3 17.0 %copy-start = (bf16[3,3,256,256]{3,2,1,0:T(8,128)(2,1)S(1)}, bf16[3,3,256,256]{3,2,1,0:T(8,128)(2,1)}, u32[]{:S(2)}) copy-start(bf16[3,3,256,256]{3,2,1,0:T(8,128)(2,1)} %param.7) | copy-start | bytes 3538948
  14.3 7.2 %collective-permute-start.7 = (bf16[4,192,128]{2,1,0:T(8,128)(2,1)S(1)}, bf16[4,192,128]{2,1,0:T(8,128)(2,1)S(1)}, u32[]{:S(2)}, u32[]{:S(2)}) collective-permute-start(bf16[4,192,128]{2,1,0:T(8,128)(2,1)S(1)} %get-tuple-element.68), channel_id=1, source_target_pairs={{0,2},{2,0},{1,3},{3,1},{4,6},{6,4},{5,7},{7,5},{8,10},{10,8},{9,1... | collective-permute-start | bytes 589832 | tf_op jit(solution)/shard_map/ppermute | solution.py:492
  15.9 11.0 %collective-permute-start.13 = (bf16[232,256]{1,0:T(8,128)(2,1)S(1)}, bf16[232,256]{1,0:T(8,128)(2,1)S(1)}, u32[]{:S(2)}, u32[]{:S(2)}) collective-permute-start(bf16[232,256]{1,0:T(8,128)(2,1)S(1)} %get-tuple-element.78), channel_id=1, source_target_pairs={{0,4},{4,8},{8,12},{12,0},{1,5},{5,9},{9,13},{13,1},{2,6},{6,10},{... | collective-permute-start | bytes 356360 | tf_op jit(solution)/shard_map/ppermute | solution.py:377
  17.5 7.8 %collective-permute-start.14 = (bf16[104,256]{1,0:T(8,128)(2,1)S(1)}, bf16[104,256]{1,0:T(8,128)(2,1)S(1)}, u32[]{:S(2)}, u32[]{:S(2)}) collective-permute-start(bf16[104,256]{1,0:T(8,128)(2,1)S(1)} %get-tuple-element.79), channel_id=1, source_target_pairs={{0,8},{4,12},{8,0},{12,4},{1,9},{5,13},{9,1},{13,5},{2,10},{6,14},... | collective-permute-start | bytes 159752 | tf_op jit(solution)/shard_map/ppermute | solution.py:377
  19.6 7.3 %collective-permute-start.15 = (bf16[104,256]{1,0:T(8,128)(2,1)S(1)}, bf16[104,256]{1,0:T(8,128)(2,1)S(1)}, u32[]{:S(2)}, u32[]{:S(2)}) collective-permute-start(bf16[104,256]{1,0:T(8,128)(2,1)S(1)} %get-tuple-element.80), channel_id=1, source_target_pairs={{0,12},{4,0},{8,4},{12,8},{1,13},{5,1},{9,5},{13,9},{2,14},{6,2},{... | collective-permute-start | bytes 159752 | tf_op jit(solution)/shard_map/ppermute | solution.py:377
  21.6 6.4 %collective-permute-start.8 = (bf16[192,128]{1,0:T(8,128)(2,1)S(1)}, bf16[192,128]{1,0:T(8,128)(2,1)S(1)}, u32[]{:S(2)}, u32[]{:S(2)}) collective-permute-start(bf16[192,128]{1,0:T(8,128)(2,1)S(1)} %get-tuple-element.70), channel_id=1, source_target_pairs={{0,4},{4,8},{8,12},{12,0},{1,5},{5,9},{9,13},{13,1},{2,6},{6,10},{... | collective-permute-start | bytes 147464 | tf_op jit(solution)/shard_map/ppermute | solution.py:377
  23.1 6.5 %collective-permute-start.9 = (bf16[192,128]{1,0:T(8,128)(2,1)S(1)}, bf16[192,128]{1,0:T(8,128)(2,1)S(1)}, u32[]{:S(2)}, u32[]{:S(2)}) collective-permute-start(bf16[192,128]{1,0:T(8,128)(2,1)S(1)} %get-tuple-element.71), channel_id=1, source_target_pairs={{0,8},{4,12},{8,0},{12,4},{1,9},{5,13},{9,1},{13,5},{2,10},{6,14},... | collective-permute-start | bytes 147464 | tf_op jit(solution)/shard_map/ppermute | solution.py:377
  25.3 4.7 %collective-permute-start.10 = (bf16[192,128]{1,0:T(8,128)(2,1)S(1)}, bf16[192,128]{1,0:T(8,128)(2,1)S(1)}, u32[]{:S(2)}, u32[]{:S(2)}) collective-permute-start(bf16[192,128]{1,0:T(8,128)(2,1)S(1)} %get-tuple-element.72), channel_id=1, source_target_pairs={{0,12},{4,0},{8,4},{12,8},{1,13},{5,1},{9,5},{13,9},{2,14},{6,2},{... | collective-permute-start | bytes 147464 | tf_op jit(solution)/shard_map/ppermute | solution.py:377
  26.9 4.3 %collective-permute-start.16 = (bf16[128,256]{1,0:T(8,128)(2,1)S(1)}, bf16[128,256]{1,0:T(8,128)(2,1)S(1)}, u32[]{:S(2)}, u32[]{:S(2)}) collective-permute-start(bf16[128,256]{1,0:T(8,128)(2,1)S(1)} %get-tuple-element.81.high_ref), channel_id=1, source_target_pairs={{0,1},{1,0},{2,3},{3,2},{4,5},{5,4},{6,7},{7,6},{8,9},{9,8},{10,11... | collective-permute-start | bytes 196616 | tf_op jit(solution)/shard_map/ppermute | solution.py:524
  27.0 7.2 %collective-permute-start.17 = (bf16[104,256]{1,0:T(8,128)(2,1)S(1)}, bf16[104,256]{1,0:T(8,128)(2,1)S(1)}, u32[]{:S(2)}, u32[]{:S(2)}) collective-permute-start(bf16[104,256]{1,0:T(8,128)(2,1)S(1)} %get-tuple-element.84.b_ref), channel_id=1, source_target_pairs={{0,2},{2,0},{1,3},{3,1},{4,6},{6,4},{5,7},{7,5},{8,10},{10,8},{9,1... | collective-permute-start | bytes 159752 | tf_op jit(solution)/shard_map/ppermute | solution.py:523
  30.1 4.2 %collective-permute-start.11 = (bf16[192,128]{1,0:T(8,128)(2,1)S(1)}, bf16[192,128]{1,0:T(8,128)(2,1)S(1)}, u32[]{:S(2)}, u32[]{:S(2)}) collective-permute-start(bf16[192,128]{1,0:T(8,128)(2,1)S(1)} %shard_map.103.a_ref), channel_id=1, source_target_pairs={{0,2},{2,0},{1,3},{3,1},{4,6},{6,4},{5,7},{7,5},{8,10},{10,8},{9,1... | collective-permute-start | bytes 147464 | tf_op jit(solution)/shard_map/ppermute | solution.py:528

commit v9 on v8

--- a/solution.py
+++ b/solution.py
@@ -12,6 +12,8 @@
 bf16 = jnp.bfloat16
 kl_weight = 1.0
 LANES = 128
+A_ORDER = (1, 2, 3)
+B_ORDER = (1, 3, 2)
 HALVED = 6
 TAIL = 8
 
@@ -282,13 +284,13 @@
     refs[-1][...] = total.astype(bf16)
 
 
-def line_rim_kernel(own_ref, *refs):
+def line_rim_kernel(rim_at, own_ref, *refs):
     rows = own_ref.shape[0]
     total = own_ref[...]
     for ref in refs[:-2]:
         total = total + ref[:rows, :].astype(f32)
     refs[-2][...] = total.astype(bf16)
-    refs[-1][...] = refs[0][rows:, :]
+    refs[-1][...] = refs[rim_at][rows:, :]
 
 
 def final_kernel(
@@ -513,18 +515,18 @@
     )(space_at, own_a, crossed_a)
     far_a = over_space(pieces_a)
     sum_b, high = full_call(
-        line_rim_kernel,
+        functools.partial(line_rim_kernel, B_ORDER.index(1)),
         (array((rows_b, channels), bf16), array((half_grad, channels), bf16)),
         [],
         4 * rows_b * channels,
         1 << 19,
         "v" * spaces,
-    )(pieces_b[0], *far_b)
+    )(pieces_b[0], *(far_b[k - 1] for k in B_ORDER))
     other_b = lax.ppermute(sum_b, "tm", swap)
     low = lax.ppermute(high, "col", swap)
     sum_a = full_call(
         line_kernel, array((rows_a, half), bf16), [], 4 * rows_a * half, 1 << 19, "v" * spaces
-    )(pieces_a[0], *far_a)
+    )(pieces_a[0], *(far_a[k - 1] for k in A_ORDER))
     other_a = lax.ppermute(sum_a, "tm", swap)
     x_grad = full_call(
         input_chip_kernel,

time: 35.2 us -> 35 us (level)
  starting transfers between devices: 19.8 us -> 18.7 us
  waiting for transfers between devices: 6.86 us -> 7.88 us
    ppermute x6, waiting for transfers between devices: 2.52 us -> 3.36 us  [over_space(): lax.ppermute(pieces[k], 'space', [(i, (i + k) % spaces) for i in range(sp...]
    ppermute x6, starting transfers between devices: 9.49 us -> 8.68 us  [over_space(): lax.ppermute(pieces[k], 'space', [(i, (i + k) % spaces) for i in range(sp...]
    ppermute x1, starting transfers between devices: 0.58 us -> 0.07 us  [body(): other_b = lax.ppermute(sum_b, 'tm', swap)]
where the time goes in v9:
time: 35 us; the launch traced here: 34.9 us
  starting transfers between devices  18.7 us (53%)
  waiting for transfers between devices  7.88 us (23%)
  Pallas kernels  7.53 us (22%)
  between operations  0.78 us (2%)
    ppermute x6, starting transfers between devices, over_space(): lax.ppermute(pieces[k], 'space', [(i, (i + k) % spaces) for i in range(sp...  8.68 us
    pallas_call x16, Pallas kernels, placed(): return call(*pinned)  7.53 us
    ppermute x6, waiting for transfers between devices, over_space(): lax.ppermute(pieces[k], 'space', [(i, (i + k) % spaces) for i in range(sp...  3.36 us
    ppermute x1, starting transfers between devices, body(): far = lax.ppermute(far, line, hops)  2.91 us
    ppermute x1, starting transfers between devices, body(): lax.ppermute(row, line, [(i, (i - 1) % peers) for i in range(peers)])  1.89 us
    ppermute x1, waiting for transfers between devices, body(): crossed_a = lax.ppermute(cross_a, 'tm', swap)  1.72 us
    ppermute x1, starting transfers between devices, body(): crossed_a = lax.ppermute(cross_a, 'tm', swap)  1.57 us
    ppermute x1, waiting for transfers between devices, body(): other_a = lax.ppermute(sum_a, 'tm', swap)  1.45 us
  transfers between devices with their start and end apart: 18, of which 8 were waited for; matrix products, arithmetic and copies ran while one was open for 0% of the time, Pallas kernels for 18%

profile of v9, /device:TPU:0, one launch (start us, length us, event | category | flops | bytes accessed | tf_op | source)
XLA Modules:
  0.0 34.9 jit_solution(16951741667306064561)
XLA Ops:
  0.6 0.5 %collective-permute-start = (bf16[8,16,32]{2,1,0:T(8,128)(2,1)}, bf16[8,16,32]{2,1,0:T(8,128)(2,1)S(1)}, u32[]{:S(2)}, u32[]{:S(2)}) collective-permute-start(bf16[8,16,32]{2,1,0:T(8,128)(2,1)} %bitcast.20), channel_id=1, source_target_pairs={{0,1},{1,0},{2,3},{3,2},{4,5},{5,4},{6,7},{7,6},{8,9},{9,8},{10,11... | collective-permute-start | bytes 24584 | tf_op jit(solution)/shard_map/ppermute | solution.py:384
  1.1 1.1 %shard_map.93 = (bf16[512,256]{1,0:T(8,128)(2,1)S(1)}, bf16[512,256]{1,0:T(8,128)(2,1)S(1)}, bf16[8,16,32]{2,1,0:T(8,128)(2,1)S(1)}) custom-call(bf16[2,512,256]{2,1,0:T(8,128)(2,1)} %bitcast.18, bf16[8,16,32]{2,1,0:T(8,128)(2,1)} %bitcast.21), custom_call_target="tpu_custom_call" | custom-call | bytes 524288 | tf_op jit(solution)/shard_map/pallas_call | solution.py:48
  2.2 0.0 collective-permute-done.got_ref
  2.2 0.1 shard_map.94
  2.3 2.9 %collective-permute-start.2 = (bf16[16,128]{1,0:T(8,128)(2,1)S(1)}, bf16[16,128]{1,0:T(8,128)(2,1)S(1)}, u32[]{:S(2)}, u32[]{:S(2)}) collective-permute-start(bf16[16,128]{1,0:T(8,128)(2,1)S(1)} %get-tuple-element.55), channel_id=1, source_target_pairs={{0,4},{1,9},{4,8},{5,13},{8,12},{9,1},{12,0},{13,5},{2,6},{3,11},{... | collective-permute-start | bytes 12296 | tf_op jit(solution)/shard_map/ppermute | solution.py:399
  5.2 1.9 %collective-permute-start.4 = (bf16[512,256]{1,0:T(8,128)(2,1)S(1)}, bf16[512,256]{1,0:T(8,128)(2,1)S(1)}, u32[]{:S(2)}, u32[]{:S(2)}) collective-permute-start(bf16[512,256]{1,0:T(8,128)(2,1)S(1)} %get-tuple-element.49.row_ref), channel_id=1, source_target_pairs={{0,13},{1,0},{4,1},{5,4},{8,5},{9,8},{12,9},{13,12},{2,15},{3,2},{... | collective-permute-start | bytes 786440 | tf_op jit(solution)/shard_map/ppermute | solution.py:397
  7.2 0.1 collective-permute-start.3
  7.2 0.6 %collective-permute-start.1 = (bf16[2,512,256]{2,1,0:T(8,128)(2,1)S(1)}, bf16[2,512,256]{2,1,0:T(8,128)(2,1)S(1)}, u32[]{:S(2)}, u32[]{:S(2)}) collective-permute-start(bf16[2,512,256]{2,1,0:T(8,128)(2,1)S(1)} %get-tuple-element.52.act_ref), channel_id=1, source_target_pairs={{0,1},{1,0},{2,3},{3,2},{4,5},{5,4},{6,7},{7,6},{8,9},{9,8},{10,11... | collective-permute-start | bytes 1572872 | tf_op jit(solution)/shard_map/ppermute | solution.py:435
  7.8 1.9 %shard_map.96 = (f32[320,256]{1,0:T(8,128)S(1)}, bf16[9,256,256]{2,1,0:T(8,128)(2,1)S(1)}) custom-call(f32[1,256]{1,0:T(1,128)} %bitcast.25, bf16[32,256]{1,0:T(8,128)(2,1)} %bitcast.23, bf16[16,256]{1,0:T(8,128)(2,1)} %bitcast.24, bf16[9,256,256]{2,1,0:T(8,128)(2,1)} %bitcast.16, bf16[2,512,256]{2,1,0:T(8,128)(2,1)S(1)} %get-tuple-element.52.act_ref, ...), custom_call_target="tpu_custom_call" | custom-call | flops 10066329600 | bytes 3145728 | tf_op jit(solution)/shard_map/pallas_call | solution.py:48
  9.7 0.0 collective-permute-done.1.beside_ref
  9.7 0.6 %shard_map.97.windows_ref = bf16[6,512,128]{2,1,0:T(8,128)(2,1)S(1)} custom-call(s32[1]{0:T(128)} %bitcast.10.core_ref, bf16[2,512,256]{2,1,0:T(8,128)(2,1)S(1)} %get-tuple-element.52.act_ref, bf16[2,512,256]{2,1,0:T(8,128)(2,1)S(1)} %collective-permute-done.1.beside_ref), custom_call_target="tpu_custom_call" | custom-call | flops 134217728 | bytes 2097152 | tf_op jit(solution)/shard_map/pallas_call | solution.py:48
  10.2 0.0 collective-permute-done.2.far_ref
  10.3 0.0 collective-permute-done.3.next_ref
  10.3 0.1 collective-permute-start.5
  10.4 0.7 %collective-permute-done.4.above_ref = bf16[512,256]{1,0:T(8,128)(2,1)S(1)} collective-permute-done((bf16[512,256]{1,0:T(8,128)(2,1)S(1)}, bf16[512,256]{1,0:T(8,128)(2,1)S(1)}, u32[]{:S(2)}, u32[]{:S(2)}) %collective-permute-start.4) | collective-permute-done | bytes 262176 | tf_op jit(solution)/shard_map/ppermute | solution.py:397
  11.0 0.3 shard_map.99
  11.4 0.2 collective-permute-done.5.other_tiles_ref
  11.5 0.4 %shard_map.100 = (bf16[256,256]{1,0:T(8,128)(2,1)S(1)}, bf16[32,256]{1,0:T(8,128)(2,1)S(1)}) custom-call(s32[1]{0:T(128)} %bitcast.10.core_ref, s32[1]{0:T(128)} %bitcast.space_ref, f32[320,256]{1,0:T(8,128)S(1)} %get-tuple-element.58.early_ref, f32[256,256]{1,0:T(8,128)S(1)} %get-tuple-element.63.pre_act_ref, ...), custom_call_target="tpu_custom_call" | custom-call | flops 33554432 | bytes 1048576 | tf_op jit(solution)/shard_map/pallas_call | solution.py:48
  12.0 0.9 %collective-permute-start.6 = (bf16[256,256]{1,0:T(8,128)(2,1)S(1)}, bf16[256,256]{1,0:T(8,128)(2,1)S(1)}, u32[]{:S(2)}, u32[]{:S(2)}) collective-permute-start(bf16[256,256]{1,0:T(8,128)(2,1)S(1)} %get-tuple-element.66.pre_grad_ref.mine_ref), channel_id=1, source_target_pairs={{0,1},{1,0},{2,3},{3,2},{4,5},{5,4},{6,7},{7,6},{8,9},{9,8},{10,11... | collective-permute-start | bytes 393224 | tf_op jit(solution)/shard_map/ppermute | solution.py:473
  12.8 0.4 %shard_map.104 = (f32[4,104,256]{2,1,0:T(8,128)S(1)}, bf16[4,104,256]{2,1,0:T(8,128)(2,1)S(1)}) custom-call(s32[1]{0:T(128)} %bitcast.10.core_ref, bf16[3,256,256]{2,1,0:T(8,128)(2,1)S(1)} %get-tuple-element.73.windows_ref, bf16[256,256]{1,0:T(8,128)(2,1)S(1)} %get-tuple-element.66.pre_grad_ref.mine_ref, bf16[256,256]{1,0:T(8,128)(2,1)S(1)} %get-tuple-element.64.hidden_ref, ...), custom_call_target="tpu_custom_call" | custom-call | flops 256 | bytes 256 | tf_op jit(solution)/shard_map/pallas_call | solution.py:48
  13.3 0.1 collective-permute-start.12
  13.3 0.5 %collective-permute-done.6.beside_ref = bf16[256,256]{1,0:T(8,128)(2,1)S(1)} collective-permute-done((bf16[256,256]{1,0:T(8,128)(2,1)S(1)}, bf16[256,256]{1,0:T(8,128)(2,1)S(1)}, u32[]{:S(2)}, u32[]{:S(2)}) %collective-permute-start.6) | collective-permute-done | bytes 131104 | tf_op jit(solution)/shard_map/ppermute | solution.py:473
  13.8 0.4 %shard_map.101 = (f32[4,192,128]{2,1,0:T(8,128)S(1)}, bf16[4,192,128]{2,1,0:T(8,128)(2,1)S(1)}) custom-call(s32[1]{0:T(128)} %bitcast.1.time_ref, bf16[6,512,128]{2,1,0:T(8,128)(2,1)S(1)} %shard_map.97.windows_ref, bf16[256,256]{1,0:T(8,128)(2,1)S(1)} %get-tuple-element.66.pre_grad_ref.mine_ref, bf16[256,256]{1,0:T(8,128)(2,1)S(1)} %collective-permute-done.6.beside_ref), custom_call_target="tpu_custom_call" | custom-call | flops 201326592 | bytes 2097152 | tf_op jit(solution)/shard_map/pallas_call | solution.py:48
  14.3 0.0 copy-start
  14.3 1.6 %collective-permute-start.7 = (bf16[4,192,128]{2,1,0:T(8,128)(2,1)S(1)}, bf16[4,192,128]{2,1,0:T(8,128)(2,1)S(1)}, u32[]{:S(2)}, u32[]{:S(2)}) collective-permute-start(bf16[4,192,128]{2,1,0:T(8,128)(2,1)S(1)} %get-tuple-element.68), channel_id=1, source_target_pairs={{0,2},{2,0},{1,3},{3,1},{4,6},{6,4},{5,7},{7,5},{8,10},{10,8},{9,1... | collective-permute-start | bytes 589832 | tf_op jit(solution)/shard_map/ppermute | solution.py:494
  15.8 0.0 collective-permute-done.12.got_ref
  15.8 0.1 shard_map.105
  15.9 1.6 %collective-permute-start.13 = (bf16[232,256]{1,0:T(8,128)(2,1)S(1)}, bf16[232,256]{1,0:T(8,128)(2,1)S(1)}, u32[]{:S(2)}, u32[]{:S(2)}) collective-permute-start(bf16[232,256]{1,0:T(8,128)(2,1)S(1)} %get-tuple-element.78), channel_id=1, source_target_pairs={{0,4},{4,8},{8,12},{12,0},{1,5},{5,9},{9,13},{13,1},{2,6},{6,10},{... | collective-permute-start | bytes 356360 | tf_op jit(solution)/shard_map/ppermute | solution.py:379
  17.5 2.3 %collective-permute-start.14 = (bf16[104,256]{1,0:T(8,128)(2,1)S(1)}, bf16[104,256]{1,0:T(8,128)(2,1)S(1)}, u32[]{:S(2)}, u32[]{:S(2)}) collective-permute-start(bf16[104,256]{1,0:T(8,128)(2,1)S(1)} %get-tuple-element.79), channel_id=1, source_target_pairs={{0,12},{4,0},{8,4},{12,8},{1,13},{5,1},{9,5},{13,9},{2,14},{6,2},{... | collective-permute-start | bytes 159752 | tf_op jit(solution)/shard_map/ppermute | solution.py:379
  19.8 0.0 collective-permute-start.15
  19.8 1.7 %collective-permute-done.7.got_ref = bf16[4,192,128]{2,1,0:T(8,128)(2,1)S(1)} collective-permute-done((bf16[4,192,128]{2,1,0:T(8,128)(2,1)S(1)}, bf16[4,192,128]{2,1,0:T(8,128)(2,1)S(1)}, u32[]{:S(2)}, u32[]{:S(2)}) %collective-permute-start.7) | collective-permute-done | bytes 196640 | tf_op jit(solution)/shard_map/ppermute | solution.py:494
  21.6 1.6 %collective-permute-start.8 = (bf16[192,128]{1,0:T(8,128)(2,1)S(1)}, bf16[192,128]{1,0:T(8,128)(2,1)S(1)}, u32[]{:S(2)}, u32[]{:S(2)}) collective-permute-start(bf16[192,128]{1,0:T(8,128)(2,1)S(1)} %get-tuple-element.70), channel_id=1, source_target_pairs={{0,4},{4,8},{8,12},{12,0},{1,5},{5,9},{9,13},{13,1},{2,6},{6,10},{... | collective-permute-start | bytes 147464 | tf_op jit(solution)/shard_map/ppermute | solution.py:379
  23.1 2.1 %collective-permute-start.9 = (bf16[192,128]{1,0:T(8,128)(2,1)S(1)}, bf16[192,128]{1,0:T(8,128)(2,1)S(1)}, u32[]{:S(2)}, u32[]{:S(2)}) collective-permute-start(bf16[192,128]{1,0:T(8,128)(2,1)S(1)} %get-tuple-element.71), channel_id=1, source_target_pairs={{0,8},{4,12},{8,0},{12,4},{1,9},{5,13},{9,1},{13,5},{2,10},{6,14},... | collective-permute-start | bytes 147464 | tf_op jit(solution)/shard_map/ppermute | solution.py:379
  25.3 0.0 collective-permute-done.14.refs_1_
  25.3 1.1 %collective-permute-start.10 = (bf16[192,128]{1,0:T(8,128)(2,1)S(1)}, bf16[192,128]{1,0:T(8,128)(2,1)S(1)}, u32[]{:S(2)}, u32[]{:S(2)}) collective-permute-start(bf16[192,128]{1,0:T(8,128)(2,1)S(1)} %get-tuple-element.72), channel_id=1, source_target_pairs={{0,12},{4,0},{8,4},{12,8},{1,13},{5,1},{9,5},{13,9},{2,14},{6,2},{... | collective-permute-start | bytes 147464 | tf_op jit(solution)/shard_map/ppermute | solution.py:379
  26.4 2.2 %collective-permute-done.15.refs_2_ = bf16[104,256]{1,0:T(8,128)(2,1)S(1)} collective-permute-done((bf16[104,256]{1,0:T(8,128)(2,1)S(1)}, bf16[104,256]{1,0:T(8,128)(2,1)S(1)}, u32[]{:S(2)}, u32[]{:S(2)}) %collective-permute-start.15) | collective-permute-done | bytes 53280 | tf_op jit(solution)/shard_map/ppermute | solution.py:379
  28.6 0.0 collective-permute-done.13.refs_0_
  28.6 0.1 collective-permute-start.16
  28.7 0.1 collective-permute-start.17
  28.8 0.0 collective-permute-done.8.refs_0_
  28.8 0.8 %collective-permute-done.9.refs_1_ = bf16[192,128]{1,0:T(8,128)(2,1)S(1)} collective-permute-done((bf16[192,128]{1,0:T(8,128)(2,1)S(1)}, bf16[192,128]{1,0:T(8,128)(2,1)S(1)}, u32[]{:S(2)}, u32[]{:S(2)}) %collective-permute-start.9) | collective-permute-done | bytes 49184 | tf_op jit(solution)/shard_map/ppermute | solution.py:379
  29.6 0.3 collective-permute-done.10.refs_2_
  30.0 1.3 %collective-permute-start.11 = (bf16[192,128]{1,0:T(8,128)(2,1)S(1)}, bf16[192,128]{1,0:T(8,128)(2,1)S(1)}, u32[]{:S(2)}, u32[]{:S(2)}) collective-permute-start(bf16[192,128]{1,0:T(8,128)(2,1)S(1)} %shard_map.103.a_ref), channel_id=1, source_target_pairs={{0,2},{2,0},{1,3},{3,1},{4,6},{6,4},{5,7},{7,5},{8,10},{10,8},{9,1... | collective-permute-start | bytes 147464 | tf_op jit(solution)/shard_map/ppermute | solution.py:530
  31.2 0.0 collective-permute-done.16.low_ref
  31.2 0.0 copy-done
  31.2 1.4 %shard_map.107 = bf16[2,512,256]{2,1,0:T(8,128)(2,1)} custom-call(s32[1]{0:T(128)} %bitcast.10.core_ref, s32[1]{0:T(128)} %bitcast.space_ref, bf16[256,256]{1,0:T(8,128)(2,1)S(1)} %get-tuple-element.66.pre_grad_ref.mine_ref, bf16[256,256]{1,0:T(8,128)(2,1)S(1)} %collective-permute-done.6.beside_ref, bf16[128,256]{1,0:T(8,128)(2,1)S(1)} %collective-permute-done.16.low_ref, ...), custom_call_target="tpu_custom_call" | custom-call | flops 301989888 | bytes 4194304 | tf_op jit(solution)/shard_map/pallas_call | solution.py:48
  32.7 1.5 %collective-permute-done.11.a_far_ref = bf16[192,128]{1,0:T(8,128)(2,1)S(1)} collective-permute-done((bf16[192,128]{1,0:T(8,128)(2,1)S(1)}, bf16[192,128]{1,0:T(8,128)(2,1)S(1)}, u32[]{:S(2)}, u32[]{:S(2)}) %collective-permute-start.11) | collective-permute-done | bytes 49184 | tf_op jit(solution)/shard_map/ppermute | solution.py:530
  34.1 0.0 collective-permute-done.17.b_far_ref
  34.1 0.8 %shard_map.108 = (f32[9,32,256]{2,1,0:T(8,128)}, f32[32,32]{1,0:T(8,128)}, f32[1,32]{1,0:T(1,128)}) custom-call(s32[1]{0:T(128)} %bitcast.1.time_ref, bf16[192,128]{1,0:T(8,128)(2,1)S(1)} %shard_map.103.a_ref, bf16[192,128]{1,0:T(8,128)(2,1)S(1)} %collective-permute-done.11.a_far_ref, bf16[104,256]{1,0:T(8,128)(2,1)S(1)} %get-tuple-element.84.b_ref, ...), custom_call_target="tpu_custom_call" | custom-call | flops 51200 | bytes 1048576 | tf_op jit(solution)/shard_map/pallas_call | solution.py:48
  (5 shorter events, 0.1 us)
Async XLA Ops:
  0.6 1.6 %collective-permute-start = (bf16[8,16,32]{2,1,0:T(8,128)(2,1)}, bf16[8,16,32]{2,1,0:T(8,128)(2,1)S(1)}, u32[]{:S(2)}, u32[]{:S(2)}) collective-permute-start(bf16[8,16,32]{2,1,0:T(8,128)(2,1)} %bitcast.20), channel_id=1, source_target_pairs={{0,1},{1,0},{2,3},{3,2},{4,5},{5,4},{6,7},{7,6},{8,9},{9,8},{10,11... | collective-permute-start | bytes 24584 | tf_op jit(solution)/shard_map/ppermute | solution.py:384
  2.3 7.9 %collective-permute-start.2 = (bf16[16,128]{1,0:T(8,128)(2,1)S(1)}, bf16[16,128]{1,0:T(8,128)(2,1)S(1)}, u32[]{:S(2)}, u32[]{:S(2)}) collective-permute-start(bf16[16,128]{1,0:T(8,128)(2,1)S(1)} %get-tuple-element.55), channel_id=1, source_target_pairs={{0,4},{1,9},{4,8},{5,13},{8,12},{9,1},{12,0},{13,5},{2,6},{3,11},{... | collective-permute-start | bytes 12296 | tf_op jit(solution)/shard_map/ppermute | solution.py:399
  5.2 5.8 %collective-permute-start.4 = (bf16[512,256]{1,0:T(8,128)(2,1)S(1)}, bf16[512,256]{1,0:T(8,128)(2,1)S(1)}, u32[]{:S(2)}, u32[]{:S(2)}) collective-permute-start(bf16[512,256]{1,0:T(8,128)(2,1)S(1)} %get-tuple-element.49.row_ref), channel_id=1, source_target_pairs={{0,13},{1,0},{4,1},{5,4},{8,5},{9,8},{12,9},{13,12},{2,15},{3,2},{... | collective-permute-start | bytes 786440 | tf_op jit(solution)/shard_map/ppermute | solution.py:397
  7.2 3.1 %collective-permute-start.3 = (bf16[16,128]{1,0:T(8,128)(2,1)S(1)}, bf16[16,128]{1,0:T(8,128)(2,1)S(1)}, u32[]{:S(2)}, u32[]{:S(2)}) collective-permute-start(bf16[16,128]{1,0:T(8,128)(2,1)S(1)} %get-tuple-element.56), channel_id=1, source_target_pairs={{1,12},{5,0},{9,4},{13,8},{0,1},{4,5},{8,9},{12,13},{3,14},{7,2},{... | collective-permute-start | bytes 12296 | tf_op jit(solution)/shard_map/ppermute | solution.py:434
  7.2 2.4 %collective-permute-start.1 = (bf16[2,512,256]{2,1,0:T(8,128)(2,1)S(1)}, bf16[2,512,256]{2,1,0:T(8,128)(2,1)S(1)}, u32[]{:S(2)}, u32[]{:S(2)}) collective-permute-start(bf16[2,512,256]{2,1,0:T(8,128)(2,1)S(1)} %get-tuple-element.52.act_ref), channel_id=1, source_target_pairs={{0,1},{1,0},{2,3},{3,2},{4,5},{5,4},{6,7},{7,6},{8,9},{9,8},{10,11... | collective-permute-start | bytes 1572872 | tf_op jit(solution)/shard_map/ppermute | solution.py:435
  10.3 1.2 %collective-permute-start.5 = (bf16[32,128]{1,0:T(8,128)(2,1)S(1)}, bf16[32,128]{1,0:T(8,128)(2,1)S(1)}, u32[]{:S(2)}, u32[]{:S(2)}) collective-permute-start(bf16[32,128]{1,0:T(8,128)(2,1)S(1)} %shard_map.98.tiles_ref), channel_id=1, source_target_pairs={{0,1},{1,0},{2,3},{3,2},{4,5},{5,4},{6,7},{7,6},{8,9},{9,8},{10,11... | collective-permute-start | bytes 24584 | tf_op jit(solution)/shard_map/ppermute | solution.py:448
  12.0 1.9 %collective-permute-start.6 = (bf16[256,256]{1,0:T(8,128)(2,1)S(1)}, bf16[256,256]{1,0:T(8,128)(2,1)S(1)}, u32[]{:S(2)}, u32[]{:S(2)}) collective-permute-start(bf16[256,256]{1,0:T(8,128)(2,1)S(1)} %get-tuple-element.66.pre_grad_ref.mine_ref), channel_id=1, source_target_pairs={{0,1},{1,0},{2,3},{3,2},{4,5},{5,4},{6,7},{7,6},{8,9},{9,8},{10,11... | collective-permute-start | bytes 393224 | tf_op jit(solution)/shard_map/ppermute | solution.py:473
  13.3 2.6 %collective-permute-start.12 = (bf16[4,104,256]{2,1,0:T(8,128)(2,1)S(1)}, bf16[4,104,256]{2,1,0:T(8,128)(2,1)S(1)}, u32[]{:S(2)}, u32[]{:S(2)}) collective-permute-start(bf16[4,104,256]{2,1,0:T(8,128)(2,1)S(1)} %get-tuple-element.76), channel_id=1, source_target_pairs={{0,1},{1,0},{2,3},{3,2},{4,5},{5,4},{6,7},{7,6},{8,9},{9,8},{10,11... | collective-permute-start | bytes 638984 | tf_op jit(solution)/shard_map/ppermute | solution.py:485
  14.3 17.0 %copy-start = (bf16[3,3,256,256]{3,2,1,0:T(8,128)(2,1)S(1)}, bf16[3,3,256,256]{3,2,1,0:T(8,128)(2,1)}, u32[]{:S(2)}) copy-start(bf16[3,3,256,256]{3,2,1,0:T(8,128)(2,1)} %param.7) | copy-start | bytes 3538948
  14.3 7.2 %collective-permute-start.7 = (bf16[4,192,128]{2,1,0:T(8,128)(2,1)S(1)}, bf16[4,192,128]{2,1,0:T(8,128)(2,1)S(1)}, u32[]{:S(2)}, u32[]{:S(2)}) collective-permute-start(bf16[4,192,128]{2,1,0:T(8,128)(2,1)S(1)} %get-tuple-element.68), channel_id=1, source_target_pairs={{0,2},{2,0},{1,3},{3,1},{4,6},{6,4},{5,7},{7,5},{8,10},{10,8},{9,1... | collective-permute-start | bytes 589832 | tf_op jit(solution)/shard_map/ppermute | solution.py:494
  15.9 12.7 %collective-permute-start.13 = (bf16[232,256]{1,0:T(8,128)(2,1)S(1)}, bf16[232,256]{1,0:T(8,128)(2,1)S(1)}, u32[]{:S(2)}, u32[]{:S(2)}) collective-permute-start(bf16[232,256]{1,0:T(8,128)(2,1)S(1)} %get-tuple-element.78), channel_id=1, source_target_pairs={{0,4},{4,8},{8,12},{12,0},{1,5},{5,9},{9,13},{13,1},{2,6},{6,10},{... | collective-permute-start | bytes 356360 | tf_op jit(solution)/shard_map/ppermute | solution.py:379
  17.5 7.8 %collective-permute-start.14 = (bf16[104,256]{1,0:T(8,128)(2,1)S(1)}, bf16[104,256]{1,0:T(8,128)(2,1)S(1)}, u32[]{:S(2)}, u32[]{:S(2)}) collective-permute-start(bf16[104,256]{1,0:T(8,128)(2,1)S(1)} %get-tuple-element.79), channel_id=1, source_target_pairs={{0,12},{4,0},{8,4},{12,8},{1,13},{5,1},{9,5},{13,9},{2,14},{6,2},{... | collective-permute-start | bytes 159752 | tf_op jit(solution)/shard_map/ppermute | solution.py:379
  19.8 8.8 %collective-permute-start.15 = (bf16[104,256]{1,0:T(8,128)(2,1)S(1)}, bf16[104,256]{1,0:T(8,128)(2,1)S(1)}, u32[]{:S(2)}, u32[]{:S(2)}) collective-permute-start(bf16[104,256]{1,0:T(8,128)(2,1)S(1)} %get-tuple-element.80), channel_id=1, source_target_pairs={{0,8},{4,12},{8,0},{12,4},{1,9},{5,13},{9,1},{13,5},{2,10},{6,14},... | collective-permute-start | bytes 159752 | tf_op jit(solution)/shard_map/ppermute | solution.py:379
  21.6 7.2 %collective-permute-start.8 = (bf16[192,128]{1,0:T(8,128)(2,1)S(1)}, bf16[192,128]{1,0:T(8,128)(2,1)S(1)}, u32[]{:S(2)}, u32[]{:S(2)}) collective-permute-start(bf16[192,128]{1,0:T(8,128)(2,1)S(1)} %get-tuple-element.70), channel_id=1, source_target_pairs={{0,4},{4,8},{8,12},{12,0},{1,5},{5,9},{9,13},{13,1},{2,6},{6,10},{... | collective-permute-start | bytes 147464 | tf_op jit(solution)/shard_map/ppermute | solution.py:379
  23.1 6.5 %collective-permute-start.9 = (bf16[192,128]{1,0:T(8,128)(2,1)S(1)}, bf16[192,128]{1,0:T(8,128)(2,1)S(1)}, u32[]{:S(2)}, u32[]{:S(2)}) collective-permute-start(bf16[192,128]{1,0:T(8,128)(2,1)S(1)} %get-tuple-element.71), channel_id=1, source_target_pairs={{0,8},{4,12},{8,0},{12,4},{1,9},{5,13},{9,1},{13,5},{2,10},{6,14},... | collective-permute-start | bytes 147464 | tf_op jit(solution)/shard_map/ppermute | solution.py:379
  25.3 4.6 %collective-permute-start.10 = (bf16[192,128]{1,0:T(8,128)(2,1)S(1)}, bf16[192,128]{1,0:T(8,128)(2,1)S(1)}, u32[]{:S(2)}, u32[]{:S(2)}) collective-permute-start(bf16[192,128]{1,0:T(8,128)(2,1)S(1)} %get-tuple-element.72), channel_id=1, source_target_pairs={{0,12},{4,0},{8,4},{12,8},{1,13},{5,1},{9,5},{13,9},{2,14},{6,2},{... | collective-permute-start | bytes 147464 | tf_op jit(solution)/shard_map/ppermute | solution.py:379
  28.6 2.6 %collective-permute-start.16 = (bf16[128,256]{1,0:T(8,128)(2,1)S(1)}, bf16[128,256]{1,0:T(8,128)(2,1)S(1)}, u32[]{:S(2)}, u32[]{:S(2)}) collective-permute-start(bf16[128,256]{1,0:T(8,128)(2,1)S(1)} %get-tuple-element.81.high_ref), channel_id=1, source_target_pairs={{0,1},{1,0},{2,3},{3,2},{4,5},{5,4},{6,7},{7,6},{8,9},{9,8},{10,11... | collective-permute-start | bytes 196616 | tf_op jit(solution)/shard_map/ppermute | solution.py:526
  28.7 5.4 %collective-permute-start.17 = (bf16[104,256]{1,0:T(8,128)(2,1)S(1)}, bf16[104,256]{1,0:T(8,128)(2,1)S(1)}, u32[]{:S(2)}, u32[]{:S(2)}) collective-permute-start(bf16[104,256]{1,0:T(8,128)(2,1)S(1)} %get-tuple-element.84.b_ref), channel_id=1, source_target_pairs={{0,2},{2,0},{1,3},{3,1},{4,6},{6,4},{5,7},{7,5},{8,10},{10,8},{9,1... | collective-permute-start | bytes 159752 | tf_op jit(solution)/shard_map/ppermute | solution.py:525
  30.0 4.2 %collective-permute-start.11 = (bf16[192,128]{1,0:T(8,128)(2,1)S(1)}, bf16[192,128]{1,0:T(8,128)(2,1)S(1)}, u32[]{:S(2)}, u32[]{:S(2)}) collective-permute-start(bf16[192,128]{1,0:T(8,128)(2,1)S(1)} %shard_map.103.a_ref), channel_id=1, source_target_pairs={{0,2},{2,0},{1,3},{3,1},{4,6},{6,4},{5,7},{7,5},{8,10},{10,8},{9,1... | collective-permute-start | bytes 147464 | tf_op jit(solution)/shard_map/ppermute | solution.py:530
